TPU v7x, 256 devices: a whole 4x4x8 slice. The times are simulated.
256 devices in a mesh: gy: 32 (over y, x, core), gz: 8 (over z).
Axes of the slice: x: 4, y: 4, z: 8, core: 2. Of those that a mesh axis runs over, the one named last changes fastest.
Arguments:
- dual_flow_speeds: float32 [3, 256, 128, 1024], P(None, 'gy', 'gz'), may hold values from -6 to 6
- dual_thermal_state: float32 [256, 128, 1024], P('gy', 'gz'), may hold values from -6 to 6
- forward_flow_speeds: bfloat16 [3, 256, 128, 1024], P(None, 'gy', 'gz'), may hold values from -4 to 4
- forward_thermal_state: bfloat16 [256, 128, 1024], P('gy', 'gz'), may hold values from -6 to 6
Outputs:
- advanced_dual_motion: float32 [3, 256, 128, 1024], P(None, 'gy', 'gz')
- advanced_dual_thermal: float32 [256, 128, 1024], P('gy', 'gz')
All inputs are finite; a program needn't handle non-finite values.
Results may differ from a plain program's by a relative error of at most 0.0003.
Values sent between devices are 32-bit elements; how exact they have to be, the bound alone decides.
No kernel may reach another device: no remote copies, remote signals or barrier semaphores. Data moves between devices by JAX's collectives and lax.ppermute only.
A program may use at most 128 MiB of HBM per device.

v0:
```python
import math

import jax
import jax.numpy as jnp
from jax import lax
from jax.sharding import PartitionSpec as P

time_step = 0.2
viscosity = 0.1
diffusivity = 0.1
buoyancy = 1.0
highest = lax.Precision.HIGHEST


def padded(cells, sides, width):
    for axis, dim in sides:
        count = lax.axis_size(axis)
        head = lax.slice_in_dim(cells, 0, width, axis=dim)
        tail = lax.slice_in_dim(cells, cells.shape[dim] - width, cells.shape[dim], axis=dim)
        cells = jnp.concatenate(
            [
                lax.ppermute(tail, axis, [(i, (i + 1) % count) for i in range(count)]),
                cells,
                lax.ppermute(head, axis, [((i + 1) % count, i) for i in range(count)]),
            ],
            axis=dim,
        )
    return cells


def shifted(value, axis, by):
    length = lax.axis_size(axis)
    return lax.ppermute(value, axis, [(i, (i + by) % length) for i in range(length)])


def from_behind(block, axis, distance):
    devices = range(lax.axis_size(axis))
    route = [(i - distance, i) for i in devices if i - distance in devices]
    return lax.ppermute(block, axis, route)


def tendency_contributions(haloed_quantities, motion_pieces):
    centre = haloed_quantities[:, 1:-1, 1:-1]
    slope_x = 0.5 * (jnp.roll(centre, -1, axis=3) - jnp.roll(centre, 1, axis=3))
    slope_y = 0.5 * (haloed_quantities[:, 2:, 1:-1] - haloed_quantities[:, :-2, 1:-1])
    slope_z = 0.5 * (haloed_quantities[:, 1:-1, 2:] - haloed_quantities[:, 1:-1, :-2])
    laplace = (
        jnp.roll(centre[:4], -1, axis=3)
        + jnp.roll(centre[:4], 1, axis=3)
        + (haloed_quantities[:4, 2:, 1:-1] + haloed_quantities[:4, :-2, 1:-1])
        + (haloed_quantities[:4, 1:-1, 2:] + haloed_quantities[:4, 1:-1, :-2])
        - 6.0 * centre[:4]
    )
    advect = (
        motion_pieces[0] * slope_x[:4]
        + motion_pieces[1] * slope_y[:4]
        + motion_pieces[2] * slope_z[:4]
    )
    heat_slope = jnp.stack([slope_x[4], slope_y[4], slope_z[4]])
    unprojected_motion = centre[:3] + time_step * (
        advect[:3] + viscosity * laplace[:3] + centre[3] * heat_slope
    )
    thermal_following = centre[3] + time_step * (
        advect[3] + diffusivity * laplace[3] + buoyancy * centre[2]
    )
    return (unprojected_motion, thermal_following)


def cas_table(length):
    indices = jnp.arange(length, dtype=jnp.int32)
    phases = indices[:, None] * indices[None, :] % length
    angles = phases.astype(jnp.float32) * (2.0 * math.pi / length)
    return jnp.cos(angles) + jnp.sin(angles)


def cosine_table(length):
    indices = jnp.arange(length, dtype=jnp.int32)
    phases = indices[None, :] * (2 * indices[:, None] + 1) % (4 * length)
    return jnp.cos(phases.astype(jnp.float32) * (math.pi / (2 * length)))


def cosine_inverse(length):
    indices = jnp.arange(length, dtype=jnp.int32)
    weights = jnp.where(indices == 0, 1.0, 2.0).astype(jnp.float32)
    return cosine_table(length).T * weights[:, None] / length


def eigen_periodic(waves, length):
    return 2.0 - 2.0 * jnp.cos(waves.astype(jnp.float32) * (2.0 * math.pi / length))


def eigen_wall(waves, length):
    return 2.0 - 2.0 * jnp.cos(waves.astype(jnp.float32) * (math.pi / length))


def invert(spectral, eigen_sum):
    positive = eigen_sum > 0
    return jnp.where(positive, -spectral / jnp.where(positive, eigen_sum, 1.0), 0.0)


def wall_mask(extent, margin, position, groups):
    layer_index = jnp.arange(extent, dtype=jnp.int32)
    bottom = (layer_index < margin) & (position == 0)
    ceiling = (layer_index >= extent - margin) & (position == groups - 1)
    return jnp.where(bottom | ceiling, 0.0, 1.0).astype(jnp.float32)


def poisson(source):
    spanwise_extent, vertical_extent, lengthwise_extent = source.shape
    groups_y = lax.axis_size("gy")
    groups_z = lax.axis_size("gz")
    span_y = spanwise_extent * groups_y
    span_z = vertical_extent * groups_z
    hart_x = cas_table(lengthwise_extent)
    hart_y = cas_table(span_y)
    cos_forward = cosine_table(span_z).reshape(groups_z, vertical_extent, span_z)
    cos_backward = cosine_inverse(span_z).reshape(span_z, groups_z, vertical_extent)
    line_z = eigen_wall(jnp.arange(span_z, dtype=jnp.int32), span_z)
    piece_x = lengthwise_extent // groups_y
    quarter = span_y // groups_z
    table_x = hart_x.reshape(lengthwise_extent, groups_y, piece_x)
    table_y = hart_y.reshape(groups_y, spanwise_extent, groups_z, quarter)
    step_one = jnp.einsum("yzx,xgj->gjyz", source, table_x, precision=highest).reshape(groups_y, -1)
    step_one = lax.all_to_all(step_one, "gy", split_axis=0, concat_axis=0, tiled=True).reshape(
        groups_y, piece_x, spanwise_extent, vertical_extent
    )
    step_two = jnp.einsum("sjyz,syhq->hjqz", step_one, table_y, precision=highest).reshape(
        groups_z, -1
    )
    step_two = lax.all_to_all(step_two, "gz", split_axis=0, concat_axis=0, tiled=True).reshape(
        groups_z, piece_x, quarter, vertical_extent
    )
    spectral = jnp.einsum("tjqc,tck->jqk", step_two, cos_forward, precision=highest)
    wave_x = lax.axis_index("gy") * piece_x + jnp.arange(piece_x, dtype=jnp.int32)
    wave_y = lax.axis_index("gz") * quarter + jnp.arange(quarter, dtype=jnp.int32)
    eigen_sum = (
        eigen_periodic(wave_x, lengthwise_extent)[:, None, None]
        + eigen_periodic(wave_y, span_y)[None, :, None]
        + line_z[None, None, :]
    )
    solved = invert(spectral, eigen_sum)
    step_three = jnp.einsum("jqk,ktc->tjqc", solved, cos_backward, precision=highest).reshape(
        groups_z, -1
    )
    step_three = lax.all_to_all(step_three, "gz", split_axis=0, concat_axis=0, tiled=True).reshape(
        groups_z, piece_x, quarter, vertical_extent
    )
    step_four = (
        jnp.einsum("hjqz,syhq->sjyz", step_three, table_y, precision=highest) * (1.0 / span_y)
    ).reshape(groups_y, -1)
    step_four = lax.all_to_all(step_four, "gy", split_axis=0, concat_axis=0, tiled=True).reshape(
        groups_y, piece_x, spanwise_extent, vertical_extent
    )
    return jnp.einsum("gjyz,xgj->yzx", step_four, table_x, precision=highest) * (
        1.0 / lengthwise_extent
    )


def on_device(dual_flow_speeds, dual_thermal_state, forward_flow_speeds, forward_thermal_state):
    spanwise_extent, vertical_extent, lengthwise_extent = dual_thermal_state.shape
    groups_z = lax.axis_size("gz")
    place_z = lax.axis_index("gz")
    motion_pieces = forward_flow_speeds.astype(jnp.float32)
    forward_thermal_flux = forward_thermal_state.astype(jnp.float32)
    stacked_fields = jnp.concatenate(
        [dual_flow_speeds, dual_thermal_state[None], forward_thermal_flux[None]], 0
    )
    haloed_quantities = padded(stacked_fields, (("gy", 1), ("gz", 2)), 1)
    haloed_quantities = (
        haloed_quantities
        * wall_mask(vertical_extent + 2, 1, place_z, groups_z)[None, None, :, None]
    )
    unprojected_motion, advanced_dual_thermal = tendency_contributions(
        haloed_quantities, motion_pieces
    )
    upper_y = shifted(unprojected_motion[1][0], "gy", -1)
    upper_z = from_behind(unprojected_motion[2][:, 0], "gz", -1)
    next_y = jnp.concatenate([unprojected_motion[1][1:], upper_y[None]], 0)
    next_z = jnp.concatenate([unprojected_motion[2][:, 1:], upper_z[:, None]], 1)
    source = (
        jnp.roll(unprojected_motion[0], -1, axis=2)
        - unprojected_motion[0]
        + (next_y - unprojected_motion[1])
        + (next_z - unprojected_motion[2])
    )
    pressure = poisson(source)
    grad_x = pressure - jnp.roll(pressure, 1, axis=2)
    lower_y = shifted(pressure[spanwise_extent - 1], "gy", 1)
    grad_y = pressure - jnp.concatenate([lower_y[None], pressure[:-1]], 0)
    lower_z = from_behind(pressure[:, vertical_extent - 1], "gz", 1)
    below = jnp.concatenate([lower_z[:, None], pressure[:, :-1]], 1)
    floor_layer = (jnp.arange(vertical_extent, dtype=jnp.int32) == 0) & (place_z == 0)
    grad_z = jnp.where(floor_layer[None, :, None], 0.0, pressure - below)
    advanced_dual_motion = unprojected_motion - jnp.stack([grad_x, grad_y, grad_z])
    return (advanced_dual_motion, advanced_dual_thermal)


def solution(mesh):
    placed = (
        P(None, "gy", "gz", None),
        P("gy", "gz", None),
        P(None, "gy", "gz", None),
        P("gy", "gz", None),
    )
    return jax.shard_map(
        on_device,
        mesh=mesh,
        in_specs=placed,
        out_specs=(P(None, "gy", "gz", None), P("gy", "gz", None)),
        check_vma=False,
    )
```

profile of v0, /device:TPU:1, one launch (start us, length us, event | category | flops | bytes accessed | tf_op | source)
XLA Modules:
  0.0 276.5 jit_solution(11841710461137140810)
XLA Ops:
  1.7 2.1 pad_maximum_fusion.2
  3.8 2.6 collective-permute-start
  10.7 2.7 collective-permute-done.1
  15.5 4.7 %collective-permute-start.3 = (f32[5,10,1,1024]{3,2,1,0:T(1,128)S(1)}, f32[5,10,1,1024]{3,2,1,0:T(1,128)S(1)}, u32[]{:S(2)}, u32[]{:S(2)}) collective-permute-start(f32[5,10,1,1024]{3,2,1,0:T(1,128)S(1)} %get-tuple-element.13), channel_id=1, source_target_pairs={{1,0},{2,1},{3,2},{4,3},{5,4},{6,5},{7,6},{0,7},{9,8},{10,9},{11,1... | collective-permute-start | bytes 614408 | tf_op jit(solution)/shard_map/ppermute | solution.py:24
  32.7 1.9 fusion.13
  37.9 2.9 %collective-permute-start.4 = (f32[16,1024]{1,0:T(8,128)S(1)}, f32[16,1024]{1,0:T(8,128)S(1)}, u32[]{:S(2)}, u32[]{:S(2)}) collective-permute-start(f32[16,1024]{1,0:T(8,128)S(1)} %slice_bitcast_fusion.9), channel_id=1, source_target_pairs={{0,248},{8,0},{16,8},{24,16},{32,24},{40,32},{48,40},{56,48},{64,5... | collective-permute-start | bytes 196616 | tf_op jit(solution)/shard_map/ppermute | solution.py:33
  42.5 37.0 %fusion.5 = f32[32,32,8,16]{0,3,2,1:T(8,128)} fusion(s32[32,32]{0,1:T(8,128)S(1)} %copy-done.10, f32[8,16,1024,1]{2,1,0,3:T(8,128)S(1)} %fusion.142), kind=kOutput, calls=%fused_computation.9 | convolution fusion | flops 1626341376 | bytes 1052672 | tf_op jit(solution)/shard_map/yzx,xgj->gjyz/dot_general | solution.py:123
  79.5 2.6 copy.25
  82.0 11.6 %all-to-all-start = ((f32[32,1,4096]{2,1,0:T(1,128)}), f32[32,1,4096]{2,1,0:T(1,128)S(1)}, u32[]{:S(2)}, u32[]{:S(2)}) async-start(f32[32,1,4096]{2,1,0:T(1,128)} %copy.25), calls=%async_computation | async-start | bytes 1048576 | tf_op jit(solution)/shard_map/all_to_all | solution.py:124
  93.6 11.4 %all-to-all-done = f32[32,1,4096]{2,1,0:T(1,128)S(1)} async-done(((f32[32,1,4096]{2,1,0:T(1,128)}), f32[32,1,4096]{2,1,0:T(1,128)S(1)}, u32[]{:S(2)}, u32[]{:S(2)}) %all-to-all-start) | async-done | bytes 524320 | tf_op jit(solution)/shard_map/all_to_all | solution.py:124
  106.9 3.2 %copy.28 = f32[32,32,8,16]{1,0,2,3:T(8,128)} copy(f32[32,32,8,16]{0,3,2,1:T(8,128)} %bitcast.148) | data formatting | bytes 1048576 | tf_op jit(solution)/shard_map/reshape | solution.py:124
  110.1 9.0 %fusion.23 = f32[8,32,32,16]{1,2,3,0:T(8,128)} fusion(f32[32,32,8,16]{1,0,2,3:T(8,128)} %copy.28, s32[8,32]{1,0:T(8,128)S(1)} %multiply_add_fusion.2, s32[32,8]{0,1:T(8,128)S(1)} %multiply_add_fusion.3), kind=kOutput, calls=%fused_computation.42 | convolution fusion | flops 403636224 | bytes 1050624 | tf_op jit(solution)/shard_map/sjyz,syhq->hjqz/dot_general | solution.py:127
  119.1 5.6 %copy.29 = f32[8,32,32,16]{3,2,1,0:T(8,128)} copy(f32[8,32,32,16]{1,2,3,0:T(8,128)} %fusion.23) | data formatting | bytes 1048576 | tf_op jit(solution)/shard_map/sjyz,syhq->hjqz/transpose | solution.py:127
  124.7 4.4 %all_to_all.32 = f32[8,1,16384]{2,1,0:T(1,128)} reshape(f32[8,32,32,16]{3,2,1,0:T(8,128)} %copy.29) | data formatting | bytes 1048576 | tf_op jit(solution)/shard_map/all_to_all | solution.py:130
  129.1 9.0 %all-to-all-start.1 = ((f32[8,1,16384]{2,1,0:T(1,128)}), f32[8,1,16384]{2,1,0:T(1,128)S(1)}, u32[]{:S(2)}, u32[]{:S(2)}) async-start(f32[8,1,16384]{2,1,0:T(1,128)} %all_to_all.32), calls=%async_computation.1 | async-start | bytes 1048576 | tf_op jit(solution)/shard_map/all_to_all | solution.py:130
  138.3 17.7 %all-to-all-done.1 = f32[8,1,16384]{2,1,0:T(1,128)S(1)} async-done(((f32[8,1,16384]{2,1,0:T(1,128)}), f32[8,1,16384]{2,1,0:T(1,128)S(1)}, u32[]{:S(2)}, u32[]{:S(2)}) %all-to-all-start.1) | async-done | bytes 524320 | tf_op jit(solution)/shard_map/all_to_all | solution.py:130
  157.2 3.4 %reshape.262 = f32[8,32,32,16]{3,2,1,0:T(8,128)} reshape(f32[8,16384]{1,0:T(8,128)S(1)} %reduce) | data formatting | bytes 1048576 | tf_op jit(solution)/shard_map/reshape | solution.py:130
  160.6 5.9 %fusion.38 = f32[32,32,128,1]{2,1,0,3:T(8,128)S(1)} fusion(f32[8,32,32,16]{3,2,1,0:T(8,128)} %reshape.262, f32[128]{0:T(128)S(1)} %multiply_subtract_fusion, f32[32,32]{1,0:T(8,128)S(1)} %broadcast_add_fusion, s32[8,16]{1,0:T(8,128)S(1)} %multiply_add_fusion.1), kind=kOutput, calls=%fused_computation.58 | convolution fusion | flops 202342400 | bytes 1053696 | tf_op jit(solution)/shard_map/tjqc,tck->jqk/dot_general | solution.py:133
  166.5 4.1 %convolution_bitcast_fusion = f32[8,32,32,16]{2,3,1,0:T(8,128)} fusion(f32[32,32,128,1]{2,1,0,3:T(8,128)S(1)} %fusion.38, f32[128]{0:T(128)S(1)} %compare_select_fusion, s32[8,16]{1,0:T(8,128)S(1)} %multiply_add_fusion.1), kind=kOutput, calls=%fused_computation.43 | convolution fusion | flops 201588736 | bytes 1049600 | tf_op jit(solution)/shard_map/jqk,ktc->tjqc/dot_general | solution.py:142
  170.6 3.9 %copy.32 = f32[8,32,32,16]{3,2,1,0:T(8,128)} copy(f32[8,32,32,16]{2,3,1,0:T(8,128)} %convolution_bitcast_fusion) | data formatting | bytes 1048576 | tf_op jit(solution)/shard_map/jqk,ktc->tjqc/transpose | solution.py:142
  174.5 3.7 %all_to_all.33 = f32[8,1,16384]{2,1,0:T(1,128)S(1)} reshape(f32[8,32,32,16]{3,2,1,0:T(8,128)} %copy.32) | data formatting | bytes 1048576 | tf_op jit(solution)/shard_map/all_to_all | solution.py:145
  178.2 20.1 %all_to_all.38 = f32[8,1,16384]{2,1,0:T(1,128)S(1)} all-to-all(f32[8,1,16384]{2,1,0:T(1,128)S(1)} %all_to_all.33), channel_id=1, replica_groups=mesh['gy'=32,'gz'=8] {'gz'}, dimensions={0} | all-to-all | bytes 1048576 | tf_op jit(solution)/shard_map/all_to_all | solution.py:145
  199.6 3.4 %reshape.263 = f32[8,32,32,16]{3,2,1,0:T(8,128)} reshape(f32[8,16384]{1,0:T(8,128)S(1)} %reduce.1) | data formatting | bytes 1048576 | tf_op jit(solution)/shard_map/reshape | solution.py:145
  203.0 4.5 %copy.34 = f32[8,32,32,16]{2,1,0,3:T(8,128)} copy(f32[8,32,32,16]{3,2,1,0:T(8,128)} %reshape.263) | data formatting | bytes 1048576 | tf_op jit(solution)/shard_map/reshape | solution.py:145
  207.5 13.8 %fusion.18 = f32[32,32,8,16]{1,0,3,2:T(8,128)} fusion(f32[8,32,32,16]{2,1,0,3:T(8,128)} %copy.34, s32[8,32]{1,0:T(8,128)S(1)} %multiply_add_fusion.2, s32[32,8]{0,1:T(8,128)S(1)} %multiply_add_fusion.3), kind=kOutput, calls=%fused_computation.34 | convolution fusion | flops 403767296 | bytes 1050624 | tf_op jit(solution)/shard_map/hjqz,syhq->sjyz/dot_general | solution.py:149
  221.4 3.8 %copy.35 = f32[32,32,8,16]{0,3,2,1:T(8,128)} copy(f32[32,32,8,16]{1,0,3,2:T(8,128)} %fusion.18) | data formatting | bytes 1048576 | tf_op jit(solution)/shard_map/mul | solution.py:149
  225.2 2.6 copy.36
  227.8 4.7 %all-to-all-start.3 = ((f32[32,1,4096]{2,1,0:T(1,128)}), f32[32,1,4096]{2,1,0:T(1,128)S(1)}, u32[]{:S(2)}, u32[]{:S(2)}) async-start(f32[32,1,4096]{2,1,0:T(1,128)} %copy.36), calls=%async_computation.3 | async-start | bytes 1048576 | tf_op jit(solution)/shard_map/all_to_all | solution.py:151
  232.5 11.4 %all-to-all-done.3 = f32[32,1,4096]{2,1,0:T(1,128)S(1)} async-done(((f32[32,1,4096]{2,1,0:T(1,128)}), f32[32,1,4096]{2,1,0:T(1,128)S(1)}, u32[]{:S(2)}, u32[]{:S(2)}) %all-to-all-start.3) | async-done | bytes 524320 | tf_op jit(solution)/shard_map/all_to_all | solution.py:151
  245.7 23.0 %fusion.39 = f32[8,16,1024]{2,1,0:T(8,128)S(1)} fusion(f32[32,32,8,16]{0,3,2,1:T(8,128)} %bitcast.153, s32[32,32]{0,1:T(8,128)S(1)} %copy-done.10), kind=kOutput, calls=%fused_computation.59 | convolution fusion | flops 1626472448 | bytes 1052672 | tf_op jit(solution)/shard_map/gjyz,xgj->yzx/dot_general | solution.py:154
  269.4 2.2 collective-permute-start.7
  271.6 2.8 fusion.49
  (83 shorter events, 33.5 us)
Async XLA Ops:
  1.6 11.8 %copy-start.1 = (f32[3,8,16,1024]{3,2,1,0:T(8,128)S(1)}, f32[3,8,16,1024]{3,2,1,0:T(8,128)}, u32[]{:S(2)}) copy-start(f32[3,8,16,1024]{3,2,1,0:T(8,128)} %param.4) | copy-start | bytes 4718596
  1.6 11.7 %copy-start.5 = (f32[8,16,1024]{2,1,0:T(8,128)S(1)}, f32[8,16,1024]{2,1,0:T(8,128)}, u32[]{:S(2)}) copy-start(f32[8,16,1024]{2,1,0:T(8,128)} %param.5) | copy-start | bytes 1572868
  3.8 6.9 %collective-permute-start = (f32[5,1,16,1024]{3,2,1,0:T(8,128)}, f32[5,1,16,1024]{3,2,1,0:T(8,128)S(1)}, u32[]{:S(2)}, u32[]{:S(2)}) collective-permute-start(f32[5,1,16,1024]{3,2,1,0:T(8,128)} %get-tuple-element.14), channel_id=1, source_target_pairs={{0,8},{8,16},{16,24},{24,32},{32,40},{40,48},{48,56},{56,64},{64,7... | collective-permute-start | bytes 983048 | tf_op jit(solution)/shard_map/ppermute | solution.py:22
  6.4 7.0 %collective-permute-start.1 = (f32[5,1,16,1024]{3,2,1,0:T(8,128)}, f32[5,1,16,1024]{3,2,1,0:T(8,128)S(1)}, u32[]{:S(2)}, u32[]{:S(2)}) collective-permute-start(f32[5,1,16,1024]{3,2,1,0:T(8,128)} %get-tuple-element.15), channel_id=1, source_target_pairs={{8,0},{16,8},{24,16},{32,24},{40,32},{48,40},{56,48},{64,56},{72,6... | collective-permute-start | bytes 983048 | tf_op jit(solution)/shard_map/ppermute | solution.py:24
  13.4 2.1 copy-start.8
  13.8 8.8 %collective-permute-start.2 = (f32[5,10,1,1024]{3,2,1,0:T(1,128)S(1)}, f32[5,10,1,1024]{3,2,1,0:T(1,128)S(1)}, u32[]{:S(2)}, u32[]{:S(2)}) collective-permute-start(f32[5,10,1,1024]{3,2,1,0:T(1,128)S(1)} %get-tuple-element.12), channel_id=1, source_target_pairs={{0,1},{1,2},{2,3},{3,4},{4,5},{5,6},{6,7},{7,0},{8,9},{9,10},{10,1... | collective-permute-start | bytes 614408 | tf_op jit(solution)/shard_map/ppermute | solution.py:22
  15.5 7.4 %collective-permute-start.3 = (f32[5,10,1,1024]{3,2,1,0:T(1,128)S(1)}, f32[5,10,1,1024]{3,2,1,0:T(1,128)S(1)}, u32[]{:S(2)}, u32[]{:S(2)}) collective-permute-start(f32[5,10,1,1024]{3,2,1,0:T(1,128)S(1)} %get-tuple-element.13), channel_id=1, source_target_pairs={{1,0},{2,1},{3,2},{4,3},{5,4},{6,5},{7,6},{0,7},{9,8},{10,9},{11,1... | collective-permute-start | bytes 614408 | tf_op jit(solution)/shard_map/ppermute | solution.py:24
  20.1 2.7 copy-start.9
  24.3 10.4 %copy-start = (f32[5,10,18,1024]{3,2,1,0:T(8,128)}, f32[5,10,18,1024]{3,2,1,0:T(8,128)S(1)}, u32[]{:S(2)}) copy-start(f32[5,10,18,1024]{3,2,1,0:T(8,128)S(1)} %maximum_multiply_fusion) | copy-start | bytes 11059204
  29.7 2.9 %copy-start.2 = (f32[5,8,16,1024]{3,2,1,0:T(8,128)}, f32[5,8,16,1024]{3,2,1,0:T(8,128)S(1)}, u32[]{:S(2)}) copy-start(f32[5,8,16,1024]{3,2,1,0:T(8,128)S(1)} %fusion.12) | copy-start | bytes 7864324
  29.7 1.4 copy-start.6
  29.8 2.0 copy-start.7
  32.7 2.0 copy-start.3
  32.7 2.0 slice-start
  34.7 1.4 copy-start.4
  36.5 5.9 %copy-start.10 = (s32[32,32]{0,1:T(8,128)S(1)}, s32[32,32]{0,1:T(8,128)}, u32[]{:S(2)}) copy-start(s32[32,32]{0,1:T(8,128)} %multiply_add_fusion) | copy-start | bytes 12292
  36.6 4.7 %collective-permute-start.5 = (f32[8,1024]{1,0:T(8,128)S(1)}, f32[8,1024]{1,0:T(8,128)S(1)}, u32[]{:S(2)}, u32[]{:S(2)}) collective-permute-start(f32[8,1024]{1,0:T(8,128)S(1)} %bitcast.157), channel_id=1, source_target_pairs={{1,0},{2,1},{3,2},{4,3},{5,4},{6,5},{7,6},{9,8},{10,9},{11,10},{12... | collective-permute-start | bytes 98312 | tf_op jit(solution)/shard_map/ppermute | solution.py:39
  37.9 4.2 %collective-permute-start.4 = (f32[16,1024]{1,0:T(8,128)S(1)}, f32[16,1024]{1,0:T(8,128)S(1)}, u32[]{:S(2)}, u32[]{:S(2)}) collective-permute-start(f32[16,1024]{1,0:T(8,128)S(1)} %slice_bitcast_fusion.9), channel_id=1, source_target_pairs={{0,248},{8,0},{16,8},{24,16},{32,24},{40,32},{48,40},{56,48},{64,5... | collective-permute-start | bytes 196616 | tf_op jit(solution)/shard_map/ppermute | solution.py:33
  82.0 23.0 %all-to-all-start = ((f32[32,1,4096]{2,1,0:T(1,128)}), f32[32,1,4096]{2,1,0:T(1,128)S(1)}, u32[]{:S(2)}, u32[]{:S(2)}) async-start(f32[32,1,4096]{2,1,0:T(1,128)} %copy.25), calls=%async_computation | async-start | bytes 1048576 | tf_op jit(solution)/shard_map/all_to_all | solution.py:124
  129.1 26.9 %all-to-all-start.1 = ((f32[8,1,16384]{2,1,0:T(1,128)}), f32[8,1,16384]{2,1,0:T(1,128)S(1)}, u32[]{:S(2)}, u32[]{:S(2)}) async-start(f32[8,1,16384]{2,1,0:T(1,128)} %all_to_all.32), calls=%async_computation.1 | async-start | bytes 1048576 | tf_op jit(solution)/shard_map/all_to_all | solution.py:130
  227.8 16.2 %all-to-all-start.3 = ((f32[32,1,4096]{2,1,0:T(1,128)}), f32[32,1,4096]{2,1,0:T(1,128)S(1)}, u32[]{:S(2)}, u32[]{:S(2)}) async-start(f32[32,1,4096]{2,1,0:T(1,128)} %copy.36), calls=%async_computation.3 | async-start | bytes 1048576 | tf_op jit(solution)/shard_map/all_to_all | solution.py:151
  268.7 5.8 %collective-permute-start.6 = (f32[16,1024]{1,0:T(8,128)S(1)}, f32[16,1024]{1,0:T(8,128)S(1)}, u32[]{:S(2)}, u32[]{:S(2)}) collective-permute-start(f32[16,1024]{1,0:T(8,128)S(1)} %slice_bitcast_fusion.8), channel_id=1, source_target_pairs={{0,8},{8,16},{16,24},{24,32},{32,40},{40,48},{48,56},{56,64},{64,7... | collective-permute-start | bytes 196616 | tf_op jit(solution)/shard_map/ppermute | solution.py:33
  269.4 5.1 %collective-permute-start.7 = (f32[8,1024]{1,0:T(8,128)S(1)}, f32[8,1024]{1,0:T(8,128)S(1)}, u32[]{:S(2)}, u32[]{:S(2)}) collective-permute-start(f32[8,1024]{1,0:T(8,128)S(1)} %bitcast.158), channel_id=1, source_target_pairs={{0,1},{1,2},{2,3},{3,4},{4,5},{5,6},{6,7},{8,9},{9,10},{10,11},{11... | collective-permute-start | bytes 98312 | tf_op jit(solution)/shard_map/ppermute | solution.py:39
where the time goes:
time: 281 us; the launch traced here: 277 us
  matrix products  92.8 us (33%)
  local copies, waits for them, and re-layouts  51.9 us (18%)
  waiting for transfers between devices  47.9 us (17%)
  starting transfers between devices  41.9 us (15%)
  other arithmetic  20.5 us (7%)
  blocking collectives  20.1 us (7%)
    dot_general x1, matrix products, poisson(): jnp.einsum('yzx,xgj->gjyz', source, table_x, precision=highest)  37 us
    dot_general x1, matrix products, poisson(): jnp.einsum('gjyz,xgj->yzx', step_four, table_x, precision=highest)  23 us
    all_to_all x1, blocking collectives, poisson(): lax.all_to_all(step_three, 'gz', split_axis=0, concat_axis=0, tiled=True)  20.1 us
    all_to_all x1, waiting for transfers between devices, poisson(): lax.all_to_all(step_two, 'gz', split_axis=0, concat_axis=0, tiled=True)  17.7 us
    dot_general x1, matrix products, poisson(): jnp.einsum('hjqz,syhq->sjyz', step_three, table_y, precision=highest)  13.8 us
    all_to_all x1, starting transfers between devices, poisson(): lax.all_to_all(step_one, 'gy', split_axis=0, concat_axis=0, tiled=True)  11.6 us
    all_to_all x1, waiting for transfers between devices, poisson(): lax.all_to_all(step_four, 'gy', split_axis=0, concat_axis=0, tiled=True)  11.4 us
    all_to_all x1, waiting for transfers between devices, poisson(): lax.all_to_all(step_one, 'gy', split_axis=0, concat_axis=0, tiled=True)  11.4 us
  transfers between devices with their start and end apart: 11, of which 9 were waited for; matrix products, arithmetic and copies ran while one was open for 2% of the time, Pallas kernels for 0%

commit v1 on v0

v1 whole, which is shorter than its diff:
```python
import functools

import jax
import jax.numpy as jnp
import ml_dtypes
import numpy as np
from jax import lax
from jax.experimental import pallas as pl
from jax.experimental.pallas import tpu as pltpu
from jax.sharding import PartitionSpec as P

F32 = jnp.float32
BF16 = jnp.bfloat16
ROWS = 8
LAYERS = 16
WAVES = 32
QUADS = LAYERS // 4
PIECE = 8 * (QUADS + 1)
VMEM = pl.BlockSpec(memory_space=pltpu.VMEM)
SMEM = pl.BlockSpec(memory_space=pltpu.SMEM)


def two_parts(table):
    head = table.astype(ml_dtypes.bfloat16)
    return head, (table - head.astype(np.float64)).astype(ml_dtypes.bfloat16)


def cas(phases, length):
    angles = (phases % length) * (2.0 * np.pi / length)
    return np.cos(angles) + np.sin(angles)


@functools.lru_cache(None)
def tables(size_x, size_y):
    half = np.arange(size_x // 2)
    even = two_parts(cas(half[:, None] * half[None, :], size_x // 2))
    odd = two_parts(cas(half[:, None] * (2 * half[None, :] + 1), size_x))
    full = np.arange(size_y)
    span = two_parts(cas(full[:, None] * full[None, :], size_y))
    waves = np.concatenate([2 * half, 2 * half + 1])
    line_x = 4.0 * np.sin(np.pi * waves / size_x) ** 2
    line_x = np.tile(line_x.reshape(-1, WAVES), (1, 128 // WAVES)).astype(np.float32)
    row = np.arange(size_y // 4)[:, None]
    lane = np.arange(128)[None, :]
    wave_y = 32 * (row // 8) + 8 * (lane // WAVES) + row % 8
    line_y = (4.0 * np.sin(np.pi * wave_y / size_y) ** 2).astype(np.float32)
    return even, odd, span, line_x, line_y


def split(values):
    head = values.astype(BF16)
    return head, (values - head.astype(F32)).astype(BF16)


def lane_group(shape):
    return lax.broadcasted_iota(jnp.int32, shape, len(shape) - 1) // WAVES


def swap_groups(a):
    axis = a[0].ndim - 1
    group = lane_group(a[0].shape)
    low = group < 2
    even = group % 2 == 0
    b0 = jnp.where(low, a[0], pltpu.roll(a[2], 64, axis))
    b2 = jnp.where(low, pltpu.roll(a[0], 64, axis), a[2])
    b1 = jnp.where(low, a[1], pltpu.roll(a[3], 64, axis))
    b3 = jnp.where(low, pltpu.roll(a[1], 64, axis), a[3])
    return (
        jnp.where(even, b0, pltpu.roll(b1, 32, axis)),
        jnp.where(even, pltpu.roll(b0, 96, axis), b1),
        jnp.where(even, b2, pltpu.roll(b3, 32, axis)),
        jnp.where(even, pltpu.roll(b2, 96, axis), b3),
    )


def dot(a, b):
    return jnp.dot(a, b, preferred_element_type=F32)


def dot_nt(a, b):
    return lax.dot_general(a, b, (((1,), (1,)), ((), ())), preferred_element_type=F32)


def product(values, head, tail, how):
    a, b = split(values)
    return how(a, head) + (how(b, head) + how(a, tail))


def keep(ref, start, values):
    for b in range(ref.shape[0]):
        ref[b, pl.ds(start, values.shape[0]), :] = values[:, b * 128:(b + 1) * 128]


def kept(ref, start, count):
    return jnp.concatenate([ref[b, pl.ds(start, count), :] for b in range(ref.shape[0])], 1)


def stencil_kernel(
    motion, thermal, flow, base, y_low, y_high, z_low, z_high, even_h, even_t, odd_h, odd_t,
    provisional, thermal_out, message, source, lines, row_p, layer_p,
):
    size_x = motion.shape[-1]
    row = lax.broadcasted_iota(jnp.int32, (LAYERS, size_x), 0)
    top = row == LAYERS - 1
    bottom = row == 0

    def field(c, y):
        if c < 3:
            return motion[c, y]
        if c == 3:
            return thermal[y]
        return base[y].astype(F32)

    def neighbours(c, y):
        centre = field(c, y)
        y_plus = field(c, y + 1) if y < ROWS - 1 else y_high[c]
        y_minus = field(c, y - 1) if y > 0 else y_low[c]
        z_plus = jnp.where(top, z_high[c, y:y + 1, :], pltpu.roll(centre, LAYERS - 1, 0))
        z_minus = jnp.where(bottom, z_low[c, y:y + 1, :], pltpu.roll(centre, 1, 0))
        x_plus = pltpu.roll(centre, size_x - 1, 1)
        x_minus = pltpu.roll(centre, 1, 1)
        return centre, x_plus, x_minus, y_plus, y_minus, z_plus, z_minus

    carried = None
    for y in range(ROWS):
        weights = []
        for c in range(3):
            speed = flow[c, y].astype(F32) * 0.1
            weights += [0.02 + speed, 0.02 - speed]
        _, hx, gx, hy, gy, hz, gz = neighbours(4, y)
        slopes = (hx - gx, hy - gy, hz - gz)
        heat = thermal[y] * 0.1
        moved = []
        for c in range(4):
            parts = neighbours(c, y)
            value = parts[0] * 0.88
            for weight, part in zip(weights, parts[1:]):
                value = value + weight * part
            if c < 3:
                value = value + heat * slopes[c]
                provisional[c, y] = value
            else:
                thermal_out[y] = value + 0.2 * motion[2, y]
            moved.append(value)
        p0, p1, p2 = moved[:3]
        if y == 0:
            keep(row_p, 0, p1)
        else:
            keep(source, (y - 1) * LAYERS, carried + p1)
        keep(layer_p, y, p2[0:1, :])
        above = jnp.where(top, 0.0, pltpu.roll(p2, LAYERS - 1, 0))
        carried = (pltpu.roll(p0, size_x - 1, 1) - p0) - p1 + (above - p2)
    keep(source, (ROWS - 1) * LAYERS, carried)

    for b in range(size_x // 128):
        lanes = pl.ds(b * 128, 128)
        for j in range(4):
            for q in range(QUADS):
                lines[pl.ds(j * PIECE + q * 8, 8), lanes] = source[b, pl.ds(4 * q + j, ROWS, stride=LAYERS), :]
            lines[pl.ds(j * PIECE + 32, 4), lanes] = row_p[b, pl.ds(j, 4, stride=4), :]
            lines[pl.ds(j * PIECE + 36, 2), lanes] = layer_p[b, pl.ds(j, 2, stride=4), :]
            lines[pl.ds(j * PIECE + 38, 2), lanes] = jnp.zeros((2, 128), F32)
    near = lines[:, : size_x // 2]
    far = lines[:, size_x // 2:]
    evens = product(near + far, even_h[...], even_t[...], dot)
    odds = product(near - far, odd_h[...], odd_t[...], dot)
    for block in range(size_x // 128):
        part, at = (evens, block) if block < size_x // 256 else (odds, block - size_x // 256)
        a = [part[j * PIECE:(j + 1) * PIECE, at * 128:(at + 1) * 128] for j in range(4)]
        for i, piece in enumerate(swap_groups(a)):
            message[4 * block + i] = piece


def mode_constants(place, line_x, line_y):
    a = line_x[pl.ds(place[0], 1), :] + line_y[...]
    sinh = jnp.sqrt(a * (1.0 + 0.25 * a))
    lam = 1.0 / (1.0 + 0.5 * a + sinh)
    return a, sinh, lam


def wall_factors(lam, slab, slabs):
    square = lam * lam
    powers = [jnp.ones_like(lam), square]
    for m in range(2, LAYERS + 1):
        powers.append(powers[m // 2] * powers[m - m // 2])
    step = powers[LAYERS]

    def raised(count):
        value = lam
        factor = step
        for bit in range((slabs - 1).bit_length()):
            value = jnp.where((count // (1 << bit)) % 2 == 1, value * factor, value)
            factor = factor * factor
        return value

    low = raised(slab)
    high = raised(slabs - 1 - slab)
    below = low * (1.0 / square)
    floor = [1.0 + jnp.where(slab == 0, lam, below)] + [1.0 + low * powers[l] for l in range(LAYERS)]
    ceiling = [1.0 + high * powers[LAYERS - 1 - l] for l in range(-1, LAYERS)]
    return floor, ceiling, powers


def down_kernel(place, received, span_h, span_t, line_x, line_y, spectral, handed):
    sources = received.shape[0]
    size_y = sources * ROWS
    slabs = handed.shape[0]
    slab = place[1]
    row = lax.broadcasted_iota(jnp.int32, (sources, 8, 128), 1)
    group = lane_group((sources, 8, 128))
    extra = received[:, 8 * QUADS:, :]
    onward = jnp.concatenate([extra[1:], extra[:1]], 0)
    columns = []
    for q in range(QUADS):
        more = jnp.broadcast_to(onward[:, q:q + 1, :], (sources, 8, 128))
        values = received[:, 8 * q:8 * q + 8, :] + jnp.where(row == ROWS - 1, more, 0.0)
        columns.append(values.reshape(size_y, 128))
    first = jnp.broadcast_to(extra[:, 4:5, :], (sources, 8, 128))
    second = jnp.broadcast_to(extra[:, 5:6, :], (sources, 8, 128))
    layer = jnp.where(row < 4, first, second)
    layer = jnp.where((row % 4 == group) & (slab > 0), layer, 0.0)
    columns.append(layer.reshape(size_y, 128))
    stacked = jnp.concatenate(columns, 1)
    head, tail = split(stacked)
    waves = dot(span_h[...], head) + (dot(span_h[...], tail) + dot(span_t[...], head))

    last = waves[:, 128 * QUADS:]
    last = last + pltpu.roll(last, 64, 1)
    last = (last + pltpu.roll(last, 32, 1)).reshape(size_y // 32, 4, 8, 128)
    modes = size_y // 4
    mode_group = lane_group((modes, 128))
    pick = [last[:, i].reshape(modes, 128) for i in range(4)]
    layers = [
        jnp.where(
            mode_group < 2,
            jnp.where(mode_group == 0, pick[0], pick[1]),
            jnp.where(mode_group == 2, pick[2], pick[3]),
        )
    ]
    for q in range(QUADS):
        block = waves[:, 128 * q:128 * (q + 1)].reshape(size_y // 32, 4, 8, 128)
        layers += swap_groups([block[:, i].reshape(modes, 128) for i in range(4)])
    _, _, lam = mode_constants(place, line_x, line_y)
    floor, ceiling, _ = wall_factors(lam, slab, slabs)
    upward = jnp.zeros_like(lam)
    downward = jnp.zeros_like(lam)
    for l in range(LAYERS + 1):
        spectral[l] = layers[l]
        upward = lam * upward + floor[l] * layers[l]
        m = LAYERS - l
        downward = lam * downward + ceiling[m] * layers[m]
    for d in range(slabs):
        handed[d] = jnp.where(d > slab, upward, downward)


def up_kernel(place, spectral, handed, span_h, span_t, line_x, line_y, message):
    size_y = span_h.shape[0]
    sources = size_y // ROWS
    slabs = handed.shape[0]
    size_x = line_x.shape[0] * WAVES
    size_z = slabs * LAYERS
    slab = place[1]
    a, sinh, lam = mode_constants(place, line_x, line_y)
    floor, ceiling, powers = wall_factors(lam, slab, slabs)
    scale = 1.0 / (size_x * size_y)
    whole = powers[LAYERS]
    reach = powers[LAYERS // 2]
    for _ in range((slabs - 1).bit_length()):
        whole = whole * whole
    zero = a == 0.0
    weight = (-scale) / jnp.where(zero, 1.0, 2.0 * sinh * (1.0 - whole))
    weight = jnp.where(zero, 0.0, weight)
    upward = jnp.zeros_like(lam)
    downward = jnp.zeros_like(lam)
    for d in range(slabs - 1):
        upward = jnp.where(d < slab, reach * upward + handed[d], upward)
        e = slabs - 1 - d
        downward = jnp.where(e > slab, reach * downward + handed[e], downward)
    below = []
    for l in range(LAYERS + 1):
        upward = (lam * upward if l else upward) + floor[l] * spectral[l]
        below.append(upward)
    pressure = [None] * (LAYERS + 1)
    for l in reversed(range(LAYERS + 1)):
        pressure[l] = weight * (ceiling[l] * below[l] + floor[l] * downward)
        if l == LAYERS:
            mean = (0.5 / size_z) * (below[l][:8] + downward[:8])
        downward = lam * (downward + ceiling[l] * spectral[l])
    modes = size_y // 4
    flat = jnp.zeros((8, 128), F32)
    first_zero = zero[:8]
    for l in range(LAYERS + 1):
        if l:
            count = (slab * LAYERS + (l - 1)).astype(F32)
            flat = flat + (0.5 * below[l - 1][:8] - count * mean)
        pressure[l] = jnp.concatenate(
            [jnp.where(first_zero, flat * scale, pressure[l][:8]), pressure[l][8:]], 0
        )

    columns = []
    tall = (size_y // 32, 1, 8, 128)
    for q in range(QUADS):
        block = swap_groups(pressure[1 + 4 * q:5 + 4 * q])
        columns.append(jnp.concatenate([b.reshape(tall) for b in block], 1).reshape(size_y, 128))
    mode_group = lane_group((modes, 128))
    spread = []
    for i in range(4):
        part = jnp.where(mode_group == i, pressure[0], 0.0)
        part = part + pltpu.roll(part, 64, 1)
        spread.append((part + pltpu.roll(part, 32, 1)).reshape(tall))
    columns.append(jnp.concatenate(spread, 1).reshape(size_y, 128))
    stacked = jnp.concatenate(columns, 1)
    head, tail = split(stacked)
    values = dot(span_h[...], head) + (dot(span_h[...], tail) + dot(span_t[...], head))

    row = lax.broadcasted_iota(jnp.int32, (sources, 8, 128), 1)
    group = lane_group((sources, 8, 128))
    extra = jnp.zeros((sources, 8, 128), F32)
    for q in range(QUADS):
        block = values[:, 128 * q:128 * (q + 1)].reshape(sources, 8, 128)
        message[:, 8 * q:8 * q + 8, :] = block
        edge = jnp.concatenate([block[-1:], block[:-1]], 0)[:, ROWS - 1:ROWS, :]
        extra = jnp.where(row == q, jnp.broadcast_to(edge, extra.shape), extra)
    layer = values[:, 128 * QUADS:].reshape(sources, 8, 128)
    layer = jnp.where(row % 4 == group, layer, 0.0)
    layer = layer + pltpu.roll(layer, 7, 1)
    layer = layer + pltpu.roll(layer, 6, 1)
    extra = jnp.where(row == 4, jnp.broadcast_to(layer[:, 0:1, :], extra.shape), extra)
    extra = jnp.where(row == 5, jnp.broadcast_to(layer[:, 4:5, :], extra.shape), extra)
    message[:, 8 * QUADS:, :] = extra


def gradient_kernel(
    place, received, even_h, even_t, odd_h, odd_t, provisional, motion, lines, pressure, row_p, layer_p
):
    size_x = provisional.shape[-1]
    for block in range(size_x // 128):
        for j, piece in enumerate(swap_groups([received[4 * block + i] for i in range(4)])):
            lines[j * PIECE:(j + 1) * PIECE, block * 128:(block + 1) * 128] = piece
    evens = product(lines[:, : size_x // 2], even_h[...], even_t[...], dot)
    odds = product(lines[:, size_x // 2:], odd_h[...], odd_t[...], dot_nt)
    lines[:, : size_x // 2] = evens + odds
    lines[:, size_x // 2:] = evens - odds
    for b in range(size_x // 128):
        lanes = pl.ds(b * 128, 128)
        for j in range(4):
            for q in range(QUADS):
                pressure[b, pl.ds(4 * q + j, ROWS, stride=LAYERS), :] = lines[pl.ds(j * PIECE + q * 8, 8), lanes]
            row_p[b, pl.ds(j, 4, stride=4), :] = lines[pl.ds(j * PIECE + 32, 4), lanes]
            layer_p[b, pl.ds(j, 2, stride=4), :] = lines[pl.ds(j * PIECE + 36, 2), lanes]
    bottom = lax.broadcasted_iota(jnp.int32, (LAYERS, size_x), 0) == 0
    for y in range(ROWS):
        p = kept(pressure, y * LAYERS, LAYERS)
        before = kept(row_p, 0, LAYERS) if y == 0 else kept(pressure, (y - 1) * LAYERS, LAYERS)
        below = jnp.where(bottom, kept(layer_p, y, 1), pltpu.roll(p, 1, 0))
        slope_z = jnp.where(bottom & (place[1] == 0), 0.0, p - below)
        motion[0, y] = provisional[0, y] - (p - pltpu.roll(p, 1, 1))
        motion[1, y] = provisional[1, y] - (p - before)
        motion[2, y] = provisional[2, y] - slope_z


def shifted(value, axis, by, periodic):
    size = lax.axis_size(axis)
    pairs = [(i, (i + by) % size) for i in range(size) if periodic or 0 <= i + by < size]
    return lax.ppermute(value, axis, pairs)


def exchanged(pieces, axis):
    return lax.all_to_all(pieces, axis, split_axis=0, concat_axis=0, tiled=True)


def shape_of(*shape):
    return jax.ShapeDtypeStruct(shape, F32)


def on_device(dual_motion, dual_thermal, flow, base):
    size_x = dual_thermal.shape[-1]
    groups_y = lax.axis_size("gy")
    groups_z = lax.axis_size("gz")
    even, odd, span, line_x, line_y = tables(size_x, ROWS * groups_y)
    even_h, even_t = map(jnp.asarray, even)
    odd_h, odd_t = map(jnp.asarray, odd)
    span_h, span_t = map(jnp.asarray, span)
    line_x, line_y = jnp.asarray(line_x), jnp.asarray(line_y)
    modes = line_y.shape[0]
    place = jnp.stack([lax.axis_index("gy"), lax.axis_index("gz")]).astype(jnp.int32)
    params = pltpu.CompilerParams(vmem_limit_bytes=48 << 20)

    def side(index, dim):
        def cut(a, at):
            return lax.index_in_dim(a, index, at, keepdims=False)

        return jnp.concatenate(
            [
                cut(dual_motion, dim + 1),
                cut(dual_thermal, dim)[None],
                cut(base, dim)[None].astype(F32),
            ],
            0,
        )

    y_low = shifted(side(ROWS - 1, 0), "gy", 1, True)
    y_high = shifted(side(0, 0), "gy", -1, True)
    z_low = shifted(side(LAYERS - 1, 1), "gz", 1, False)
    z_high = shifted(side(0, 1), "gz", -1, False)

    provisional, thermal_out, message = pl.pallas_call(
        stencil_kernel,
        out_shape=(
            shape_of(3, ROWS, LAYERS, size_x),
            shape_of(ROWS, LAYERS, size_x),
            shape_of(groups_y, PIECE, 128),
        ),
        in_specs=[VMEM] * 12,
        out_specs=(VMEM,) * 3,
        scratch_shapes=[
            pltpu.VMEM((size_x // 128, ROWS * LAYERS, 128), F32),
            pltpu.VMEM((4 * PIECE, size_x), F32),
            pltpu.VMEM((size_x // 128, LAYERS, 128), F32),
            pltpu.VMEM((size_x // 128, ROWS, 128), F32),
        ],
        compiler_params=params,
        name="stencil",
    )(
        dual_motion, dual_thermal, flow, base, y_low, y_high, z_low, z_high,
        even_h, even_t, odd_h, odd_t,
    )
    received = exchanged(message, "gy")
    spectral, handed = pl.pallas_call(
        down_kernel,
        out_shape=(shape_of(LAYERS + 1, modes, 128), shape_of(groups_z, modes, 128)),
        in_specs=[SMEM] + [VMEM] * 5,
        out_specs=(VMEM,) * 2,
        compiler_params=params,
        name="down",
    )(place, received, span_h, span_t, line_x, line_y)
    handed = exchanged(handed, "gz")
    message = pl.pallas_call(
        up_kernel,
        out_shape=shape_of(groups_y, PIECE, 128),
        in_specs=[SMEM] + [VMEM] * 6,
        out_specs=VMEM,
        compiler_params=params,
        name="up",
    )(place, spectral, handed, span_h, span_t, line_x, line_y)
    received = exchanged(message, "gy")
    motion = pl.pallas_call(
        gradient_kernel,
        out_shape=shape_of(3, ROWS, LAYERS, size_x),
        in_specs=[SMEM] + [VMEM] * 6,
        out_specs=VMEM,
        scratch_shapes=[
            pltpu.VMEM((4 * PIECE, size_x), F32),
            pltpu.VMEM((size_x // 128, ROWS * LAYERS, 128), F32),
            pltpu.VMEM((size_x // 128, LAYERS, 128), F32),
            pltpu.VMEM((size_x // 128, ROWS, 128), F32),
        ],
        compiler_params=params,
        name="gradient",
    )(place, received, even_h, even_t, odd_h, odd_t, provisional)
    return motion, thermal_out


def solution(mesh):
    split_y = P(None, "gy", "gz", None)
    split_flat = P("gy", "gz", None)
    return jax.shard_map(
        on_device,
        mesh=mesh,
        in_specs=(split_y, split_flat, split_y, split_flat),
        out_specs=(split_y, split_flat),
        check_vma=False,
    )
```

time: 281 us -> 92.4 us (0.33); the launches traced: 277 us -> 91.9 us
  matrix products: 92.8 us -> 0 us
  local copies, waits for them, and re-layouts: 51.9 us -> 5.74 us
  waiting for transfers between devices: 47.9 us -> 18.1 us
  starting transfers between devices: 41.9 us -> 17.2 us
  other arithmetic: 20.5 us -> 0.18 us
  blocking collectives: 20.1 us -> 36.9 us
  Pallas kernels: 0 us -> 12.9 us
    dot_general x6 -> x0, matrix products: 92.8 us -> none  [the longest x1 37 us: poisson(): jnp.einsum('yzx,xgj->gjyz', source, table_x, precision=highest)]
    all_to_all x3 -> x1, waiting for transfers between devices: 40.5 us -> 12.8 us  [exchanged(): return lax.all_to_all(pieces, axis, split_axis=0, concat_axis=0, tiled=True)]
    all_to_all x6 -> x0, local copies, waits for them, and re-layouts: 16.7 us -> none  [the longest x1 4.38 us: poisson(): lax.all_to_all(step_two, 'gz', split_axis=0, concat_axis=0, tiled=True)]
    all_to_all x1 -> x2, blocking collectives: 20.1 us -> 36.9 us  [exchanged(): return lax.all_to_all(pieces, axis, split_axis=0, concat_axis=0, tiled=True)]
    all_to_all x3 -> x1, starting transfers between devices: 25.3 us -> 8.93 us  [exchanged(): return lax.all_to_all(pieces, axis, split_axis=0, concat_axis=0, tiled=True)]
    reshape x4 -> x0, local copies, waits for them, and re-layouts: 14.6 us -> none  [the longest x2 7.97 us: poisson(): lax.all_to_all(step_three, 'gz', split_axis=0, concat_axis=0, tiled=True)]
    pallas_call x0 -> x4, Pallas kernels: none -> 12.9 us  [the longest x1 6.44 us: on_device(): pl.pallas_call(stencil_kernel, out_shape=(shape_of(3, ROWS, LAYERS, size_...]
    transpose x2 -> x0, local copies, waits for them, and re-layouts: 9.52 us -> none  [the longest x1 5.62 us: poisson(): jnp.einsum('sjyz,syhq->hjqz', step_one, table_y, precision=highest)]
  transfers between devices with their start and end apart: 11 -> 5, of which waited for: 9 -> 2; matrix products, arithmetic and copies ran while one was open for 2% -> 2% of each run, Pallas kernels for 0% -> 0%
where the time goes in v1:
time: 92.4 us; the launch traced here: 91.9 us
  blocking collectives  36.9 us (40%)
  waiting for transfers between devices  18.1 us (20%)
  starting transfers between devices  17.2 us (19%)
  Pallas kernels  12.9 us (14%)
  local copies, waits for them, and re-layouts  5.74 us (6%)
  between operations  0.94 us (1%)
    all_to_all x2, blocking collectives, exchanged(): return lax.all_to_all(pieces, axis, split_axis=0, concat_axis=0, tiled=True)  36.9 us
    all_to_all x1, waiting for transfers between devices, exchanged(): return lax.all_to_all(pieces, axis, split_axis=0, concat_axis=0, tiled=True)  12.8 us
    all_to_all x1, starting transfers between devices, exchanged(): return lax.all_to_all(pieces, axis, split_axis=0, concat_axis=0, tiled=True)  8.93 us
    ppermute x4, starting transfers between devices, shifted(): return lax.ppermute(value, axis, pairs)  8.28 us
    pallas_call x1, Pallas kernels, on_device(): pl.pallas_call(stencil_kernel, out_shape=(shape_of(3, ROWS, LAYERS, size_...  6.44 us
    ppermute x4, waiting for transfers between devices, shifted(): return lax.ppermute(value, axis, pairs)  5.23 us
    slice x4, local copies, waits for them, and re-layouts, cut(): return lax.index_in_dim(a, index, at, keepdims=False)  4.55 us
    pallas_call x1, Pallas kernels, on_device(): pl.pallas_call(gradient_kernel, out_shape=shape_of(3, ROWS, LAYERS, size_...  3.3 us
  transfers between devices with their start and end apart: 5, of which 2 were waited for; matrix products, arithmetic and copies ran while one was open for 2% of the time, Pallas kernels for 0%

profile of v1, /device:TPU:1, one launch (start us, length us, event | category | flops | bytes accessed | tf_op | source)
XLA Modules:
  0.0 91.9 jit_solution(4723757726892575358)
XLA Ops:
  0.6 0.0 copy-start.7
  0.6 1.1 %fusion.3 = (f32[8,1,1024]{2,1,0:T(1,128)S(1)}, f32[8,1,1024]{2,1,0:T(1,128)S(1)}) fusion(f32[8,16,1024]{2,1,0:T(8,128)} %thermal.1), kind=kLoop, calls=%fused_computation.18 | loop fusion | bytes 131072 | tf_op jit(solution)/shard_map/slice | solution.py:391
  1.8 1.0 %fusion.5 = (bf16[8,1,1024]{2,1,0:T(2,128)(2,1)S(1)}, bf16[8,1,1024]{2,1,0:T(2,128)(2,1)S(1)}) fusion(bf16[8,16,1024]{2,1,0:T(8,128)(2,1)} %base.1), kind=kLoop, calls=%fused_computation.20 | loop fusion | bytes 65536 | tf_op jit(solution)/shard_map/slice | solution.py:391
  2.8 1.5 %fusion.2 = (f32[3,8,1,1024]{3,2,1,0:T(1,128)S(1)}, f32[3,8,1,1024]{3,2,1,0:T(1,128)S(1)}) fusion(f32[3,8,16,1024]{3,2,1,0:T(8,128)} %motion.1), kind=kLoop, calls=%fused_computation.17 | loop fusion | bytes 393216 | tf_op jit(solution)/shard_map/slice | solution.py:391
  4.4 0.0 copy-start.6
  4.4 0.0 copy-start
  4.4 0.0 copy-start.1
  4.4 0.0 copy-start.2
  4.5 0.0 copy-start.3
  4.5 0.0 copy-start.5
  4.5 4.6 %collective-permute-start.2 = (f32[5,8,1024]{2,1,0:T(8,128)S(1)}, f32[5,8,1024]{2,1,0:T(8,128)S(1)}, u32[]{:S(2)}, u32[]{:S(2)}) collective-permute-start(f32[5,8,1024]{2,1,0:T(8,128)S(1)} %pad_maximum_fusion.2), channel_id=1, source_target_pairs={{0,1},{1,2},{2,3},{3,4},{4,5},{5,6},{6,7},{8,9},{9,10},{10,11},{11... | collective-permute-start | bytes 491528 | tf_op jit(solution)/shard_map/ppermute | solution.py:365
  9.1 0.9 fusion.4
  10.0 1.1 %slice_bitcast_fusion = (f32[3,16,1024]{2,1,0:T(8,128)S(1)}, f32[3,16,1024]{2,1,0:T(8,128)S(1)}) fusion(f32[3,8,16,1024]{3,2,1,0:T(8,128)} %motion.1), kind=kLoop, calls=%fused_computation.2 | loop fusion | bytes 786432 | tf_op jit(solution)/shard_map/squeeze | solution.py:391
  11.1 2.1 %collective-permute-start = (f32[5,16,1024]{2,1,0:T(8,128)S(1)}, f32[5,16,1024]{2,1,0:T(8,128)S(1)}, u32[]{:S(2)}, u32[]{:S(2)}) collective-permute-start(f32[5,16,1024]{2,1,0:T(8,128)S(1)} %pad_maximum_fusion), channel_id=1, source_target_pairs={{0,8},{8,16},{16,24},{24,32},{32,40},{40,48},{48,56},{56,64},{64,7... | collective-permute-start | bytes 983048 | tf_op jit(solution)/shard_map/ppermute | solution.py:365
  13.3 0.1 collective-permute-start.1
  13.5 0.0 copy-start.8
  13.5 0.0 copy-start.9
  13.5 0.0 copy-start.10
  13.5 0.0 copy-start.11
  13.5 1.4 %collective-permute-start.3 = (f32[5,8,1024]{2,1,0:T(8,128)S(1)}, f32[5,8,1024]{2,1,0:T(8,128)S(1)}, u32[]{:S(2)}, u32[]{:S(2)}) collective-permute-start(f32[5,8,1024]{2,1,0:T(8,128)S(1)} %pad_maximum_fusion.3), channel_id=1, source_target_pairs={{1,0},{2,1},{3,2},{4,3},{5,4},{6,5},{7,6},{9,8},{10,9},{11,10},{12... | collective-permute-start | bytes 491528 | tf_op jit(solution)/shard_map/ppermute | solution.py:365
  14.9 0.0 collective-permute-done.2.z_low
  15.0 5.2 %collective-permute-done.3.z_high = f32[5,8,1024]{2,1,0:T(8,128)S(1)} collective-permute-done((f32[5,8,1024]{2,1,0:T(8,128)S(1)}, f32[5,8,1024]{2,1,0:T(8,128)S(1)}, u32[]{:S(2)}, u32[]{:S(2)}) %collective-permute-start.3) | collective-permute-done | bytes 163872 | tf_op jit(solution)/shard_map/ppermute | solution.py:365
  20.2 0.0 collective-permute-done.y_low
  20.2 6.4 %stencil.1 = (f32[3,8,16,1024]{3,2,1,0:T(8,128)}, f32[8,16,1024]{2,1,0:T(8,128)}, f32[32,40,128]{2,1,0:T(8,128)}) custom-call(f32[3,8,16,1024]{3,2,1,0:T(8,128)} %motion.1, f32[8,16,1024]{2,1,0:T(8,128)S(1)} %copy-done.5, bf16[3,8,16,1024]{3,2,1,0:T(8,128)(2,1)S(1)} %copy-done.6, bf16[8,16,1024]{2,1,0:T(8,128)(2,1)S(1)} %copy-done.7, ...), custom_call_target="tpu_custom_call" | custom-call | tf_op jit(solution)/shard_map/stencil/pallas_call | solution.py:407
  26.7 8.9 %all-to-all-start = ((f32[32,40,128]{2,1,0:T(8,128)}), f32[32,40,128]{2,1,0:T(8,128)S(1)}, u32[]{:S(2)}, u32[]{:S(2)}) async-start(f32[32,40,128]{2,1,0:T(8,128)} %get-tuple-element.7), calls=%async_computation | async-start | bytes 1310720 | tf_op jit(solution)/shard_map/all_to_all | solution.py:369
  35.6 0.1 pad_add_fusion.place
  35.7 12.8 %all-to-all-done.received = f32[32,40,128]{2,1,0:T(8,128)S(1)} async-done(((f32[32,40,128]{2,1,0:T(8,128)}), f32[32,40,128]{2,1,0:T(8,128)S(1)}, u32[]{:S(2)}, u32[]{:S(2)}) %all-to-all-start) | async-done | bytes 655392 | tf_op jit(solution)/shard_map/all_to_all | solution.py:369
  48.6 1.5 %down.1 = (f32[17,64,128]{2,1,0:T(8,128)S(1)}, f32[8,64,128]{2,1,0:T(8,128)S(1)}) custom-call(s32[2]{0:T(128)S(1)} %pad_add_fusion.place, f32[32,40,128]{2,1,0:T(8,128)S(1)} %all-to-all-done.received, bf16[256,256]{1,0:T(8,128)(2,1)S(1)} %copy-done.9, bf16[256,256]{1,0:T(8,128)(2,1)S(1)} %copy-done.8, f32[32,128]{1,0:T(8,128)S(1)} %copy-done.11, ...), custom_call_target="tpu_custom_call" | custom-call | tf_op jit(solution)/shard_map/down/pallas_call | solution.py:429
  50.0 18.3 %all_to_all.15.handed = f32[8,64,128]{2,1,0:T(8,128)S(1)} all-to-all(f32[8,64,128]{2,1,0:T(8,128)S(1)} %get-tuple-element.9), channel_id=1, replica_groups=mesh['gy'=32,'gz'=8] {'gz'}, dimensions={0} | all-to-all | bytes 524288 | tf_op jit(solution)/shard_map/all_to_all | solution.py:369
  68.3 1.7 %up.1 = f32[32,40,128]{2,1,0:T(8,128)S(1)} custom-call(s32[2]{0:T(128)S(1)} %pad_add_fusion.place, f32[17,64,128]{2,1,0:T(8,128)S(1)} %get-tuple-element.8.spectral, f32[8,64,128]{2,1,0:T(8,128)S(1)} %all_to_all.15.handed, bf16[256,256]{1,0:T(8,128)(2,1)S(1)} %copy-done.9, bf16[256,256]{1,0:T(8,128)(2,1)S(1)} %copy-done.8, f32[32,128]{1,0:T(8,128)S(1)} %copy-done.11, ...), custom_call_target="tpu_custom_call" | custom-call | tf_op jit(solution)/shard_map/up/pallas_call | solution.py:438
  70.1 18.5 %all_to_all.16.received = f32[32,40,128]{2,1,0:T(8,128)S(1)} all-to-all(f32[32,40,128]{2,1,0:T(8,128)S(1)} %up.1), channel_id=1, replica_groups=mesh['gy'=32,'gz'=8] {'gy'}, dimensions={0} | all-to-all | bytes 1310720 | tf_op jit(solution)/shard_map/all_to_all | solution.py:369
  88.6 3.3 %gradient.1 = f32[3,8,16,1024]{3,2,1,0:T(8,128)} custom-call(s32[2]{0:T(128)S(1)} %pad_add_fusion.place, f32[32,40,128]{2,1,0:T(8,128)S(1)} %all_to_all.16.received, bf16[512,512]{1,0:T(8,128)(2,1)S(1)} %copy-done.3, bf16[512,512]{1,0:T(8,128)(2,1)S(1)} %copy-done.2, bf16[512,512]{1,0:T(8,128)(2,1)S(1)} %copy-done.1, bf16[512,512]{1,0:T(8,128)(2,1)S(1)} %copy-done, ...), custom_call_target="tpu_custom_call" | custom-call | tf_op jit(solution)/shard_map/gradient/pallas_call | solution.py:447
  (25 shorter events, 0.2 us)
Async XLA Ops:
  0.6 9.4 %copy-start.7 = (bf16[8,16,1024]{2,1,0:T(8,128)(2,1)S(1)}, bf16[8,16,1024]{2,1,0:T(8,128)(2,1)}, u32[]{:S(2)}) copy-start(bf16[8,16,1024]{2,1,0:T(8,128)(2,1)} %base.1) | copy-start | bytes 786436
  4.4 15.8 %copy-start.6 = (bf16[3,8,16,1024]{3,2,1,0:T(8,128)(2,1)S(1)}, bf16[3,8,16,1024]{3,2,1,0:T(8,128)(2,1)}, u32[]{:S(2)}) copy-start(bf16[3,8,16,1024]{3,2,1,0:T(8,128)(2,1)} %flow.1) | copy-start | bytes 2359300
  4.4 15.8 %copy-start = (bf16[512,512]{1,0:T(8,128)(2,1)S(1)}, bf16[512,512]{1,0:T(8,128)(2,1)}, u32[]{:S(2)}) copy-start(bf16[512,512]{1,0:T(8,128)(2,1)} %constant.28.clone.odd_t) | copy-start | bytes 1572868
  4.4 15.8 %copy-start.1 = (bf16[512,512]{1,0:T(8,128)(2,1)S(1)}, bf16[512,512]{1,0:T(8,128)(2,1)}, u32[]{:S(2)}) copy-start(bf16[512,512]{1,0:T(8,128)(2,1)} %constant.27.clone.odd_h) | copy-start | bytes 1572868
  4.4 15.8 %copy-start.2 = (bf16[512,512]{1,0:T(8,128)(2,1)S(1)}, bf16[512,512]{1,0:T(8,128)(2,1)}, u32[]{:S(2)}) copy-start(bf16[512,512]{1,0:T(8,128)(2,1)} %constant.26.clone.even_t) | copy-start | bytes 1572868
  4.5 15.8 %copy-start.3 = (bf16[512,512]{1,0:T(8,128)(2,1)S(1)}, bf16[512,512]{1,0:T(8,128)(2,1)}, u32[]{:S(2)}) copy-start(bf16[512,512]{1,0:T(8,128)(2,1)} %constant.25.clone.even_h) | copy-start | bytes 1572868
  4.5 15.8 %copy-start.5 = (f32[8,16,1024]{2,1,0:T(8,128)S(1)}, f32[8,16,1024]{2,1,0:T(8,128)}, u32[]{:S(2)}) copy-start(f32[8,16,1024]{2,1,0:T(8,128)} %thermal.1) | copy-start | bytes 1572868
  4.5 10.5 %collective-permute-start.2 = (f32[5,8,1024]{2,1,0:T(8,128)S(1)}, f32[5,8,1024]{2,1,0:T(8,128)S(1)}, u32[]{:S(2)}, u32[]{:S(2)}) collective-permute-start(f32[5,8,1024]{2,1,0:T(8,128)S(1)} %pad_maximum_fusion.2), channel_id=1, source_target_pairs={{0,1},{1,2},{2,3},{3,4},{4,5},{5,6},{6,7},{8,9},{9,10},{10,11},{11... | collective-permute-start | bytes 491528 | tf_op jit(solution)/shard_map/ppermute | solution.py:365
  11.1 9.0 %collective-permute-start = (f32[5,16,1024]{2,1,0:T(8,128)S(1)}, f32[5,16,1024]{2,1,0:T(8,128)S(1)}, u32[]{:S(2)}, u32[]{:S(2)}) collective-permute-start(f32[5,16,1024]{2,1,0:T(8,128)S(1)} %pad_maximum_fusion), channel_id=1, source_target_pairs={{0,8},{8,16},{16,24},{24,32},{32,40},{40,48},{48,56},{56,64},{64,7... | collective-permute-start | bytes 983048 | tf_op jit(solution)/shard_map/ppermute | solution.py:365
  13.3 6.9 %collective-permute-start.1 = (f32[5,16,1024]{2,1,0:T(8,128)S(1)}, f32[5,16,1024]{2,1,0:T(8,128)S(1)}, u32[]{:S(2)}, u32[]{:S(2)}) collective-permute-start(f32[5,16,1024]{2,1,0:T(8,128)S(1)} %pad_maximum_fusion.1), channel_id=1, source_target_pairs={{0,248},{8,0},{16,8},{24,16},{32,24},{40,32},{48,40},{56,48},{64,5... | collective-permute-start | bytes 983048 | tf_op jit(solution)/shard_map/ppermute | solution.py:365
  13.5 35.1 %copy-start.8 = (bf16[256,256]{1,0:T(8,128)(2,1)S(1)}, bf16[256,256]{1,0:T(8,128)(2,1)}, u32[]{:S(2)}) copy-start(bf16[256,256]{1,0:T(8,128)(2,1)} %constant.30.clone.span_t) | copy-start | bytes 393220
  13.5 35.1 %copy-start.9 = (bf16[256,256]{1,0:T(8,128)(2,1)S(1)}, bf16[256,256]{1,0:T(8,128)(2,1)}, u32[]{:S(2)}) copy-start(bf16[256,256]{1,0:T(8,128)(2,1)} %constant.29.clone.span_h) | copy-start | bytes 393220
  13.5 35.1 %copy-start.10 = (f32[64,128]{1,0:T(8,128)S(1)}, f32[64,128]{1,0:T(8,128)}, u32[]{:S(2)}) copy-start(f32[64,128]{1,0:T(8,128)} %constant.32.clone.line_y) | copy-start | bytes 98308
  13.5 35.0 %copy-start.11 = (f32[32,128]{1,0:T(8,128)S(1)}, f32[32,128]{1,0:T(8,128)}, u32[]{:S(2)}) copy-start(f32[32,128]{1,0:T(8,128)} %constant.31.clone.line_x) | copy-start | bytes 49156
  13.5 6.7 %collective-permute-start.3 = (f32[5,8,1024]{2,1,0:T(8,128)S(1)}, f32[5,8,1024]{2,1,0:T(8,128)S(1)}, u32[]{:S(2)}, u32[]{:S(2)}) collective-permute-start(f32[5,8,1024]{2,1,0:T(8,128)S(1)} %pad_maximum_fusion.3), channel_id=1, source_target_pairs={{1,0},{2,1},{3,2},{4,3},{5,4},{6,5},{7,6},{9,8},{10,9},{11,10},{12... | collective-permute-start | bytes 491528 | tf_op jit(solution)/shard_map/ppermute | solution.py:365
  26.7 21.8 %all-to-all-start = ((f32[32,40,128]{2,1,0:T(8,128)}), f32[32,40,128]{2,1,0:T(8,128)S(1)}, u32[]{:S(2)}, u32[]{:S(2)}) async-start(f32[32,40,128]{2,1,0:T(8,128)} %get-tuple-element.7), calls=%async_computation | async-start | bytes 1310720 | tf_op jit(solution)/shard_map/all_to_all | solution.py:369
  68.3 20.3 %copy-start.4 = (f32[3,8,16,1024]{3,2,1,0:T(8,128)S(1)}, f32[3,8,16,1024]{3,2,1,0:T(8,128)}, u32[]{:S(2)}) copy-start(f32[3,8,16,1024]{3,2,1,0:T(8,128)} %get-tuple-element.10.provisional) | copy-start | bytes 4718596

commit v2 on v1

--- a/solution.py
+++ b/solution.py
@@ -95,10 +95,22 @@
     return jnp.concatenate([ref[b, pl.ds(start, count), :] for b in range(ref.shape[0])], 1)
 
 
-def stencil_kernel(
-    motion, thermal, flow, base, y_low, y_high, z_low, z_high, even_h, even_t, odd_h, odd_t,
-    provisional, thermal_out, message, source, lines, row_p, layer_p,
-):
+def sides_kernel(motion, thermal, base, y_first, y_last, z_first, z_last):
+    for out, y in ((y_first, 0), (y_last, ROWS - 1)):
+        for c in range(3):
+            out[c] = motion[c, y]
+        out[3] = thermal[y]
+        out[4] = base[y].astype(F32)
+    for y in range(ROWS):
+        warm = base[y].astype(F32)
+        for out, z in ((z_first, 0), (z_last, LAYERS - 1)):
+            for c in range(3):
+                out[c, y:y + 1, :] = motion[c, y, z:z + 1, :]
+            out[3, y:y + 1, :] = thermal[y, z:z + 1, :]
+            out[4, y:y + 1, :] = warm[z:z + 1, :]
+
+
+def inner_kernel(motion, thermal, flow, base, moved, warmed):
     size_x = motion.shape[-1]
     row = lax.broadcasted_iota(jnp.int32, (LAYERS, size_x), 0)
     top = row == LAYERS - 1
@@ -113,36 +125,85 @@
 
     def neighbours(c, y):
         centre = field(c, y)
-        y_plus = field(c, y + 1) if y < ROWS - 1 else y_high[c]
-        y_minus = field(c, y - 1) if y > 0 else y_low[c]
-        z_plus = jnp.where(top, z_high[c, y:y + 1, :], pltpu.roll(centre, LAYERS - 1, 0))
-        z_minus = jnp.where(bottom, z_low[c, y:y + 1, :], pltpu.roll(centre, 1, 0))
+        y_plus = field(c, y + 1) if y < ROWS - 1 else None
+        y_minus = field(c, y - 1) if y > 0 else None
+        z_plus = jnp.where(top, 0.0, pltpu.roll(centre, LAYERS - 1, 0))
+        z_minus = jnp.where(bottom, 0.0, pltpu.roll(centre, 1, 0))
         x_plus = pltpu.roll(centre, size_x - 1, 1)
         x_minus = pltpu.roll(centre, 1, 1)
         return centre, x_plus, x_minus, y_plus, y_minus, z_plus, z_minus
 
-    carried = None
     for y in range(ROWS):
         weights = []
         for c in range(3):
             speed = flow[c, y].astype(F32) * 0.1
             weights += [0.02 + speed, 0.02 - speed]
         _, hx, gx, hy, gy, hz, gz = neighbours(4, y)
-        slopes = (hx - gx, hy - gy, hz - gz)
+        slope_y = -gy if hy is None else hy if gy is None else hy - gy
+        slopes = (hx - gx, slope_y, hz - gz)
         heat = thermal[y] * 0.1
-        moved = []
         for c in range(4):
             parts = neighbours(c, y)
             value = parts[0] * 0.88
             for weight, part in zip(weights, parts[1:]):
-                value = value + weight * part
+                if part is not None:
+                    value = value + weight * part
             if c < 3:
-                value = value + heat * slopes[c]
-                provisional[c, y] = value
+                moved[c, y] = value + heat * slopes[c]
             else:
-                thermal_out[y] = value + 0.2 * motion[2, y]
-            moved.append(value)
-        p0, p1, p2 = moved[:3]
+                warmed[y] = value + 0.2 * motion[2, y]
+
+
+def edge_weights(flow, y):
+    size_x = flow.shape[-1]
+    row = lax.broadcasted_iota(jnp.int32, (8, size_x), 0)
+    speed = flow[2, y].astype(F32) * 0.1
+    first = jnp.where(row == 0, 0.02 - speed[:8], 0.0)
+    last = jnp.where(row == 7, 0.02 + speed[LAYERS - 8:], 0.0)
+    return row, first, last
+
+
+def warm_kernel(warmed, flow, y_low, y_high, z_low, z_high, thermal_out):
+    for y in range(ROWS):
+        value = warmed[y]
+        if y == 0:
+            value = value + (0.02 - flow[1, y].astype(F32) * 0.1) * y_low[3]
+        if y == ROWS - 1:
+            value = value + (0.02 + flow[1, y].astype(F32) * 0.1) * y_high[3]
+        _, first, last = edge_weights(flow, y)
+        thermal_out[y, :8] = value[:8] + first * z_low[3, y:y + 1, :]
+        thermal_out[y, 8:] = value[8:] + last * z_high[3, y:y + 1, :]
+
+
+def source_kernel(
+    moved, thermal, flow, y_low, y_high, z_low, z_high, even_h, even_t, odd_h, odd_t,
+    provisional, message, source, lines, row_p, layer_p,
+):
+    size_x = moved.shape[-1]
+    top = lax.broadcasted_iota(jnp.int32, (LAYERS, size_x), 0) == LAYERS - 1
+    carried = None
+    for y in range(ROWS):
+        row, first, last = edge_weights(flow, y)
+        fields = []
+        for c in range(3):
+            value = moved[c, y]
+            if y == 0:
+                value = value + (0.02 - flow[1, y].astype(F32) * 0.1) * y_low[c]
+                if c == 1:
+                    value = value - thermal[y] * 0.1 * y_low[4]
+            if y == ROWS - 1:
+                value = value + (0.02 + flow[1, y].astype(F32) * 0.1) * y_high[c]
+                if c == 1:
+                    value = value + thermal[y] * 0.1 * y_high[4]
+            low = value[:8] + first * z_low[c, y:y + 1, :]
+            high = value[8:] + last * z_high[c, y:y + 1, :]
+            if c == 2:
+                low = low - jnp.where(row == 0, thermal[y, :8] * 0.1, 0.0) * z_low[4, y:y + 1, :]
+                high = high + jnp.where(row == 7, thermal[y, 8:] * 0.1, 0.0) * z_high[4, y:y + 1, :]
+            value = jnp.concatenate([low, high], 0)
+            provisional[c, y] = value
+            fields.append(value)
+        p0, p1, p2 = fields
         if y == 0:
             keep(row_p, 0, p1)
         else:
@@ -384,54 +445,63 @@
     line_x, line_y = jnp.asarray(line_x), jnp.asarray(line_y)
     modes = line_y.shape[0]
     place = jnp.stack([lax.axis_index("gy"), lax.axis_index("gz")]).astype(jnp.int32)
-    params = pltpu.CompilerParams(vmem_limit_bytes=48 << 20)
-
-    def side(index, dim):
-        def cut(a, at):
-            return lax.index_in_dim(a, index, at, keepdims=False)
-
-        return jnp.concatenate(
-            [
-                cut(dual_motion, dim + 1),
-                cut(dual_thermal, dim)[None],
-                cut(base, dim)[None].astype(F32),
-            ],
-            0,
-        )
-
-    y_low = shifted(side(ROWS - 1, 0), "gy", 1, True)
-    y_high = shifted(side(0, 0), "gy", -1, True)
-    z_low = shifted(side(LAYERS - 1, 1), "gz", 1, False)
-    z_high = shifted(side(0, 1), "gz", -1, False)
-
-    provisional, thermal_out, message = pl.pallas_call(
-        stencil_kernel,
-        out_shape=(
-            shape_of(3, ROWS, LAYERS, size_x),
-            shape_of(ROWS, LAYERS, size_x),
-            shape_of(groups_y, PIECE, 128),
-        ),
-        in_specs=[VMEM] * 12,
-        out_specs=(VMEM,) * 3,
+
+    def params(mib):
+        return pltpu.CompilerParams(vmem_limit_bytes=mib << 20)
+
+    rows = shape_of(5, LAYERS, size_x)
+    layers = shape_of(5, ROWS, size_x)
+    y_first, y_last, z_first, z_last = pl.pallas_call(
+        sides_kernel,
+        out_shape=(rows, rows, layers, layers),
+        in_specs=[VMEM] * 3,
+        out_specs=(VMEM,) * 4,
+        compiler_params=params(8),
+        name="sides",
+    )(dual_motion, dual_thermal, base)
+    z_low = shifted(z_last, "gz", 1, False)
+    z_high = shifted(z_first, "gz", -1, False)
+    y_low = shifted(y_last, "gy", 1, True)
+    y_high = shifted(y_first, "gy", -1, True)
+    moved, warmed = pl.pallas_call(
+        inner_kernel,
+        out_shape=(shape_of(3, ROWS, LAYERS, size_x), shape_of(ROWS, LAYERS, size_x)),
+        in_specs=[VMEM] * 4,
+        out_specs=(VMEM,) * 2,
+        compiler_params=params(16),
+        cost_estimate=pl.CostEstimate(flops=80 * ROWS * LAYERS * size_x, transcendentals=0, bytes_accessed=10 << 20),
+        name="inner",
+    )(dual_motion, dual_thermal, flow, base)
+    provisional, message = pl.pallas_call(
+        source_kernel,
+        out_shape=(shape_of(3, ROWS, LAYERS, size_x), shape_of(groups_y, PIECE, 128)),
+        in_specs=[VMEM] * 11,
+        out_specs=(VMEM,) * 2,
         scratch_shapes=[
             pltpu.VMEM((size_x // 128, ROWS * LAYERS, 128), F32),
             pltpu.VMEM((4 * PIECE, size_x), F32),
             pltpu.VMEM((size_x // 128, LAYERS, 128), F32),
             pltpu.VMEM((size_x // 128, ROWS, 128), F32),
         ],
-        compiler_params=params,
-        name="stencil",
-    )(
-        dual_motion, dual_thermal, flow, base, y_low, y_high, z_low, z_high,
-        even_h, even_t, odd_h, odd_t,
-    )
+        compiler_params=params(24),
+        name="source",
+    )(moved, dual_thermal, flow, y_low, y_high, z_low, z_high, even_h, even_t, odd_h, odd_t)
+    thermal_out = pl.pallas_call(
+        warm_kernel,
+        out_shape=shape_of(ROWS, LAYERS, size_x),
+        in_specs=[VMEM] * 6,
+        out_specs=VMEM,
+        compiler_params=params(8),
+        cost_estimate=pl.CostEstimate(flops=10 * ROWS * LAYERS * size_x, transcendentals=0, bytes_accessed=3 << 20),
+        name="warm",
+    )(warmed, flow, y_low, y_high, z_low, z_high)
     received = exchanged(message, "gy")
     spectral, handed = pl.pallas_call(
         down_kernel,
         out_shape=(shape_of(LAYERS + 1, modes, 128), shape_of(groups_z, modes, 128)),
         in_specs=[SMEM] + [VMEM] * 5,
         out_specs=(VMEM,) * 2,
-        compiler_params=params,
+        compiler_params=params(16),
         name="down",
     )(place, received, span_h, span_t, line_x, line_y)
     handed = exchanged(handed, "gz")
@@ -440,7 +510,7 @@
         out_shape=shape_of(groups_y, PIECE, 128),
         in_specs=[SMEM] + [VMEM] * 6,
         out_specs=VMEM,
-        compiler_params=params,
+        compiler_params=params(16),
         name="up",
     )(place, spectral, handed, span_h, span_t, line_x, line_y)
     received = exchanged(message, "gy")
@@ -455,7 +525,7 @@
             pltpu.VMEM((size_x // 128, LAYERS, 128), F32),
             pltpu.VMEM((size_x // 128, ROWS, 128), F32),
         ],
-        compiler_params=params,
+        compiler_params=params(24),
         name="gradient",
     )(place, received, even_h, even_t, odd_h, odd_t, provisional)
     return motion, thermal_out

time: 92.4 us -> 93.7 us (1.014)
  blocking collectives: 36.9 us -> 19.6 us
  local copies, waits for them, and re-layouts: 5.74 us -> 17.6 us
  starting transfers between devices: 17.2 us -> 22.3 us
  waiting for transfers between devices: 18.1 us -> 19.5 us
    unnamed x28 -> x64, local copies, waits for them, and re-layouts: 0.13 us -> 17.6 us
    all_to_all x2 -> x1, blocking collectives: 36.9 us -> 19.6 us  [exchanged(): return lax.all_to_all(pieces, axis, split_axis=0, concat_axis=0, tiled=True)]
    all_to_all x1 -> x2, waiting for transfers between devices: 12.8 us -> 19.5 us  [exchanged(): return lax.all_to_all(pieces, axis, split_axis=0, concat_axis=0, tiled=True)]
    all_to_all x1 -> x2, starting transfers between devices: 8.93 us -> 14.8 us  [exchanged(): return lax.all_to_all(pieces, axis, split_axis=0, concat_axis=0, tiled=True)]
    ppermute x4, waiting for transfers between devices: 5.23 us -> 0.01 us  [shifted(): return lax.ppermute(value, axis, pairs)]
    slice x4 -> x0, local copies, waits for them, and re-layouts: 4.55 us -> none  [cut(): return lax.index_in_dim(a, index, at, keepdims=False)]
    pallas_call x1 -> x4, Pallas kernels: 6.44 us -> 5.17 us  [the longest x1 2.36 us: on_device(): pl.pallas_call(inner_kernel, out_shape=(shape_of(3, ROWS, LAYERS, size_x)...]
    squeeze x1 -> x0, local copies, waits for them, and re-layouts: 1.05 us -> none  [cut(): return lax.index_in_dim(a, index, at, keepdims=False)]
  transfers between devices with their start and end apart: 5 -> 6, of which waited for: 2 -> 2; matrix products, arithmetic and copies ran while one was open for 2% -> 1% of each run, Pallas kernels for 0% -> 4%
where the time goes in v2:
time: 93.7 us; the launch traced here: 92.9 us
  starting transfers between devices  22.3 us (24%)
  blocking collectives  19.6 us (21%)
  waiting for transfers between devices  19.5 us (21%)
  local copies, waits for them, and re-layouts  17.6 us (19%)
  Pallas kernels  12.4 us (13%)
    all_to_all x1, blocking collectives, exchanged(): return lax.all_to_all(pieces, axis, split_axis=0, concat_axis=0, tiled=True)  19.6 us
    all_to_all x2, waiting for transfers between devices, exchanged(): return lax.all_to_all(pieces, axis, split_axis=0, concat_axis=0, tiled=True)  19.5 us
    unnamed x64, local copies, waits for them, and re-layouts  17.6 us
    all_to_all x2, starting transfers between devices, exchanged(): return lax.all_to_all(pieces, axis, split_axis=0, concat_axis=0, tiled=True)  14.8 us
    ppermute x4, starting transfers between devices, shifted(): return lax.ppermute(value, axis, pairs)  7.51 us
    pallas_call x1, Pallas kernels, on_device(): pl.pallas_call(gradient_kernel, out_shape=shape_of(3, ROWS, LAYERS, size_...  3.25 us
    pallas_call x1, Pallas kernels, on_device(): pl.pallas_call(up_kernel, out_shape=shape_of(groups_y, PIECE, 128), in_sp...  2.55 us
    pallas_call x1, Pallas kernels, on_device(): pl.pallas_call(inner_kernel, out_shape=(shape_of(3, ROWS, LAYERS, size_x)...  2.36 us
  transfers between devices with their start and end apart: 6, of which 2 were waited for; matrix products, arithmetic and copies ran while one was open for 1% of the time, Pallas kernels for 4%

profile of v2, /device:TPU:1, one launch (start us, length us, event | category | flops | bytes accessed | tf_op | source)
XLA Modules:
  0.0 92.9 jit_solution(5091514213157403886)
XLA Ops:
  0.6 1.4 %copy-done.1 = f32[3,8,16,1024]{3,2,1,0:T(8,128)S(1)} copy-done((f32[3,8,16,1024]{3,2,1,0:T(8,128)S(1)}, f32[3,8,16,1024]{3,2,1,0:T(8,128)}, u32[]{:S(2)}) %copy-start.1) | copy-done | bytes 1572888
  2.0 1.0 %copy-done.3 = f32[8,16,1024]{2,1,0:T(8,128)S(1)} copy-done((f32[8,16,1024]{2,1,0:T(8,128)S(1)}, f32[8,16,1024]{2,1,0:T(8,128)}, u32[]{:S(2)}) %copy-start.3) | copy-done | bytes 524312
  3.1 0.9 %copy-done.16 = bf16[8,16,1024]{2,1,0:T(8,128)(2,1)S(1)} copy-done((bf16[8,16,1024]{2,1,0:T(8,128)(2,1)S(1)}, bf16[8,16,1024]{2,1,0:T(8,128)(2,1)}, u32[]{:S(2)}) %copy-start.16) | copy-done | bytes 262168
  4.2 2.7 %collective-permute-start = (f32[5,16,1024]{2,1,0:T(8,128)S(1)}, f32[5,16,1024]{2,1,0:T(8,128)S(1)}, u32[]{:S(2)}, u32[]{:S(2)}) collective-permute-start(f32[5,16,1024]{2,1,0:T(8,128)S(1)} %get-tuple-element.13), channel_id=1, source_target_pairs={{0,8},{8,16},{16,24},{24,32},{32,40},{40,48},{48,56},{56,64},{64,7... | collective-permute-start | bytes 983048 | tf_op jit(solution)/shard_map/ppermute | solution.py:426
  6.8 0.7 collective-permute-start.1
  7.6 2.8 %collective-permute-start.2 = (f32[5,8,1024]{2,1,0:T(8,128)S(1)}, f32[5,8,1024]{2,1,0:T(8,128)S(1)}, u32[]{:S(2)}, u32[]{:S(2)}) collective-permute-start(f32[5,8,1024]{2,1,0:T(8,128)S(1)} %get-tuple-element.15), channel_id=1, source_target_pairs={{0,1},{1,2},{2,3},{3,4},{4,5},{5,6},{6,7},{8,9},{9,10},{10,11},{11... | collective-permute-start | bytes 491528 | tf_op jit(solution)/shard_map/ppermute | solution.py:426
  10.4 1.3 %collective-permute-start.3 = (f32[5,8,1024]{2,1,0:T(8,128)S(1)}, f32[5,8,1024]{2,1,0:T(8,128)S(1)}, u32[]{:S(2)}, u32[]{:S(2)}) collective-permute-start(f32[5,8,1024]{2,1,0:T(8,128)S(1)} %get-tuple-element.16), channel_id=1, source_target_pairs={{1,0},{2,1},{3,2},{4,3},{5,4},{6,5},{7,6},{9,8},{10,9},{11,10},{12... | collective-permute-start | bytes 491528 | tf_op jit(solution)/shard_map/ppermute | solution.py:426
  11.7 1.0 %copy-done.4 = f32[8,16,1024]{2,1,0:T(8,128)S(1)} copy-done((f32[8,16,1024]{2,1,0:T(8,128)S(1)}, f32[8,16,1024]{2,1,0:T(8,128)}, u32[]{:S(2)}) %copy-start.4) | copy-done | bytes 524312
  12.8 0.9 %copy-done.17 = bf16[8,16,1024]{2,1,0:T(8,128)(2,1)S(1)} copy-done((bf16[8,16,1024]{2,1,0:T(8,128)(2,1)S(1)}, bf16[8,16,1024]{2,1,0:T(8,128)(2,1)}, u32[]{:S(2)}) %copy-start.17) | copy-done | bytes 262168
  13.7 2.4 %inner.1 = (f32[3,8,16,1024]{3,2,1,0:T(8,128)S(1)}, f32[8,16,1024]{2,1,0:T(8,128)S(1)}) custom-call(f32[3,8,16,1024]{3,2,1,0:T(8,128)S(1)} %copy-done.2, f32[8,16,1024]{2,1,0:T(8,128)S(1)} %copy-done.4, bf16[3,8,16,1024]{3,2,1,0:T(8,128)(2,1)S(1)} %copy-done, bf16[8,16,1024]{2,1,0:T(8,128)(2,1)S(1)} %copy-done.17), custom_call_target="tpu_custom_call" | custom-call | flops 10485760 | bytes 10485760 | tf_op jit(solution)/shard_map/inner/pallas_call | solution.py:466
  16.1 0.8 copy-done.23
  17.0 1.7 %source.1 = (f32[3,8,16,1024]{3,2,1,0:T(8,128)S(1)}, f32[32,40,128]{2,1,0:T(8,128)S(1)}) custom-call(f32[3,8,16,1024]{3,2,1,0:T(8,128)S(1)} %get-tuple-element.12.moved, f32[8,16,1024]{2,1,0:T(8,128)S(1)} %copy-done.5, bf16[3,8,16,1024]{3,2,1,0:T(8,128)(2,1)S(1)} %copy-done, f32[5,16,1024]{2,1,0:T(8,128)S(1)} %collective-permute-done.y_low, ...), custom_call_target="tpu_custom_call" | custom-call | tf_op jit(solution)/shard_map/source/pallas_call | solution.py:475
  18.8 1.1 %copy-done.10 = f32[3,8,16,1024]{3,2,1,0:T(8,128)} copy-done((f32[3,8,16,1024]{3,2,1,0:T(8,128)}, f32[3,8,16,1024]{3,2,1,0:T(8,128)S(1)}, u32[]{:S(2)}) %copy-start.10) | copy-done | bytes 1572888
  20.0 0.8 copy-done.22
  20.8 8.9 %all-to-all-start = ((f32[32,40,128]{2,1,0:T(8,128)}), f32[32,40,128]{2,1,0:T(8,128)S(1)}, u32[]{:S(2)}, u32[]{:S(2)}) async-start(f32[32,40,128]{2,1,0:T(8,128)} %copy-done.22), calls=%async_computation | async-start | bytes 1310720 | tf_op jit(solution)/shard_map/all_to_all | solution.py:430
  30.3 12.3 %all-to-all-done.received = f32[32,40,128]{2,1,0:T(8,128)S(1)} async-done(((f32[32,40,128]{2,1,0:T(8,128)}), f32[32,40,128]{2,1,0:T(8,128)S(1)}, u32[]{:S(2)}, u32[]{:S(2)}) %all-to-all-start) | async-done | bytes 655392 | tf_op jit(solution)/shard_map/all_to_all | solution.py:430
  42.7 0.9 copy-done.25
  43.6 0.9 copy-done.27
  44.5 0.8 copy-done.28
  45.8 1.5 %down.1 = (f32[17,64,128]{2,1,0:T(8,128)S(1)}, f32[8,64,128]{2,1,0:T(8,128)S(1)}) custom-call(s32[2]{0:T(128)S(1)} %copy-done.30, f32[32,40,128]{2,1,0:T(8,128)S(1)} %all-to-all-done.received, bf16[256,256]{1,0:T(8,128)(2,1)S(1)} %copy-done.27, bf16[256,256]{1,0:T(8,128)(2,1)S(1)} %copy-done.25, f32[32,128]{1,0:T(8,128)S(1)} %copy-done.29, ...), custom_call_target="tpu_custom_call" | custom-call | tf_op jit(solution)/shard_map/down/pallas_call | solution.py:499
  47.3 19.6 %all_to_all.15.handed = f32[8,64,128]{2,1,0:T(8,128)S(1)} all-to-all(f32[8,64,128]{2,1,0:T(8,128)S(1)} %get-tuple-element.19), channel_id=1, replica_groups=mesh['gy'=32,'gz'=8] {'gz'}, dimensions={0} | all-to-all | bytes 524288 | tf_op jit(solution)/shard_map/all_to_all | solution.py:430
  66.9 2.5 %up.1 = f32[32,40,128]{2,1,0:T(8,128)} custom-call(s32[2]{0:T(128)S(1)} %copy-done.30, f32[17,64,128]{2,1,0:T(8,128)S(1)} %get-tuple-element.18.spectral, f32[8,64,128]{2,1,0:T(8,128)S(1)} %all_to_all.15.handed, bf16[256,256]{1,0:T(8,128)(2,1)S(1)} %copy-done.27, bf16[256,256]{1,0:T(8,128)(2,1)S(1)} %copy-done.26, f32[32,128]{1,0:T(8,128)S(1)} %copy-done.29, ...), custom_call_target="tpu_custom_call" | custom-call | tf_op jit(solution)/shard_map/up/pallas_call | solution.py:508
  69.4 5.9 %all-to-all-start.2 = ((f32[32,40,128]{2,1,0:T(8,128)}), f32[32,40,128]{2,1,0:T(8,128)S(1)}, u32[]{:S(2)}, u32[]{:S(2)}) async-start(f32[32,40,128]{2,1,0:T(8,128)} %up.1), calls=%async_computation.2 | async-start | bytes 1310720 | tf_op jit(solution)/shard_map/all_to_all | solution.py:430
  75.3 1.0 %copy-done.13 = f32[5,16,1024]{2,1,0:T(8,128)S(1)} copy-done((f32[5,16,1024]{2,1,0:T(8,128)S(1)}, f32[5,16,1024]{2,1,0:T(8,128)}, u32[]{:S(2)}) %copy-start.13) | copy-done | bytes 327704
  76.3 1.0 %copy-done.15 = f32[5,16,1024]{2,1,0:T(8,128)S(1)} copy-done((f32[5,16,1024]{2,1,0:T(8,128)S(1)}, f32[5,16,1024]{2,1,0:T(8,128)}, u32[]{:S(2)}) %copy-start.15) | copy-done | bytes 327704
  77.3 0.9 copy-done.19
  78.2 0.9 copy-done.21
  79.1 1.0 %copy-done.24 = f32[8,16,1024]{2,1,0:T(8,128)S(1)} copy-done((f32[8,16,1024]{2,1,0:T(8,128)S(1)}, f32[8,16,1024]{2,1,0:T(8,128)}, u32[]{:S(2)}) %copy-start.24) | copy-done | bytes 524312
  80.2 0.9 %warm.1 = f32[8,16,1024]{2,1,0:T(8,128)} custom-call(f32[8,16,1024]{2,1,0:T(8,128)S(1)} %copy-done.24, bf16[3,8,16,1024]{3,2,1,0:T(8,128)(2,1)S(1)} %copy-done, f32[5,16,1024]{2,1,0:T(8,128)S(1)} %copy-done.13, f32[5,16,1024]{2,1,0:T(8,128)S(1)} %copy-done.15, f32[5,8,1024]{2,1,0:T(8,128)S(1)} %copy-done.19, f32[5,8,1024]{2,1,0:T(8,128)S(1)} %copy-done.21), custom_call_target="tpu_custom_call" | custom-call | flops 1310720 | bytes 3145728 | tf_op jit(solution)/shard_map/warm/pallas_call | solution.py:489
  81.1 7.1 %all-to-all-done.2.received = f32[32,40,128]{2,1,0:T(8,128)S(1)} async-done(((f32[32,40,128]{2,1,0:T(8,128)}), f32[32,40,128]{2,1,0:T(8,128)S(1)}, u32[]{:S(2)}, u32[]{:S(2)}) %all-to-all-start.2) | async-done | bytes 655392 | tf_op jit(solution)/shard_map/all_to_all | solution.py:430
  88.2 1.4 %copy-done.11 = f32[3,8,16,1024]{3,2,1,0:T(8,128)S(1)} copy-done((f32[3,8,16,1024]{3,2,1,0:T(8,128)S(1)}, f32[3,8,16,1024]{3,2,1,0:T(8,128)}, u32[]{:S(2)}) %copy-start.11) | copy-done | bytes 1572888
  89.6 3.3 %gradient.1 = f32[3,8,16,1024]{3,2,1,0:T(8,128)} custom-call(s32[2]{0:T(128)S(1)} %copy-done.31, f32[32,40,128]{2,1,0:T(8,128)S(1)} %all-to-all-done.2.received, bf16[512,512]{1,0:T(8,128)(2,1)S(1)} %copy-done.9, bf16[512,512]{1,0:T(8,128)(2,1)S(1)} %copy-done.8, bf16[512,512]{1,0:T(8,128)(2,1)S(1)} %copy-done.7, bf16[512,512]{1,0:T(8,128)(2,1)S(1)} %copy-done.6, ...), custom_call_target="tpu_custom_call" | custom-call | tf_op jit(solution)/shard_map/gradient/pallas_call | solution.py:517
  (53 shorter events, 1.4 us)
Async XLA Ops:
  0.6 1.4 %copy-start.1 = (f32[3,8,16,1024]{3,2,1,0:T(8,128)S(1)}, f32[3,8,16,1024]{3,2,1,0:T(8,128)}, u32[]{:S(2)}) copy-start(f32[3,8,16,1024]{3,2,1,0:T(8,128)} %motion.3) | copy-start | bytes 4718596
  2.0 1.0 %copy-start.3 = (f32[8,16,1024]{2,1,0:T(8,128)S(1)}, f32[8,16,1024]{2,1,0:T(8,128)}, u32[]{:S(2)}) copy-start(f32[8,16,1024]{2,1,0:T(8,128)} %thermal.5) | copy-start | bytes 1572868
  3.1 0.9 %copy-start.16 = (bf16[8,16,1024]{2,1,0:T(8,128)(2,1)S(1)}, bf16[8,16,1024]{2,1,0:T(8,128)(2,1)}, u32[]{:S(2)}) copy-start(bf16[8,16,1024]{2,1,0:T(8,128)(2,1)} %base.3) | copy-start | bytes 786436
  4.0 7.7 %copy-start = (bf16[3,8,16,1024]{3,2,1,0:T(8,128)(2,1)S(1)}, bf16[3,8,16,1024]{3,2,1,0:T(8,128)(2,1)}, u32[]{:S(2)}) copy-start(bf16[3,8,16,1024]{3,2,1,0:T(8,128)(2,1)} %flow.5) | copy-start | bytes 2359300
  4.0 7.7 %copy-start.2 = (f32[3,8,16,1024]{3,2,1,0:T(8,128)S(1)}, f32[3,8,16,1024]{3,2,1,0:T(8,128)}, u32[]{:S(2)}) copy-start(f32[3,8,16,1024]{3,2,1,0:T(8,128)} %motion.3) | copy-start | bytes 4718596
  4.2 12.8 %collective-permute-start = (f32[5,16,1024]{2,1,0:T(8,128)S(1)}, f32[5,16,1024]{2,1,0:T(8,128)S(1)}, u32[]{:S(2)}, u32[]{:S(2)}) collective-permute-start(f32[5,16,1024]{2,1,0:T(8,128)S(1)} %get-tuple-element.13), channel_id=1, source_target_pairs={{0,8},{8,16},{16,24},{24,32},{32,40},{40,48},{48,56},{56,64},{64,7... | collective-permute-start | bytes 983048 | tf_op jit(solution)/shard_map/ppermute | solution.py:426
  6.8 10.1 %collective-permute-start.1 = (f32[5,16,1024]{2,1,0:T(8,128)S(1)}, f32[5,16,1024]{2,1,0:T(8,128)S(1)}, u32[]{:S(2)}, u32[]{:S(2)}) collective-permute-start(f32[5,16,1024]{2,1,0:T(8,128)S(1)} %get-tuple-element.14), channel_id=1, source_target_pairs={{0,248},{8,0},{16,8},{24,16},{32,24},{40,32},{48,40},{56,48},{64,5... | collective-permute-start | bytes 983048 | tf_op jit(solution)/shard_map/ppermute | solution.py:426
  7.6 9.3 %collective-permute-start.2 = (f32[5,8,1024]{2,1,0:T(8,128)S(1)}, f32[5,8,1024]{2,1,0:T(8,128)S(1)}, u32[]{:S(2)}, u32[]{:S(2)}) collective-permute-start(f32[5,8,1024]{2,1,0:T(8,128)S(1)} %get-tuple-element.15), channel_id=1, source_target_pairs={{0,1},{1,2},{2,3},{3,4},{4,5},{5,6},{6,7},{8,9},{9,10},{10,11},{11... | collective-permute-start | bytes 491528 | tf_op jit(solution)/shard_map/ppermute | solution.py:426
  10.4 6.5 %collective-permute-start.3 = (f32[5,8,1024]{2,1,0:T(8,128)S(1)}, f32[5,8,1024]{2,1,0:T(8,128)S(1)}, u32[]{:S(2)}, u32[]{:S(2)}) collective-permute-start(f32[5,8,1024]{2,1,0:T(8,128)S(1)} %get-tuple-element.16), channel_id=1, source_target_pairs={{1,0},{2,1},{3,2},{4,3},{5,4},{6,5},{7,6},{9,8},{10,9},{11,10},{12... | collective-permute-start | bytes 491528 | tf_op jit(solution)/shard_map/ppermute | solution.py:426
  11.7 1.0 %copy-start.4 = (f32[8,16,1024]{2,1,0:T(8,128)S(1)}, f32[8,16,1024]{2,1,0:T(8,128)}, u32[]{:S(2)}) copy-start(f32[8,16,1024]{2,1,0:T(8,128)} %thermal.5) | copy-start | bytes 1572868
  12.8 0.9 %copy-start.17 = (bf16[8,16,1024]{2,1,0:T(8,128)(2,1)S(1)}, bf16[8,16,1024]{2,1,0:T(8,128)(2,1)}, u32[]{:S(2)}) copy-start(bf16[8,16,1024]{2,1,0:T(8,128)(2,1)} %base.3) | copy-start | bytes 786436
  13.7 3.3 %copy-start.5 = (f32[8,16,1024]{2,1,0:T(8,128)S(1)}, f32[8,16,1024]{2,1,0:T(8,128)}, u32[]{:S(2)}) copy-start(f32[8,16,1024]{2,1,0:T(8,128)} %thermal.5) | copy-start | bytes 1572868
  13.7 3.3 %copy-start.6 = (bf16[512,512]{1,0:T(8,128)(2,1)S(1)}, bf16[512,512]{1,0:T(8,128)(2,1)}, u32[]{:S(2)}) copy-start(bf16[512,512]{1,0:T(8,128)(2,1)} %constant.28.clone.odd_t) | copy-start | bytes 1572868
  13.7 3.3 %copy-start.7 = (bf16[512,512]{1,0:T(8,128)(2,1)S(1)}, bf16[512,512]{1,0:T(8,128)(2,1)}, u32[]{:S(2)}) copy-start(bf16[512,512]{1,0:T(8,128)(2,1)} %constant.27.clone.odd_h) | copy-start | bytes 1572868
  13.7 3.3 %copy-start.8 = (bf16[512,512]{1,0:T(8,128)(2,1)S(1)}, bf16[512,512]{1,0:T(8,128)(2,1)}, u32[]{:S(2)}) copy-start(bf16[512,512]{1,0:T(8,128)(2,1)} %constant.26.clone.even_t) | copy-start | bytes 1572868
  13.7 3.3 %copy-start.9 = (bf16[512,512]{1,0:T(8,128)(2,1)S(1)}, bf16[512,512]{1,0:T(8,128)(2,1)}, u32[]{:S(2)}) copy-start(bf16[512,512]{1,0:T(8,128)(2,1)} %constant.25.clone.even_h) | copy-start | bytes 1572868
  16.9 1.9 %copy-start.18 = (f32[5,8,1024]{2,1,0:T(8,128)}, f32[5,8,1024]{2,1,0:T(8,128)S(1)}, u32[]{:S(2)}) copy-start(f32[5,8,1024]{2,1,0:T(8,128)S(1)} %collective-permute-done.2.z_low) | copy-start | bytes 491524
  16.9 1.9 %copy-start.20 = (f32[5,8,1024]{2,1,0:T(8,128)}, f32[5,8,1024]{2,1,0:T(8,128)S(1)}, u32[]{:S(2)}) copy-start(f32[5,8,1024]{2,1,0:T(8,128)S(1)} %collective-permute-done.3.z_high) | copy-start | bytes 491524
  16.9 1.9 %copy-start.12 = (f32[5,16,1024]{2,1,0:T(8,128)}, f32[5,16,1024]{2,1,0:T(8,128)S(1)}, u32[]{:S(2)}) copy-start(f32[5,16,1024]{2,1,0:T(8,128)S(1)} %collective-permute-done.y_low) | copy-start | bytes 983044
  17.0 1.9 %copy-start.14 = (f32[5,16,1024]{2,1,0:T(8,128)}, f32[5,16,1024]{2,1,0:T(8,128)S(1)}, u32[]{:S(2)}) copy-start(f32[5,16,1024]{2,1,0:T(8,128)S(1)} %collective-permute-done.1.y_high) | copy-start | bytes 983044
  17.0 25.6 %copy-start.29 = (f32[32,128]{1,0:T(8,128)S(1)}, f32[32,128]{1,0:T(8,128)}, u32[]{:S(2)}) copy-start(f32[32,128]{1,0:T(8,128)} %constant.31.clone.line_x) | copy-start | bytes 49156
  18.8 1.1 %copy-start.10 = (f32[3,8,16,1024]{3,2,1,0:T(8,128)}, f32[3,8,16,1024]{3,2,1,0:T(8,128)S(1)}, u32[]{:S(2)}) copy-start(f32[3,8,16,1024]{3,2,1,0:T(8,128)S(1)} %get-tuple-element.20.provisional) | copy-start | bytes 4718596
  20.8 21.9 %all-to-all-start = ((f32[32,40,128]{2,1,0:T(8,128)}), f32[32,40,128]{2,1,0:T(8,128)S(1)}, u32[]{:S(2)}, u32[]{:S(2)}) async-start(f32[32,40,128]{2,1,0:T(8,128)} %copy-done.22), calls=%async_computation | async-start | bytes 1310720 | tf_op jit(solution)/shard_map/all_to_all | solution.py:430
  45.8 21.1 %copy-start.26 = (bf16[256,256]{1,0:T(8,128)(2,1)S(1)}, bf16[256,256]{1,0:T(8,128)(2,1)}, u32[]{:S(2)}) copy-start(bf16[256,256]{1,0:T(8,128)(2,1)} %constant.30.clone.span_t) | copy-start | bytes 393220
  69.4 18.8 %all-to-all-start.2 = ((f32[32,40,128]{2,1,0:T(8,128)}), f32[32,40,128]{2,1,0:T(8,128)S(1)}, u32[]{:S(2)}, u32[]{:S(2)}) async-start(f32[32,40,128]{2,1,0:T(8,128)} %up.1), calls=%async_computation.2 | async-start | bytes 1310720 | tf_op jit(solution)/shard_map/all_to_all | solution.py:430
  75.3 12.9 %copy-start.31 = (s32[2]{0:T(128)S(1)}, s32[2]{0:T(128)}, u32[]{:S(2)}) copy-start(s32[2]{0:T(128)} %pad_add_fusion.place) | copy-start | bytes 28
  75.3 1.0 %copy-start.13 = (f32[5,16,1024]{2,1,0:T(8,128)S(1)}, f32[5,16,1024]{2,1,0:T(8,128)}, u32[]{:S(2)}) copy-start(f32[5,16,1024]{2,1,0:T(8,128)} %copy-done.12) | copy-start | bytes 983044
  76.3 1.0 %copy-start.15 = (f32[5,16,1024]{2,1,0:T(8,128)S(1)}, f32[5,16,1024]{2,1,0:T(8,128)}, u32[]{:S(2)}) copy-start(f32[5,16,1024]{2,1,0:T(8,128)} %copy-done.14) | copy-start | bytes 983044
  77.3 0.9 copy-start.19
  78.2 0.9 copy-start.21
  79.1 1.0 %copy-start.24 = (f32[8,16,1024]{2,1,0:T(8,128)S(1)}, f32[8,16,1024]{2,1,0:T(8,128)}, u32[]{:S(2)}) copy-start(f32[8,16,1024]{2,1,0:T(8,128)} %copy-done.23) | copy-start | bytes 1572868
  88.2 1.4 %copy-start.11 = (f32[3,8,16,1024]{3,2,1,0:T(8,128)S(1)}, f32[3,8,16,1024]{3,2,1,0:T(8,128)}, u32[]{:S(2)}) copy-start(f32[3,8,16,1024]{3,2,1,0:T(8,128)} %copy-done.10) | copy-start | bytes 4718596
  (6 other events, 4.8 us)

commit v3 on v2

--- a/solution.py
+++ b/solution.py
@@ -18,6 +18,7 @@
 PIECE = 8 * (QUADS + 1)
 VMEM = pl.BlockSpec(memory_space=pltpu.VMEM)
 SMEM = pl.BlockSpec(memory_space=pltpu.SMEM)
+HBM = pl.BlockSpec(memory_space=pltpu.HBM)
 
 
 def two_parts(table):
@@ -36,15 +37,16 @@
     even = two_parts(cas(half[:, None] * half[None, :], size_x // 2))
     odd = two_parts(cas(half[:, None] * (2 * half[None, :] + 1), size_x))
     full = np.arange(size_y)
-    span = two_parts(cas(full[:, None] * full[None, :], size_y))
+    span = cas(full[:, None] * full[None, :], size_y)
     waves = np.concatenate([2 * half, 2 * half + 1])
     line_x = 4.0 * np.sin(np.pi * waves / size_x) ** 2
-    line_x = np.tile(line_x.reshape(-1, WAVES), (1, 128 // WAVES)).astype(np.float32)
+    line_x = np.tile(line_x.reshape(-1, WAVES), (1, 128 // WAVES))
     row = np.arange(size_y // 4)[:, None]
     lane = np.arange(128)[None, :]
     wave_y = 32 * (row // 8) + 8 * (lane // WAVES) + row % 8
-    line_y = (4.0 * np.sin(np.pi * wave_y / size_y) ** 2).astype(np.float32)
-    return even, odd, span, line_x, line_y
+    line_y = 4.0 * np.sin(np.pi * wave_y / size_y) ** 2
+    halves = [span[:, n * 128:(n + 1) * 128] for n in range(size_y // 128)]
+    return even, odd, np.concatenate(halves + [line_y, line_x], 0).astype(np.float32)
 
 
 def split(values):
@@ -95,22 +97,44 @@
     return jnp.concatenate([ref[b, pl.ds(start, count), :] for b in range(ref.shape[0])], 1)
 
 
-def sides_kernel(motion, thermal, base, y_first, y_last, z_first, z_last):
-    for out, y in ((y_first, 0), (y_last, ROWS - 1)):
-        for c in range(3):
-            out[c] = motion[c, y]
-        out[3] = thermal[y]
-        out[4] = base[y].astype(F32)
+def start_copies(pairs, sems):
+    copies = [pltpu.make_async_copy(a, b, sems.at[n]) for n, (a, b) in enumerate(pairs)]
+    for copy in copies:
+        copy.start()
+    return copies
+
+
+def sides_kernel(motion_hbm, thermal_hbm, base_hbm, y_first, y_last, z_first, z_last, motion, thermal, base, sems):
+    fetched = start_copies(((base_hbm, base), (thermal_hbm, thermal), (motion_hbm, motion)), sems)
+    fetched[0].wait()
     for y in range(ROWS):
         warm = base[y].astype(F32)
-        for out, z in ((z_first, 0), (z_last, LAYERS - 1)):
-            for c in range(3):
-                out[c, y:y + 1, :] = motion[c, y, z:z + 1, :]
-            out[3, y:y + 1, :] = thermal[y, z:z + 1, :]
-            out[4, y:y + 1, :] = warm[z:z + 1, :]
-
-
-def inner_kernel(motion, thermal, flow, base, moved, warmed):
+        z_first[4, y:y + 1, :] = warm[:1]
+        z_last[4, y:y + 1, :] = warm[LAYERS - 1:]
+        if y in (0, ROWS - 1):
+            (y_last if y else y_first)[4] = warm
+    fetched[1].wait()
+    y_first[3] = thermal[0]
+    y_last[3] = thermal[ROWS - 1]
+    for y in range(ROWS):
+        z_first[3, y:y + 1, :] = thermal[y, :1, :]
+        z_last[3, y:y + 1, :] = thermal[y, LAYERS - 1:, :]
+    fetched[2].wait()
+    for c in range(3):
+        y_first[c] = motion[c, 0]
+        y_last[c] = motion[c, ROWS - 1]
+        for y in range(ROWS):
+            z_first[c, y:y + 1, :] = motion[c, y, :1, :]
+            z_last[c, y:y + 1, :] = motion[c, y, LAYERS - 1:, :]
+
+
+def inner_kernel(
+    motion_hbm, thermal_hbm, flow_hbm, base_hbm, moved, row_factors, layer_factors,
+    motion, thermal, flow, base, sems,
+):
+    pairs = ((thermal_hbm, thermal), (base_hbm, base), (flow_hbm, flow), (motion_hbm, motion))
+    for copy in start_copies(pairs, sems):
+        copy.wait()
     size_x = motion.shape[-1]
     row = lax.broadcasted_iota(jnp.int32, (LAYERS, size_x), 0)
     top = row == LAYERS - 1
@@ -142,68 +166,52 @@
         slope_y = -gy if hy is None else hy if gy is None else hy - gy
         slopes = (hx - gx, slope_y, hz - gz)
         heat = thermal[y] * 0.1
+        if y == 0:
+            row_factors[0] = weights[3]
+            row_factors[1] = -heat
+        if y == ROWS - 1:
+            row_factors[2] = weights[2]
+            row_factors[3] = heat
+        layer_factors[0, y:y + 1, :] = weights[5][:1]
+        layer_factors[1, y:y + 1, :] = -heat[:1]
+        layer_factors[2, y:y + 1, :] = weights[4][LAYERS - 1:]
+        layer_factors[3, y:y + 1, :] = heat[LAYERS - 1:]
         for c in range(4):
             parts = neighbours(c, y)
             value = parts[0] * 0.88
             for weight, part in zip(weights, parts[1:]):
                 if part is not None:
                     value = value + weight * part
-            if c < 3:
-                moved[c, y] = value + heat * slopes[c]
-            else:
-                warmed[y] = value + 0.2 * motion[2, y]
-
-
-def edge_weights(flow, y):
-    size_x = flow.shape[-1]
-    row = lax.broadcasted_iota(jnp.int32, (8, size_x), 0)
-    speed = flow[2, y].astype(F32) * 0.1
-    first = jnp.where(row == 0, 0.02 - speed[:8], 0.0)
-    last = jnp.where(row == 7, 0.02 + speed[LAYERS - 8:], 0.0)
-    return row, first, last
-
-
-def warm_kernel(warmed, flow, y_low, y_high, z_low, z_high, thermal_out):
-    for y in range(ROWS):
-        value = warmed[y]
-        if y == 0:
-            value = value + (0.02 - flow[1, y].astype(F32) * 0.1) * y_low[3]
-        if y == ROWS - 1:
-            value = value + (0.02 + flow[1, y].astype(F32) * 0.1) * y_high[3]
-        _, first, last = edge_weights(flow, y)
-        thermal_out[y, :8] = value[:8] + first * z_low[3, y:y + 1, :]
-        thermal_out[y, 8:] = value[8:] + last * z_high[3, y:y + 1, :]
+            moved[c, y] = value + (heat * slopes[c] if c < 3 else 0.2 * motion[2, y])
 
 
 def source_kernel(
-    moved, thermal, flow, y_low, y_high, z_low, z_high, even_h, even_t, odd_h, odd_t,
-    provisional, message, source, lines, row_p, layer_p,
+    moved, row_factors, layer_factors, y_low, y_high, z_low, z_high, even_h, even_t, odd_h, odd_t,
+    provisional_hbm, thermal_hbm, message_hbm,
+    provisional, message, source, lines, row_p, layer_p, sems,
 ):
     size_x = moved.shape[-1]
+    row = lax.broadcasted_iota(jnp.int32, (8, size_x), 0)
     top = lax.broadcasted_iota(jnp.int32, (LAYERS, size_x), 0) == LAYERS - 1
+    lows = [layer_factors[0] * z_low[c] for c in range(4)]
+    highs = [layer_factors[2] * z_high[c] for c in range(4)]
+    lows[2] = lows[2] + layer_factors[1] * z_low[4]
+    highs[2] = highs[2] + layer_factors[3] * z_high[4]
     carried = None
     for y in range(ROWS):
-        row, first, last = edge_weights(flow, y)
-        fields = []
-        for c in range(3):
+        for c in range(4):
             value = moved[c, y]
             if y == 0:
-                value = value + (0.02 - flow[1, y].astype(F32) * 0.1) * y_low[c]
+                value = value + row_factors[0] * y_low[c]
                 if c == 1:
-                    value = value - thermal[y] * 0.1 * y_low[4]
+                    value = value + row_factors[1] * y_low[4]
             if y == ROWS - 1:
-                value = value + (0.02 + flow[1, y].astype(F32) * 0.1) * y_high[c]
+                value = value + row_factors[2] * y_high[c]
                 if c == 1:
-                    value = value + thermal[y] * 0.1 * y_high[4]
-            low = value[:8] + first * z_low[c, y:y + 1, :]
-            high = value[8:] + last * z_high[c, y:y + 1, :]
-            if c == 2:
-                low = low - jnp.where(row == 0, thermal[y, :8] * 0.1, 0.0) * z_low[4, y:y + 1, :]
-                high = high + jnp.where(row == 7, thermal[y, 8:] * 0.1, 0.0) * z_high[4, y:y + 1, :]
-            value = jnp.concatenate([low, high], 0)
-            provisional[c, y] = value
-            fields.append(value)
-        p0, p1, p2 = fields
+                    value = value + row_factors[3] * y_high[4]
+            provisional[c, y, :8] = value[:8] + jnp.where(row == 0, lows[c][y:y + 1], 0.0)
+            provisional[c, y, 8:] = value[8:] + jnp.where(row == 7, highs[c][y:y + 1], 0.0)
+        p0, p1, p2 = (provisional[c, y] for c in range(3))
         if y == 0:
             keep(row_p, 0, p1)
         else:
@@ -212,6 +220,9 @@
         above = jnp.where(top, 0.0, pltpu.roll(p2, LAYERS - 1, 0))
         carried = (pltpu.roll(p0, size_x - 1, 1) - p0) - p1 + (above - p2)
     keep(source, (ROWS - 1) * LAYERS, carried)
+    stored = start_copies(
+        ((provisional.at[pl.ds(0, 3)], provisional_hbm), (provisional.at[3], thermal_hbm)), sems
+    )
 
     for b in range(size_x // 128):
         lanes = pl.ds(b * 128, 128)
@@ -223,20 +234,30 @@
             lines[pl.ds(j * PIECE + 38, 2), lanes] = jnp.zeros((2, 128), F32)
     near = lines[:, : size_x // 2]
     far = lines[:, size_x // 2:]
-    evens = product(near + far, even_h[...], even_t[...], dot)
-    odds = product(near - far, odd_h[...], odd_t[...], dot)
-    for block in range(size_x // 128):
-        part, at = (evens, block) if block < size_x // 256 else (odds, block - size_x // 256)
-        a = [part[j * PIECE:(j + 1) * PIECE, at * 128:(at + 1) * 128] for j in range(4)]
-        for i, piece in enumerate(swap_groups(a)):
-            message[4 * block + i] = piece
-
-
-def mode_constants(place, line_x, line_y):
-    a = line_x[pl.ds(place[0], 1), :] + line_y[...]
-    sinh = jnp.sqrt(a * (1.0 + 0.25 * a))
-    lam = 1.0 / (1.0 + 0.5 * a + sinh)
-    return a, sinh, lam
+    half = size_x // 256
+    for turn in range(2):
+        if turn == 0:
+            waves = product(near + far, even_h[...], even_t[...], dot)
+        else:
+            waves = product(near - far, odd_h[...], odd_t[...], dot)
+        for block in range(half):
+            a = [waves[j * PIECE:(j + 1) * PIECE, block * 128:(block + 1) * 128] for j in range(4)]
+            for i, piece in enumerate(swap_groups(a)):
+                message[4 * (turn * half + block) + i] = piece
+        part = pl.ds(turn * 4 * half, 4 * half)
+        copy = pltpu.make_async_copy(message.at[part], message_hbm.at[part], sems.at[2 + turn])
+        copy.start()
+        stored.append(copy)
+    for copy in stored:
+        copy.wait()
+
+
+def span_product(table, values):
+    size_y = values.shape[0]
+    wide = jnp.concatenate([table[pl.ds(n * size_y, size_y), :] for n in range(size_y // 128)], 1)
+    left = split(wide)
+    right = split(values)
+    return dot(left[0], right[0]) + (dot(left[0], right[1]) + dot(left[1], right[0]))
 
 
 def wall_factors(lam, slab, slabs):
@@ -262,10 +283,12 @@
     return floor, ceiling, powers
 
 
-def down_kernel(place, received, span_h, span_t, line_x, line_y, spectral, handed):
+def down_kernel(place, received, table_hbm, spectral, handed, table, sems):
+    fetched = start_copies(((table_hbm, table),), sems)
     sources = received.shape[0]
     size_y = sources * ROWS
     slabs = handed.shape[0]
+    size_x = sources * WAVES
     slab = place[1]
     row = lax.broadcasted_iota(jnp.int32, (sources, 8, 128), 1)
     group = lane_group((sources, 8, 128))
@@ -281,9 +304,8 @@
     layer = jnp.where(row < 4, first, second)
     layer = jnp.where((row % 4 == group) & (slab > 0), layer, 0.0)
     columns.append(layer.reshape(size_y, 128))
-    stacked = jnp.concatenate(columns, 1)
-    head, tail = split(stacked)
-    waves = dot(span_h[...], head) + (dot(span_h[...], tail) + dot(span_t[...], head))
+    fetched[0].wait()
+    waves = span_product(table, jnp.concatenate(columns, 1))
 
     last = waves[:, 128 * QUADS:]
     last = last + pltpu.roll(last, 64, 1)
@@ -301,8 +323,19 @@
     for q in range(QUADS):
         block = waves[:, 128 * q:128 * (q + 1)].reshape(size_y // 32, 4, 8, 128)
         layers += swap_groups([block[:, i].reshape(modes, 128) for i in range(4)])
-    _, _, lam = mode_constants(place, line_x, line_y)
-    floor, ceiling, _ = wall_factors(lam, slab, slabs)
+    modes = size_y // 4
+    line_y = table[pl.ds(2 * size_y, modes), :]
+    a = table[pl.ds(2 * size_y + modes + place[0], 1), :] + line_y
+    sinh = jnp.sqrt(a * (1.0 + 0.25 * a))
+    lam = 1.0 / (1.0 + 0.5 * a + sinh)
+    floor, ceiling, powers = wall_factors(lam, slab, slabs)
+    spectral[LAYERS + 1] = lam
+    whole = powers[LAYERS]
+    for _ in range((slabs - 1).bit_length()):
+        whole = whole * whole
+    zero = a == 0.0
+    weight = (-1.0 / (size_x * size_y)) / jnp.where(zero, 1.0, 2.0 * sinh * (1.0 - whole))
+    spectral[LAYERS + 2] = jnp.where(zero, 0.0, weight)
     upward = jnp.zeros_like(lam)
     downward = jnp.zeros_like(lam)
     for l in range(LAYERS + 1):
@@ -314,23 +347,19 @@
         handed[d] = jnp.where(d > slab, upward, downward)
 
 
-def up_kernel(place, spectral, handed, span_h, span_t, line_x, line_y, message):
-    size_y = span_h.shape[0]
-    sources = size_y // ROWS
+def up_kernel(place, spectral, handed, table_hbm, message_hbm, table, message, sems):
+    fetched = start_copies(((table_hbm, table),), sems)
+    sources = message.shape[0]
+    size_y = sources * ROWS
     slabs = handed.shape[0]
-    size_x = line_x.shape[0] * WAVES
+    size_x = sources * WAVES
     size_z = slabs * LAYERS
     slab = place[1]
-    a, sinh, lam = mode_constants(place, line_x, line_y)
+    lam = spectral[LAYERS + 1]
+    weight = spectral[LAYERS + 2]
     floor, ceiling, powers = wall_factors(lam, slab, slabs)
     scale = 1.0 / (size_x * size_y)
-    whole = powers[LAYERS]
     reach = powers[LAYERS // 2]
-    for _ in range((slabs - 1).bit_length()):
-        whole = whole * whole
-    zero = a == 0.0
-    weight = (-scale) / jnp.where(zero, 1.0, 2.0 * sinh * (1.0 - whole))
-    weight = jnp.where(zero, 0.0, weight)
     upward = jnp.zeros_like(lam)
     downward = jnp.zeros_like(lam)
     for d in range(slabs - 1):
@@ -349,7 +378,7 @@
         downward = lam * (downward + ceiling[l] * spectral[l])
     modes = size_y // 4
     flat = jnp.zeros((8, 128), F32)
-    first_zero = zero[:8]
+    first_zero = weight[:8] == 0.0
     for l in range(LAYERS + 1):
         if l:
             count = (slab * LAYERS + (l - 1)).astype(F32)
@@ -370,9 +399,8 @@
         part = part + pltpu.roll(part, 64, 1)
         spread.append((part + pltpu.roll(part, 32, 1)).reshape(tall))
     columns.append(jnp.concatenate(spread, 1).reshape(size_y, 128))
-    stacked = jnp.concatenate(columns, 1)
-    head, tail = split(stacked)
-    values = dot(span_h[...], head) + (dot(span_h[...], tail) + dot(span_t[...], head))
+    fetched[0].wait()
+    values = span_product(table, jnp.concatenate(columns, 1))
 
     row = lax.broadcasted_iota(jnp.int32, (sources, 8, 128), 1)
     group = lane_group((sources, 8, 128))
@@ -389,11 +417,16 @@
     extra = jnp.where(row == 4, jnp.broadcast_to(layer[:, 0:1, :], extra.shape), extra)
     extra = jnp.where(row == 5, jnp.broadcast_to(layer[:, 4:5, :], extra.shape), extra)
     message[:, 8 * QUADS:, :] = extra
+    copy = pltpu.make_async_copy(message, message_hbm, sems.at[1])
+    copy.start()
+    copy.wait()
 
 
 def gradient_kernel(
-    place, received, even_h, even_t, odd_h, odd_t, provisional, motion, lines, pressure, row_p, layer_p
+    place, received, even_h, even_t, odd_h, odd_t, provisional_hbm, motion_hbm,
+    provisional, motion, lines, pressure, row_p, layer_p, sems,
 ):
+    fetched = start_copies(((provisional_hbm, provisional),), sems)
     size_x = provisional.shape[-1]
     for block in range(size_x // 128):
         for j, piece in enumerate(swap_groups([received[4 * block + i] for i in range(4)])):
@@ -409,6 +442,8 @@
                 pressure[b, pl.ds(4 * q + j, ROWS, stride=LAYERS), :] = lines[pl.ds(j * PIECE + q * 8, 8), lanes]
             row_p[b, pl.ds(j, 4, stride=4), :] = lines[pl.ds(j * PIECE + 32, 4), lanes]
             layer_p[b, pl.ds(j, 2, stride=4), :] = lines[pl.ds(j * PIECE + 36, 2), lanes]
+    fetched[0].wait()
+    stored = []
     bottom = lax.broadcasted_iota(jnp.int32, (LAYERS, size_x), 0) == 0
     for y in range(ROWS):
         p = kept(pressure, y * LAYERS, LAYERS)
@@ -418,6 +453,11 @@
         motion[0, y] = provisional[0, y] - (p - pltpu.roll(p, 1, 1))
         motion[1, y] = provisional[1, y] - (p - before)
         motion[2, y] = provisional[2, y] - slope_z
+        copy = pltpu.make_async_copy(motion.at[:, pl.ds(y, 1)], motion_hbm.at[:, pl.ds(y, 1)], sems.at[1 + y])
+        copy.start()
+        stored.append(copy)
+    for copy in stored:
+        copy.wait()
 
 
 def shifted(value, axis, by, periodic):
@@ -438,96 +478,130 @@
     size_x = dual_thermal.shape[-1]
     groups_y = lax.axis_size("gy")
     groups_z = lax.axis_size("gz")
-    even, odd, span, line_x, line_y = tables(size_x, ROWS * groups_y)
+    even, odd, table = tables(size_x, ROWS * groups_y)
     even_h, even_t = map(jnp.asarray, even)
     odd_h, odd_t = map(jnp.asarray, odd)
-    span_h, span_t = map(jnp.asarray, span)
-    line_x, line_y = jnp.asarray(line_x), jnp.asarray(line_y)
-    modes = line_y.shape[0]
+    size_t = table.shape[0]
+    modes = ROWS * groups_y // 4
+    blocks = size_x // 128
     place = jnp.stack([lax.axis_index("gy"), lax.axis_index("gz")]).astype(jnp.int32)
+
+    def hbm(value):
+        return pltpu.with_memory_space_constraint(value, pltpu.HBM)
 
     def params(mib):
         return pltpu.CompilerParams(vmem_limit_bytes=mib << 20)
 
+    motion_in, thermal_in, flow_in, base_in = map(hbm, (dual_motion, dual_thermal, flow, base))
+    table = hbm(jnp.asarray(table))
     rows = shape_of(5, LAYERS, size_x)
     layers = shape_of(5, ROWS, size_x)
+    motion_shape = (3, ROWS, LAYERS, size_x)
+    thermal_shape = motion_shape[1:]
+    message_shape = (groups_y, PIECE, 128)
     y_first, y_last, z_first, z_last = pl.pallas_call(
         sides_kernel,
         out_shape=(rows, rows, layers, layers),
-        in_specs=[VMEM] * 3,
+        in_specs=[HBM] * 3,
         out_specs=(VMEM,) * 4,
-        compiler_params=params(8),
+        scratch_shapes=[
+            pltpu.VMEM(motion_shape, F32),
+            pltpu.VMEM(thermal_shape, F32),
+            pltpu.VMEM(thermal_shape, BF16),
+            pltpu.SemaphoreType.DMA((3,)),
+        ],
+        compiler_params=params(16),
         name="sides",
-    )(dual_motion, dual_thermal, base)
+    )(motion_in, thermal_in, base_in)
     z_low = shifted(z_last, "gz", 1, False)
     z_high = shifted(z_first, "gz", -1, False)
     y_low = shifted(y_last, "gy", 1, True)
     y_high = shifted(y_first, "gy", -1, True)
-    moved, warmed = pl.pallas_call(
+    moved, row_factors, layer_factors = pl.pallas_call(
         inner_kernel,
-        out_shape=(shape_of(3, ROWS, LAYERS, size_x), shape_of(ROWS, LAYERS, size_x)),
-        in_specs=[VMEM] * 4,
-        out_specs=(VMEM,) * 2,
+        out_shape=(
+            shape_of(4, *thermal_shape),
+            shape_of(4, LAYERS, size_x),
+            shape_of(4, ROWS, size_x),
+        ),
+        in_specs=[HBM] * 4,
+        out_specs=(VMEM,) * 3,
+        scratch_shapes=[
+            pltpu.VMEM(motion_shape, F32),
+            pltpu.VMEM(thermal_shape, F32),
+            pltpu.VMEM(motion_shape, BF16),
+            pltpu.VMEM(thermal_shape, BF16),
+            pltpu.SemaphoreType.DMA((4,)),
+        ],
         compiler_params=params(16),
-        cost_estimate=pl.CostEstimate(flops=80 * ROWS * LAYERS * size_x, transcendentals=0, bytes_accessed=10 << 20),
+        cost_estimate=pl.CostEstimate(
+            flops=80 * ROWS * LAYERS * size_x, transcendentals=0, bytes_accessed=10 << 20
+        ),
         name="inner",
-    )(dual_motion, dual_thermal, flow, base)
-    provisional, message = pl.pallas_call(
+    )(motion_in, thermal_in, flow_in, base_in)
+    provisional, thermal_out, message = pl.pallas_call(
         source_kernel,
-        out_shape=(shape_of(3, ROWS, LAYERS, size_x), shape_of(groups_y, PIECE, 128)),
+        out_shape=(
+            pltpu.HBM(motion_shape, F32),
+            pltpu.HBM(thermal_shape, F32),
+            pltpu.HBM(message_shape, F32),
+        ),
         in_specs=[VMEM] * 11,
-        out_specs=(VMEM,) * 2,
+        out_specs=(HBM,) * 3,
         scratch_shapes=[
-            pltpu.VMEM((size_x // 128, ROWS * LAYERS, 128), F32),
+            pltpu.VMEM((4, *thermal_shape), F32),
+            pltpu.VMEM(message_shape, F32),
+            pltpu.VMEM((blocks, ROWS * LAYERS, 128), F32),
             pltpu.VMEM((4 * PIECE, size_x), F32),
-            pltpu.VMEM((size_x // 128, LAYERS, 128), F32),
-            pltpu.VMEM((size_x // 128, ROWS, 128), F32),
+            pltpu.VMEM((blocks, LAYERS, 128), F32),
+            pltpu.VMEM((blocks, ROWS, 128), F32),
+            pltpu.SemaphoreType.DMA((4,)),
         ],
         compiler_params=params(24),
         name="source",
-    )(moved, dual_thermal, flow, y_low, y_high, z_low, z_high, even_h, even_t, odd_h, odd_t)
-    thermal_out = pl.pallas_call(
-        warm_kernel,
-        out_shape=shape_of(ROWS, LAYERS, size_x),
-        in_specs=[VMEM] * 6,
-        out_specs=VMEM,
-        compiler_params=params(8),
-        cost_estimate=pl.CostEstimate(flops=10 * ROWS * LAYERS * size_x, transcendentals=0, bytes_accessed=3 << 20),
-        name="warm",
-    )(warmed, flow, y_low, y_high, z_low, z_high)
+    )(moved, row_factors, layer_factors, y_low, y_high, z_low, z_high, even_h, even_t, odd_h, odd_t)
     received = exchanged(message, "gy")
     spectral, handed = pl.pallas_call(
         down_kernel,
-        out_shape=(shape_of(LAYERS + 1, modes, 128), shape_of(groups_z, modes, 128)),
-        in_specs=[SMEM] + [VMEM] * 5,
+        out_shape=(shape_of(LAYERS + 3, modes, 128), shape_of(groups_z, modes, 128)),
+        in_specs=[SMEM, VMEM, HBM],
         out_specs=(VMEM,) * 2,
+        scratch_shapes=[pltpu.VMEM((size_t, 128), F32), pltpu.SemaphoreType.DMA((1,))],
         compiler_params=params(16),
         name="down",
-    )(place, received, span_h, span_t, line_x, line_y)
+    )(place, received, table)
     handed = exchanged(handed, "gz")
     message = pl.pallas_call(
         up_kernel,
-        out_shape=shape_of(groups_y, PIECE, 128),
-        in_specs=[SMEM] + [VMEM] * 6,
-        out_specs=VMEM,
+        out_shape=pltpu.HBM(message_shape, F32),
+        in_specs=[SMEM, VMEM, VMEM, HBM],
+        out_specs=HBM,
+        scratch_shapes=[
+            pltpu.VMEM((size_t, 128), F32),
+            pltpu.VMEM(message_shape, F32),
+            pltpu.SemaphoreType.DMA((2,)),
+        ],
         compiler_params=params(16),
         name="up",
-    )(place, spectral, handed, span_h, span_t, line_x, line_y)
+    )(place, spectral, handed, table)
     received = exchanged(message, "gy")
     motion = pl.pallas_call(
         gradient_kernel,
-        out_shape=shape_of(3, ROWS, LAYERS, size_x),
-        in_specs=[SMEM] + [VMEM] * 6,
-        out_specs=VMEM,
+        out_shape=pltpu.HBM(motion_shape, F32),
+        in_specs=[SMEM] + [VMEM] * 5 + [HBM],
+        out_specs=HBM,
         scratch_shapes=[
+            pltpu.VMEM(motion_shape, F32),
+            pltpu.VMEM(motion_shape, F32),
             pltpu.VMEM((4 * PIECE, size_x), F32),
-            pltpu.VMEM((size_x // 128, ROWS * LAYERS, 128), F32),
-            pltpu.VMEM((size_x // 128, LAYERS, 128), F32),
-            pltpu.VMEM((size_x // 128, ROWS, 128), F32),
+            pltpu.VMEM((blocks, ROWS * LAYERS, 128), F32),
+            pltpu.VMEM((blocks, LAYERS, 128), F32),
+            pltpu.VMEM((blocks, ROWS, 128), F32),
+            pltpu.SemaphoreType.DMA((1 + ROWS,)),
         ],
         compiler_params=params(24),
         name="gradient",
-    )(place, received, even_h, even_t, odd_h, odd_t, provisional)
+    )(place, received, even_h, even_t, odd_h, odd_t, hbm(provisional))
     return motion, thermal_out
 
 

time: 93.7 us -> 87.6 us (0.935)
  blocking collectives: 19.6 us -> 37.5 us
  local copies, waits for them, and re-layouts: 17.6 us -> 0.03 us
  waiting for transfers between devices: 19.5 us -> 13.5 us
  Pallas kernels: 12.4 us -> 18.4 us
  starting transfers between devices: 22.3 us -> 16.8 us
    all_to_all x1 -> x2, blocking collectives: 19.6 us -> 37.5 us  [exchanged(): return lax.all_to_all(pieces, axis, split_axis=0, concat_axis=0, tiled=True)]
    unnamed x64 -> x8, local copies, waits for them, and re-layouts: 17.6 us -> 0.03 us
    all_to_all x2 -> x1, waiting for transfers between devices: 19.5 us -> 12.8 us  [exchanged(): return lax.all_to_all(pieces, axis, split_axis=0, concat_axis=0, tiled=True)]
    all_to_all x2 -> x1, starting transfers between devices: 14.8 us -> 9.16 us  [exchanged(): return lax.all_to_all(pieces, axis, split_axis=0, concat_axis=0, tiled=True)]
    pallas_call x6 -> x5, Pallas kernels: 12.3 us -> 16.6 us  [the longest x1 4.3 us: on_device(): pl.pallas_call(inner_kernel, out_shape=(shape_of(4, *thermal_shape), shap...]
    pallas_call x1, Pallas kernels: 0.13 us -> 1.76 us  [on_device(): pl.pallas_call(sides_kernel, out_shape=(rows, rows, layers, layers), in_s...]
  transfers between devices with their start and end apart: 6 -> 5, of which waited for: 2 -> 2; matrix products, arithmetic and copies ran while one was open for 1% -> 0% of each run, Pallas kernels for 4% -> 5%
where the time goes in v3:
time: 87.6 us; the launch traced here: 87.1 us
  blocking collectives  37.5 us (43%)
  Pallas kernels  18.4 us (21%)
  starting transfers between devices  16.8 us (19%)
  waiting for transfers between devices  13.5 us (15%)
    all_to_all x2, blocking collectives, exchanged(): return lax.all_to_all(pieces, axis, split_axis=0, concat_axis=0, tiled=True)  37.5 us
    all_to_all x1, waiting for transfers between devices, exchanged(): return lax.all_to_all(pieces, axis, split_axis=0, concat_axis=0, tiled=True)  12.8 us
    all_to_all x1, starting transfers between devices, exchanged(): return lax.all_to_all(pieces, axis, split_axis=0, concat_axis=0, tiled=True)  9.16 us
    ppermute x4, starting transfers between devices, shifted(): return lax.ppermute(value, axis, pairs)  7.64 us
    pallas_call x1, Pallas kernels, on_device(): pl.pallas_call(inner_kernel, out_shape=(shape_of(4, *thermal_shape), shap...  4.3 us
    pallas_call x1, Pallas kernels, on_device(): pl.pallas_call(gradient_kernel, out_shape=pltpu.HBM(motion_shape, F32), i...  4.03 us
    pallas_call x1, Pallas kernels, on_device(): pl.pallas_call(up_kernel, out_shape=pltpu.HBM(message_shape, F32), in_spe...  3.52 us
    pallas_call x1, Pallas kernels, on_device(): pl.pallas_call(down_kernel, out_shape=(shape_of(LAYERS + 3, modes, 128),...  2.39 us
  transfers between devices with their start and end apart: 5, of which 2 were waited for; matrix products, arithmetic and copies ran while one was open for 0% of the time, Pallas kernels for 5%

profile of v3, /device:TPU:1, one launch (start us, length us, event | category | flops | bytes accessed | tf_op | source)
XLA Modules:
  0.0 87.1 jit_solution(18349447033949731606)
XLA Ops:
  0.6 1.8 %sides.1 = (f32[5,16,1024]{2,1,0:T(8,128)S(1)}, f32[5,16,1024]{2,1,0:T(8,128)S(1)}, f32[5,8,1024]{2,1,0:T(8,128)S(1)}, f32[5,8,1024]{2,1,0:T(8,128)S(1)}) custom-call(f32[3,8,16,1024]{3,2,1,0:T(8,128)} %motion_hbm.3, f32[8,16,1024]{2,1,0:T(8,128)} %thermal_hbm.3, bf16[8,16,1024]{2,1,0:T(8,128)(2,1)} %base_hbm.3), custom_call_target="tpu_custom_call" | custom-call | tf_op jit(solution)/shard_map/sides/pallas_call | solution.py:502
  2.4 2.7 %collective-permute-start = (f32[5,16,1024]{2,1,0:T(8,128)S(1)}, f32[5,16,1024]{2,1,0:T(8,128)S(1)}, u32[]{:S(2)}, u32[]{:S(2)}) collective-permute-start(f32[5,16,1024]{2,1,0:T(8,128)S(1)} %get-tuple-element.17), channel_id=1, source_target_pairs={{0,8},{8,16},{16,24},{24,32},{32,40},{40,48},{48,56},{56,64},{64,7... | collective-permute-start | bytes 983048 | tf_op jit(solution)/shard_map/ppermute | solution.py:466
  5.1 0.7 collective-permute-start.1
  5.8 2.8 %collective-permute-start.2 = (f32[5,8,1024]{2,1,0:T(8,128)S(1)}, f32[5,8,1024]{2,1,0:T(8,128)S(1)}, u32[]{:S(2)}, u32[]{:S(2)}) collective-permute-start(f32[5,8,1024]{2,1,0:T(8,128)S(1)} %get-tuple-element.19), channel_id=1, source_target_pairs={{0,1},{1,2},{2,3},{3,4},{4,5},{5,6},{6,7},{8,9},{9,10},{10,11},{11... | collective-permute-start | bytes 491528 | tf_op jit(solution)/shard_map/ppermute | solution.py:466
  8.6 0.0 copy-start
  8.6 0.0 copy-start.1
  8.7 0.0 copy-start.2
  8.7 0.0 copy-start.3
  8.7 1.4 %collective-permute-start.3 = (f32[5,8,1024]{2,1,0:T(8,128)S(1)}, f32[5,8,1024]{2,1,0:T(8,128)S(1)}, u32[]{:S(2)}, u32[]{:S(2)}) collective-permute-start(f32[5,8,1024]{2,1,0:T(8,128)S(1)} %get-tuple-element.20), channel_id=1, source_target_pairs={{1,0},{2,1},{3,2},{4,3},{5,4},{6,5},{7,6},{9,8},{10,9},{11,10},{12... | collective-permute-start | bytes 491528 | tf_op jit(solution)/shard_map/ppermute | solution.py:466
  10.1 4.3 %inner.1 = (f32[4,8,16,1024]{3,2,1,0:T(8,128)S(1)}, f32[4,16,1024]{2,1,0:T(8,128)S(1)}, f32[4,8,1024]{2,1,0:T(8,128)S(1)}) custom-call(f32[3,8,16,1024]{3,2,1,0:T(8,128)} %motion_hbm.3, f32[8,16,1024]{2,1,0:T(8,128)} %thermal_hbm.3, bf16[3,8,16,1024]{3,2,1,0:T(8,128)(2,1)} %flow_hbm.1, bf16[8,16,1024]{2,1,0:T(8,128)(2,1)} %base_hbm.3), custom_call_target="tpu_custom_call" | custom-call | flops 10485760 | bytes 10485760 | tf_op jit(solution)/shard_map/inner/pallas_call | solution.py:520
  14.4 0.0 collective-permute-done.2.z_low
  14.4 0.7 collective-permute-done.3.z_high
  15.1 0.0 collective-permute-done.y_low
  15.1 0.0 collective-permute-done.1.y_high
  15.2 0.0 copy-done
  15.2 0.0 copy-done.1
  15.2 0.0 copy-done.2
  15.2 0.0 copy-done.3
  15.2 2.4 %source.1 = (f32[3,8,16,1024]{3,2,1,0:T(8,128)}, f32[8,16,1024]{2,1,0:T(8,128)}, f32[32,40,128]{2,1,0:T(8,128)}) custom-call(f32[4,8,16,1024]{3,2,1,0:T(8,128)S(1)} %get-tuple-element.14.moved, f32[4,16,1024]{2,1,0:T(8,128)S(1)} %get-tuple-element.15.row_factors, f32[4,8,1024]{2,1,0:T(8,128)S(1)} %get-tuple-element.16.layer_factors, ...), custom_call_target="tpu_custom_call" | custom-call | tf_op jit(solution)/shard_map/source/pallas_call | solution.py:542
  17.6 9.2 %all-to-all-start = ((f32[32,40,128]{2,1,0:T(8,128)}), f32[32,40,128]{2,1,0:T(8,128)S(1)}, u32[]{:S(2)}, u32[]{:S(2)}) async-start(f32[32,40,128]{2,1,0:T(8,128)} %get-tuple-element.21), calls=%async_computation | async-start | bytes 1310720 | tf_op jit(solution)/shard_map/all_to_all | solution.py:470
  26.7 0.1 pad_add_fusion.place
  26.8 12.8 %all-to-all-done.received = f32[32,40,128]{2,1,0:T(8,128)S(1)} async-done(((f32[32,40,128]{2,1,0:T(8,128)}), f32[32,40,128]{2,1,0:T(8,128)S(1)}, u32[]{:S(2)}, u32[]{:S(2)}) %all-to-all-start) | async-done | bytes 655392 | tf_op jit(solution)/shard_map/all_to_all | solution.py:470
  39.6 2.4 %down.1 = (f32[19,64,128]{2,1,0:T(8,128)S(1)}, f32[8,64,128]{2,1,0:T(8,128)S(1)}) custom-call(s32[2]{0:T(128)S(1)} %pad_add_fusion.place, f32[32,40,128]{2,1,0:T(8,128)S(1)} %all-to-all-done.received, f32[608,128]{1,0:T(8,128)} %constant.23.clone.table_hbm), custom_call_target="tpu_custom_call" | custom-call | tf_op jit(solution)/shard_map/down/pallas_call | solution.py:564
  42.0 18.7 %all_to_all.15.handed = f32[8,64,128]{2,1,0:T(8,128)S(1)} all-to-all(f32[8,64,128]{2,1,0:T(8,128)S(1)} %get-tuple-element.23), channel_id=1, replica_groups=mesh['gy'=32,'gz'=8] {'gz'}, dimensions={0} | all-to-all | bytes 524288 | tf_op jit(solution)/shard_map/all_to_all | solution.py:470
  60.7 3.5 %up.1 = f32[32,40,128]{2,1,0:T(8,128)} custom-call(s32[2]{0:T(128)S(1)} %pad_add_fusion.place, f32[19,64,128]{2,1,0:T(8,128)S(1)} %get-tuple-element.22.spectral, f32[8,64,128]{2,1,0:T(8,128)S(1)} %all_to_all.15.handed, f32[608,128]{1,0:T(8,128)} %constant.23.clone.table_hbm), custom_call_target="tpu_custom_call" | custom-call | tf_op jit(solution)/shard_map/up/pallas_call | solution.py:574
  64.3 18.8 %all_to_all.16.received = f32[32,40,128]{2,1,0:T(8,128)S(1)} all-to-all(f32[32,40,128]{2,1,0:T(8,128)} %up.1), channel_id=1, replica_groups=mesh['gy'=32,'gz'=8] {'gy'}, dimensions={0} | all-to-all | bytes 1310720 | tf_op jit(solution)/shard_map/all_to_all | solution.py:470
  83.0 4.0 %gradient.1 = f32[3,8,16,1024]{3,2,1,0:T(8,128)} custom-call(s32[2]{0:T(128)S(1)} %pad_add_fusion.place, f32[32,40,128]{2,1,0:T(8,128)S(1)} %all_to_all.16.received, bf16[512,512]{1,0:T(8,128)(2,1)S(1)} %copy-done, bf16[512,512]{1,0:T(8,128)(2,1)S(1)} %copy-done.1, bf16[512,512]{1,0:T(8,128)(2,1)S(1)} %copy-done.2, bf16[512,512]{1,0:T(8,128)(2,1)S(1)} %copy-done.3, ...), custom_call_target="tpu_custom_call" | custom-call | tf_op jit(solution)/shard_map/gradient/pallas_call | solution.py:588
Async XLA Ops:
  2.4 12.7 %collective-permute-start = (f32[5,16,1024]{2,1,0:T(8,128)S(1)}, f32[5,16,1024]{2,1,0:T(8,128)S(1)}, u32[]{:S(2)}, u32[]{:S(2)}) collective-permute-start(f32[5,16,1024]{2,1,0:T(8,128)S(1)} %get-tuple-element.17), channel_id=1, source_target_pairs={{0,8},{8,16},{16,24},{24,32},{32,40},{40,48},{48,56},{56,64},{64,7... | collective-permute-start | bytes 983048 | tf_op jit(solution)/shard_map/ppermute | solution.py:466
  5.1 10.1 %collective-permute-start.1 = (f32[5,16,1024]{2,1,0:T(8,128)S(1)}, f32[5,16,1024]{2,1,0:T(8,128)S(1)}, u32[]{:S(2)}, u32[]{:S(2)}) collective-permute-start(f32[5,16,1024]{2,1,0:T(8,128)S(1)} %get-tuple-element.18), channel_id=1, source_target_pairs={{0,248},{8,0},{16,8},{24,16},{32,24},{40,32},{48,40},{56,48},{64,5... | collective-permute-start | bytes 983048 | tf_op jit(solution)/shard_map/ppermute | solution.py:466
  5.8 8.6 %collective-permute-start.2 = (f32[5,8,1024]{2,1,0:T(8,128)S(1)}, f32[5,8,1024]{2,1,0:T(8,128)S(1)}, u32[]{:S(2)}, u32[]{:S(2)}) collective-permute-start(f32[5,8,1024]{2,1,0:T(8,128)S(1)} %get-tuple-element.19), channel_id=1, source_target_pairs={{0,1},{1,2},{2,3},{3,4},{4,5},{5,6},{6,7},{8,9},{9,10},{10,11},{11... | collective-permute-start | bytes 491528 | tf_op jit(solution)/shard_map/ppermute | solution.py:466
  8.6 6.5 %copy-start = (bf16[512,512]{1,0:T(8,128)(2,1)S(1)}, bf16[512,512]{1,0:T(8,128)(2,1)}, u32[]{:S(2)}) copy-start(bf16[512,512]{1,0:T(8,128)(2,1)} %constant.19.clone.even_h) | copy-start | bytes 1572868
  8.6 6.5 %copy-start.1 = (bf16[512,512]{1,0:T(8,128)(2,1)S(1)}, bf16[512,512]{1,0:T(8,128)(2,1)}, u32[]{:S(2)}) copy-start(bf16[512,512]{1,0:T(8,128)(2,1)} %constant.20.clone.even_t) | copy-start | bytes 1572868
  8.7 6.5 %copy-start.2 = (bf16[512,512]{1,0:T(8,128)(2,1)S(1)}, bf16[512,512]{1,0:T(8,128)(2,1)}, u32[]{:S(2)}) copy-start(bf16[512,512]{1,0:T(8,128)(2,1)} %constant.21.clone.odd_h) | copy-start | bytes 1572868
  8.7 6.5 %copy-start.3 = (bf16[512,512]{1,0:T(8,128)(2,1)S(1)}, bf16[512,512]{1,0:T(8,128)(2,1)}, u32[]{:S(2)}) copy-start(bf16[512,512]{1,0:T(8,128)(2,1)} %constant.22.clone.odd_t) | copy-start | bytes 1572868
  8.7 6.5 %collective-permute-start.3 = (f32[5,8,1024]{2,1,0:T(8,128)S(1)}, f32[5,8,1024]{2,1,0:T(8,128)S(1)}, u32[]{:S(2)}, u32[]{:S(2)}) collective-permute-start(f32[5,8,1024]{2,1,0:T(8,128)S(1)} %get-tuple-element.20), channel_id=1, source_target_pairs={{1,0},{2,1},{3,2},{4,3},{5,4},{6,5},{7,6},{9,8},{10,9},{11,10},{12... | collective-permute-start | bytes 491528 | tf_op jit(solution)/shard_map/ppermute | solution.py:466
  17.6 22.1 %all-to-all-start = ((f32[32,40,128]{2,1,0:T(8,128)}), f32[32,40,128]{2,1,0:T(8,128)S(1)}, u32[]{:S(2)}, u32[]{:S(2)}) async-start(f32[32,40,128]{2,1,0:T(8,128)} %get-tuple-element.21), calls=%async_computation | async-start | bytes 1310720 | tf_op jit(solution)/shard_map/all_to_all | solution.py:470

commit v4 on v3

--- a/solution.py
+++ b/solution.py
@@ -17,7 +17,6 @@
 QUADS = LAYERS // 4
 PIECE = 8 * (QUADS + 1)
 VMEM = pl.BlockSpec(memory_space=pltpu.VMEM)
-SMEM = pl.BlockSpec(memory_space=pltpu.SMEM)
 HBM = pl.BlockSpec(memory_space=pltpu.HBM)
 
 
@@ -104,8 +103,12 @@
     return copies
 
 
-def sides_kernel(motion_hbm, thermal_hbm, base_hbm, y_first, y_last, z_first, z_last, motion, thermal, base, sems):
-    fetched = start_copies(((base_hbm, base), (thermal_hbm, thermal), (motion_hbm, motion)), sems)
+def sides_kernel(
+    motion_hbm, thermal_hbm, flow_hbm, base_hbm,
+    y_first, y_last, z_first, z_last, motion, thermal, flow, base, sems,
+):
+    pairs = ((base_hbm, base), (thermal_hbm, thermal), (motion_hbm, motion), (flow_hbm, flow))
+    fetched = start_copies(pairs, sems)
     fetched[0].wait()
     for y in range(ROWS):
         warm = base[y].astype(F32)
@@ -126,15 +129,10 @@
         for y in range(ROWS):
             z_first[c, y:y + 1, :] = motion[c, y, :1, :]
             z_last[c, y:y + 1, :] = motion[c, y, LAYERS - 1:, :]
-
-
-def inner_kernel(
-    motion_hbm, thermal_hbm, flow_hbm, base_hbm, moved, row_factors, layer_factors,
-    motion, thermal, flow, base, sems,
-):
-    pairs = ((thermal_hbm, thermal), (base_hbm, base), (flow_hbm, flow), (motion_hbm, motion))
-    for copy in start_copies(pairs, sems):
-        copy.wait()
+    fetched[3].wait()
+
+
+def inner_kernel(motion, thermal, flow, base, moved, row_factors, layer_factors):
     size_x = motion.shape[-1]
     row = lax.broadcasted_iota(jnp.int32, (LAYERS, size_x), 0)
     top = row == LAYERS - 1
@@ -187,8 +185,8 @@
 
 def source_kernel(
     moved, row_factors, layer_factors, y_low, y_high, z_low, z_high, even_h, even_t, odd_h, odd_t,
-    provisional_hbm, thermal_hbm, message_hbm,
-    provisional, message, source, lines, row_p, layer_p, sems,
+    provisional_hbm, thermal_hbm, message,
+    provisional, source, lines, row_p, layer_p, sems,
 ):
     size_x = moved.shape[-1]
     row = lax.broadcasted_iota(jnp.int32, (8, size_x), 0)
@@ -244,10 +242,6 @@
             a = [waves[j * PIECE:(j + 1) * PIECE, block * 128:(block + 1) * 128] for j in range(4)]
             for i, piece in enumerate(swap_groups(a)):
                 message[4 * (turn * half + block) + i] = piece
-        part = pl.ds(turn * 4 * half, 4 * half)
-        copy = pltpu.make_async_copy(message.at[part], message_hbm.at[part], sems.at[2 + turn])
-        copy.start()
-        stored.append(copy)
     for copy in stored:
         copy.wait()
 
@@ -283,13 +277,12 @@
     return floor, ceiling, powers
 
 
-def down_kernel(place, received, table_hbm, spectral, handed, table, sems):
-    fetched = start_copies(((table_hbm, table),), sems)
+def down_kernel(received, table, spectral, handed):
     sources = received.shape[0]
     size_y = sources * ROWS
     slabs = handed.shape[0]
     size_x = sources * WAVES
-    slab = place[1]
+    slab = lax.axis_index("gz")
     row = lax.broadcasted_iota(jnp.int32, (sources, 8, 128), 1)
     group = lane_group((sources, 8, 128))
     extra = received[:, 8 * QUADS:, :]
@@ -304,7 +297,6 @@
     layer = jnp.where(row < 4, first, second)
     layer = jnp.where((row % 4 == group) & (slab > 0), layer, 0.0)
     columns.append(layer.reshape(size_y, 128))
-    fetched[0].wait()
     waves = span_product(table, jnp.concatenate(columns, 1))
 
     last = waves[:, 128 * QUADS:]
@@ -325,7 +317,7 @@
         layers += swap_groups([block[:, i].reshape(modes, 128) for i in range(4)])
     modes = size_y // 4
     line_y = table[pl.ds(2 * size_y, modes), :]
-    a = table[pl.ds(2 * size_y + modes + place[0], 1), :] + line_y
+    a = table[pl.ds(2 * size_y + modes + lax.axis_index("gy"), 1), :] + line_y
     sinh = jnp.sqrt(a * (1.0 + 0.25 * a))
     lam = 1.0 / (1.0 + 0.5 * a + sinh)
     floor, ceiling, powers = wall_factors(lam, slab, slabs)
@@ -347,14 +339,13 @@
         handed[d] = jnp.where(d > slab, upward, downward)
 
 
-def up_kernel(place, spectral, handed, table_hbm, message_hbm, table, message, sems):
-    fetched = start_copies(((table_hbm, table),), sems)
+def up_kernel(spectral, handed, table, message):
     sources = message.shape[0]
     size_y = sources * ROWS
     slabs = handed.shape[0]
     size_x = sources * WAVES
     size_z = slabs * LAYERS
-    slab = place[1]
+    slab = lax.axis_index("gz")
     lam = spectral[LAYERS + 1]
     weight = spectral[LAYERS + 2]
     floor, ceiling, powers = wall_factors(lam, slab, slabs)
@@ -399,7 +390,6 @@
         part = part + pltpu.roll(part, 64, 1)
         spread.append((part + pltpu.roll(part, 32, 1)).reshape(tall))
     columns.append(jnp.concatenate(spread, 1).reshape(size_y, 128))
-    fetched[0].wait()
     values = span_product(table, jnp.concatenate(columns, 1))
 
     row = lax.broadcasted_iota(jnp.int32, (sources, 8, 128), 1)
@@ -417,13 +407,10 @@
     extra = jnp.where(row == 4, jnp.broadcast_to(layer[:, 0:1, :], extra.shape), extra)
     extra = jnp.where(row == 5, jnp.broadcast_to(layer[:, 4:5, :], extra.shape), extra)
     message[:, 8 * QUADS:, :] = extra
-    copy = pltpu.make_async_copy(message, message_hbm, sems.at[1])
-    copy.start()
-    copy.wait()
 
 
 def gradient_kernel(
-    place, received, even_h, even_t, odd_h, odd_t, provisional_hbm, motion_hbm,
+    received, even_h, even_t, odd_h, odd_t, provisional_hbm, motion_hbm,
     provisional, motion, lines, pressure, row_p, layer_p, sems,
 ):
     fetched = start_copies(((provisional_hbm, provisional),), sems)
@@ -449,7 +436,7 @@
         p = kept(pressure, y * LAYERS, LAYERS)
         before = kept(row_p, 0, LAYERS) if y == 0 else kept(pressure, (y - 1) * LAYERS, LAYERS)
         below = jnp.where(bottom, kept(layer_p, y, 1), pltpu.roll(p, 1, 0))
-        slope_z = jnp.where(bottom & (place[1] == 0), 0.0, p - below)
+        slope_z = jnp.where(bottom & (lax.axis_index("gz") == 0), 0.0, p - below)
         motion[0, y] = provisional[0, y] - (p - pltpu.roll(p, 1, 1))
         motion[1, y] = provisional[1, y] - (p - before)
         motion[2, y] = provisional[2, y] - slope_z
@@ -481,10 +468,8 @@
     even, odd, table = tables(size_x, ROWS * groups_y)
     even_h, even_t = map(jnp.asarray, even)
     odd_h, odd_t = map(jnp.asarray, odd)
-    size_t = table.shape[0]
     modes = ROWS * groups_y // 4
     blocks = size_x // 128
-    place = jnp.stack([lax.axis_index("gy"), lax.axis_index("gz")]).astype(jnp.int32)
 
     def hbm(value):
         return pltpu.with_memory_space_constraint(value, pltpu.HBM)
@@ -492,27 +477,22 @@
     def params(mib):
         return pltpu.CompilerParams(vmem_limit_bytes=mib << 20)
 
-    motion_in, thermal_in, flow_in, base_in = map(hbm, (dual_motion, dual_thermal, flow, base))
-    table = hbm(jnp.asarray(table))
+    table = jnp.asarray(table)
     rows = shape_of(5, LAYERS, size_x)
     layers = shape_of(5, ROWS, size_x)
     motion_shape = (3, ROWS, LAYERS, size_x)
     thermal_shape = motion_shape[1:]
     message_shape = (groups_y, PIECE, 128)
-    y_first, y_last, z_first, z_last = pl.pallas_call(
+    fields = tuple(jax.ShapeDtypeStruct(a.shape, a.dtype) for a in (dual_motion, dual_thermal, flow, base))
+    y_first, y_last, z_first, z_last, *fields = pl.pallas_call(
         sides_kernel,
-        out_shape=(rows, rows, layers, layers),
-        in_specs=[HBM] * 3,
-        out_specs=(VMEM,) * 4,
-        scratch_shapes=[
-            pltpu.VMEM(motion_shape, F32),
-            pltpu.VMEM(thermal_shape, F32),
-            pltpu.VMEM(thermal_shape, BF16),
-            pltpu.SemaphoreType.DMA((3,)),
-        ],
+        out_shape=(rows, rows, layers, layers, *fields),
+        in_specs=[HBM] * 4,
+        out_specs=(VMEM,) * 8,
+        scratch_shapes=[pltpu.SemaphoreType.DMA((4,))],
         compiler_params=params(16),
         name="sides",
-    )(motion_in, thermal_in, base_in)
+    )(*map(hbm, (dual_motion, dual_thermal, flow, base)))
     z_low = shifted(z_last, "gz", 1, False)
     z_high = shifted(z_first, "gz", -1, False)
     y_low = shifted(y_last, "gy", 1, True)
@@ -524,38 +504,30 @@
             shape_of(4, LAYERS, size_x),
             shape_of(4, ROWS, size_x),
         ),
-        in_specs=[HBM] * 4,
+        in_specs=[VMEM] * 4,
         out_specs=(VMEM,) * 3,
-        scratch_shapes=[
-            pltpu.VMEM(motion_shape, F32),
-            pltpu.VMEM(thermal_shape, F32),
-            pltpu.VMEM(motion_shape, BF16),
-            pltpu.VMEM(thermal_shape, BF16),
-            pltpu.SemaphoreType.DMA((4,)),
-        ],
         compiler_params=params(16),
         cost_estimate=pl.CostEstimate(
             flops=80 * ROWS * LAYERS * size_x, transcendentals=0, bytes_accessed=10 << 20
         ),
         name="inner",
-    )(motion_in, thermal_in, flow_in, base_in)
+    )(*fields)
     provisional, thermal_out, message = pl.pallas_call(
         source_kernel,
         out_shape=(
             pltpu.HBM(motion_shape, F32),
             pltpu.HBM(thermal_shape, F32),
-            pltpu.HBM(message_shape, F32),
+            shape_of(*message_shape),
         ),
         in_specs=[VMEM] * 11,
-        out_specs=(HBM,) * 3,
+        out_specs=(HBM, HBM, VMEM),
         scratch_shapes=[
             pltpu.VMEM((4, *thermal_shape), F32),
-            pltpu.VMEM(message_shape, F32),
             pltpu.VMEM((blocks, ROWS * LAYERS, 128), F32),
             pltpu.VMEM((4 * PIECE, size_x), F32),
             pltpu.VMEM((blocks, LAYERS, 128), F32),
             pltpu.VMEM((blocks, ROWS, 128), F32),
-            pltpu.SemaphoreType.DMA((4,)),
+            pltpu.SemaphoreType.DMA((2,)),
         ],
         compiler_params=params(24),
         name="source",
@@ -564,31 +536,25 @@
     spectral, handed = pl.pallas_call(
         down_kernel,
         out_shape=(shape_of(LAYERS + 3, modes, 128), shape_of(groups_z, modes, 128)),
-        in_specs=[SMEM, VMEM, HBM],
+        in_specs=[VMEM] * 2,
         out_specs=(VMEM,) * 2,
-        scratch_shapes=[pltpu.VMEM((size_t, 128), F32), pltpu.SemaphoreType.DMA((1,))],
         compiler_params=params(16),
         name="down",
-    )(place, received, table)
+    )(received, table)
     handed = exchanged(handed, "gz")
     message = pl.pallas_call(
         up_kernel,
-        out_shape=pltpu.HBM(message_shape, F32),
-        in_specs=[SMEM, VMEM, VMEM, HBM],
-        out_specs=HBM,
-        scratch_shapes=[
-            pltpu.VMEM((size_t, 128), F32),
-            pltpu.VMEM(message_shape, F32),
-            pltpu.SemaphoreType.DMA((2,)),
-        ],
+        out_shape=shape_of(*message_shape),
+        in_specs=[VMEM] * 3,
+        out_specs=VMEM,
         compiler_params=params(16),
         name="up",
-    )(place, spectral, handed, table)
+    )(spectral, handed, table)
     received = exchanged(message, "gy")
     motion = pl.pallas_call(
         gradient_kernel,
         out_shape=pltpu.HBM(motion_shape, F32),
-        in_specs=[SMEM] + [VMEM] * 5 + [HBM],
+        in_specs=[VMEM] * 5 + [HBM],
         out_specs=HBM,
         scratch_shapes=[
             pltpu.VMEM(motion_shape, F32),
@@ -601,7 +567,7 @@
         ],
         compiler_params=params(24),
         name="gradient",
-    )(place, received, even_h, even_t, odd_h, odd_t, hbm(provisional))
+    )(received, even_h, even_t, odd_h, odd_t, hbm(provisional))
     return motion, thermal_out
 
 

time: 87.6 us -> 81.7 us (0.933)
  blocking collectives: 37.5 us -> 58.5 us
  waiting for transfers between devices: 13.5 us -> 2.71 us
  starting transfers between devices: 16.8 us -> 7.51 us
  Pallas kernels: 18.4 us -> 11.9 us
    all_to_all x2 -> x3, blocking collectives: 37.5 us -> 58.5 us  [exchanged(): return lax.all_to_all(pieces, axis, split_axis=0, concat_axis=0, tiled=True)]
    all_to_all x1 -> x0, waiting for transfers between devices: 12.8 us -> none  [exchanged(): return lax.all_to_all(pieces, axis, split_axis=0, concat_axis=0, tiled=True)]
    all_to_all x1 -> x0, starting transfers between devices: 9.16 us -> none  [exchanged(): return lax.all_to_all(pieces, axis, split_axis=0, concat_axis=0, tiled=True)]
    pallas_call x2, Pallas kernels: 5.28 us -> 3 us  [the longest x1 1.89 us: on_device(): pl.pallas_call(sides_kernel, out_shape=(rows, rows, layers, layers, *fiel...]
    ppermute x4, waiting for transfers between devices: 0.72 us -> 2.71 us  [shifted(): return lax.ppermute(value, axis, pairs)]
    pallas_call x1, Pallas kernels: 4.3 us -> 2.45 us  [on_device(): pl.pallas_call(inner_kernel, out_shape=(shape_of(4, *thermal_shape), shap...]
    pallas_call x1, Pallas kernels: 2.39 us -> 0.88 us  [on_device(): pl.pallas_call(down_kernel, out_shape=(shape_of(LAYERS + 3, modes, 128),...]
  transfers between devices with their start and end apart: 5 -> 4, of which waited for: 2 -> 1; matrix products, arithmetic and copies ran while one was open for 0% -> 0% of each run, Pallas kernels for 5% -> 3%
where the time goes in v4:
time: 81.7 us; the launch traced here: 81.4 us
  blocking collectives  58.5 us (72%)
  Pallas kernels  11.9 us (15%)
  starting transfers between devices  7.51 us (9%)
  waiting for transfers between devices  2.71 us (3%)
    all_to_all x3, blocking collectives, exchanged(): return lax.all_to_all(pieces, axis, split_axis=0, concat_axis=0, tiled=True)  58.5 us
    ppermute x4, starting transfers between devices, shifted(): return lax.ppermute(value, axis, pairs)  7.51 us
    pallas_call x1, Pallas kernels, on_device(): pl.pallas_call(gradient_kernel, out_shape=pltpu.HBM(motion_shape, F32), i...  3.47 us
    ppermute x4, waiting for transfers between devices, shifted(): return lax.ppermute(value, axis, pairs)  2.71 us
    pallas_call x1, Pallas kernels, on_device(): pl.pallas_call(inner_kernel, out_shape=(shape_of(4, *thermal_shape), shap...  2.45 us
    pallas_call x1, Pallas kernels, on_device(): pl.pallas_call(source_kernel, out_shape=(pltpu.HBM(motion_shape, F32), pl...  2.09 us
    pallas_call x1, Pallas kernels, on_device(): pl.pallas_call(sides_kernel, out_shape=(rows, rows, layers, layers, *fiel...  1.89 us
  transfers between devices with their start and end apart: 4, of which 1 were waited for; matrix products, arithmetic and copies ran while one was open for 0% of the time, Pallas kernels for 3%

profile of v4, /device:TPU:1, one launch (start us, length us, event | category | flops | bytes accessed | tf_op | source)
XLA Modules:
  0.0 81.4 jit_solution(7504327869912391327)
XLA Ops:
  0.6 1.9 %sides.1 = (f32[5,16,1024]{2,1,0:T(8,128)S(1)}, f32[5,16,1024]{2,1,0:T(8,128)S(1)}, f32[5,8,1024]{2,1,0:T(8,128)S(1)}, f32[5,8,1024]{2,1,0:T(8,128)S(1)}, f32[3,...) custom-call(f32[3,8,16,1024]{3,2,1,0:T(8,128)} %motion_hbm.1, ...), custom_call_target="tpu_custom_call" | custom-call | tf_op jit(solution)/shard_map/sides/pallas_call | solution.py:487
  2.5 2.7 %collective-permute-start = (f32[5,16,1024]{2,1,0:T(8,128)S(1)}, f32[5,16,1024]{2,1,0:T(8,128)S(1)}, u32[]{:S(2)}, u32[]{:S(2)}) collective-permute-start(f32[5,16,1024]{2,1,0:T(8,128)S(1)} %get-tuple-element.25), channel_id=1, source_target_pairs={{0,8},{8,16},{16,24},{24,32},{32,40},{40,48},{48,56},{56,64},{64,7... | collective-permute-start | bytes 983048 | tf_op jit(solution)/shard_map/ppermute | solution.py:453
  5.2 0.7 collective-permute-start.1
  5.9 2.8 %collective-permute-start.2 = (f32[5,8,1024]{2,1,0:T(8,128)S(1)}, f32[5,8,1024]{2,1,0:T(8,128)S(1)}, u32[]{:S(2)}, u32[]{:S(2)}) collective-permute-start(f32[5,8,1024]{2,1,0:T(8,128)S(1)} %get-tuple-element.27), channel_id=1, source_target_pairs={{0,1},{1,2},{2,3},{3,4},{4,5},{5,6},{6,7},{8,9},{9,10},{10,11},{11... | collective-permute-start | bytes 491528 | tf_op jit(solution)/shard_map/ppermute | solution.py:453
  8.8 1.3 %collective-permute-start.3 = (f32[5,8,1024]{2,1,0:T(8,128)S(1)}, f32[5,8,1024]{2,1,0:T(8,128)S(1)}, u32[]{:S(2)}, u32[]{:S(2)}) collective-permute-start(f32[5,8,1024]{2,1,0:T(8,128)S(1)} %get-tuple-element.28), channel_id=1, source_target_pairs={{1,0},{2,1},{3,2},{4,3},{5,4},{6,5},{7,6},{9,8},{10,9},{11,10},{12... | collective-permute-start | bytes 491528 | tf_op jit(solution)/shard_map/ppermute | solution.py:453
  10.1 0.0 copy-start
  10.1 0.0 copy-start.1
  10.1 0.0 copy-start.2
  10.1 0.0 copy-start.3
  10.1 2.4 %inner.1 = (f32[4,8,16,1024]{3,2,1,0:T(8,128)S(1)}, f32[4,16,1024]{2,1,0:T(8,128)S(1)}, f32[4,8,1024]{2,1,0:T(8,128)S(1)}) custom-call(f32[3,8,16,1024]{3,2,1,0:T(8,128)S(1)} %get-tuple-element.18.motion, f32[8,16,1024]{2,1,0:T(8,128)S(1)} %get-tuple-element.19.thermal, bf16[3,8,16,1024]{3,2,1,0:T(8,128)(2,1)S(1)} %get-tuple-element.20.flow, ...), custom_call_target="tpu_custom_call" | custom-call | flops 10485760 | bytes 10485760 | tf_op jit(solution)/shard_map/inner/pallas_call | solution.py:500
  12.6 0.0 collective-permute-done.2.z_low
  12.6 2.7 %collective-permute-done.3.z_high = f32[5,8,1024]{2,1,0:T(8,128)S(1)} collective-permute-done((f32[5,8,1024]{2,1,0:T(8,128)S(1)}, f32[5,8,1024]{2,1,0:T(8,128)S(1)}, u32[]{:S(2)}, u32[]{:S(2)}) %collective-permute-start.3) | collective-permute-done | bytes 163872 | tf_op jit(solution)/shard_map/ppermute | solution.py:453
  15.3 0.0 collective-permute-done.y_low
  15.3 0.0 collective-permute-done.1.y_high
  15.3 0.0 copy-done
  15.3 0.0 copy-done.1
  15.3 0.0 copy-done.2
  15.3 0.0 copy-done.3
  15.3 0.0 copy-start.4
  15.3 2.1 %source.1 = (f32[3,8,16,1024]{3,2,1,0:T(8,128)}, f32[8,16,1024]{2,1,0:T(8,128)}, f32[32,40,128]{2,1,0:T(8,128)S(1)}) custom-call(f32[4,8,16,1024]{3,2,1,0:T(8,128)S(1)} %get-tuple-element.22.moved, f32[4,16,1024]{2,1,0:T(8,128)S(1)} %get-tuple-element.23.row_factors, f32[4,8,1024]{2,1,0:T(8,128)S(1)} %get-tuple-element.24.layer_factors, ...), custom_call_target="tpu_custom_call" | custom-call | tf_op jit(solution)/shard_map/source/pallas_call | solution.py:515
  17.4 21.7 %all_to_all.15.received = f32[32,40,128]{2,1,0:T(8,128)S(1)} all-to-all(f32[32,40,128]{2,1,0:T(8,128)S(1)} %get-tuple-element.29), channel_id=1, replica_groups=mesh['gy'=32,'gz'=8] {'gy'}, dimensions={0} | all-to-all | bytes 1310720 | tf_op jit(solution)/shard_map/all_to_all | solution.py:457
  39.1 0.0 copy-done.4
  39.1 0.9 %down.1 = (f32[19,64,128]{2,1,0:T(8,128)S(1)}, f32[8,64,128]{2,1,0:T(8,128)S(1)}) custom-call(f32[32,40,128]{2,1,0:T(8,128)S(1)} %all_to_all.15.received, f32[608,128]{1,0:T(8,128)S(1)} %copy-done.4), custom_call_target="tpu_custom_call" | custom-call | tf_op jit(solution)/shard_map/down/pallas_call | solution.py:536
  40.0 18.3 %all_to_all.16.handed = f32[8,64,128]{2,1,0:T(8,128)S(1)} all-to-all(f32[8,64,128]{2,1,0:T(8,128)S(1)} %get-tuple-element.31), channel_id=1, replica_groups=mesh['gy'=32,'gz'=8] {'gz'}, dimensions={0} | all-to-all | bytes 524288 | tf_op jit(solution)/shard_map/all_to_all | solution.py:457
  58.3 1.1 %up.1 = f32[32,40,128]{2,1,0:T(8,128)S(1)} custom-call(f32[19,64,128]{2,1,0:T(8,128)S(1)} %get-tuple-element.30.spectral, f32[8,64,128]{2,1,0:T(8,128)S(1)} %all_to_all.16.handed, f32[608,128]{1,0:T(8,128)S(1)} %copy-done.4), custom_call_target="tpu_custom_call" | custom-call | tf_op jit(solution)/shard_map/up/pallas_call | solution.py:545
  59.4 18.6 %all_to_all.17.received = f32[32,40,128]{2,1,0:T(8,128)S(1)} all-to-all(f32[32,40,128]{2,1,0:T(8,128)S(1)} %up.1), channel_id=1, replica_groups=mesh['gy'=32,'gz'=8] {'gy'}, dimensions={0} | all-to-all | bytes 1310720 | tf_op jit(solution)/shard_map/all_to_all | solution.py:457
  78.0 3.5 %gradient.1 = f32[3,8,16,1024]{3,2,1,0:T(8,128)} custom-call(f32[32,40,128]{2,1,0:T(8,128)S(1)} %all_to_all.17.received, bf16[512,512]{1,0:T(8,128)(2,1)S(1)} %copy-done.3, bf16[512,512]{1,0:T(8,128)(2,1)S(1)} %copy-done.2, bf16[512,512]{1,0:T(8,128)(2,1)S(1)} %copy-done.1, bf16[512,512]{1,0:T(8,128)(2,1)S(1)} %copy-done, ...), custom_call_target="tpu_custom_call" | custom-call | tf_op jit(solution)/shard_map/gradient/pallas_call | solution.py:554
Async XLA Ops:
  2.5 12.7 %collective-permute-start = (f32[5,16,1024]{2,1,0:T(8,128)S(1)}, f32[5,16,1024]{2,1,0:T(8,128)S(1)}, u32[]{:S(2)}, u32[]{:S(2)}) collective-permute-start(f32[5,16,1024]{2,1,0:T(8,128)S(1)} %get-tuple-element.25), channel_id=1, source_target_pairs={{0,8},{8,16},{16,24},{24,32},{32,40},{40,48},{48,56},{56,64},{64,7... | collective-permute-start | bytes 983048 | tf_op jit(solution)/shard_map/ppermute | solution.py:453
  5.2 10.1 %collective-permute-start.1 = (f32[5,16,1024]{2,1,0:T(8,128)S(1)}, f32[5,16,1024]{2,1,0:T(8,128)S(1)}, u32[]{:S(2)}, u32[]{:S(2)}) collective-permute-start(f32[5,16,1024]{2,1,0:T(8,128)S(1)} %get-tuple-element.26), channel_id=1, source_target_pairs={{0,248},{8,0},{16,8},{24,16},{32,24},{40,32},{48,40},{56,48},{64,5... | collective-permute-start | bytes 983048 | tf_op jit(solution)/shard_map/ppermute | solution.py:453
  5.9 6.6 %collective-permute-start.2 = (f32[5,8,1024]{2,1,0:T(8,128)S(1)}, f32[5,8,1024]{2,1,0:T(8,128)S(1)}, u32[]{:S(2)}, u32[]{:S(2)}) collective-permute-start(f32[5,8,1024]{2,1,0:T(8,128)S(1)} %get-tuple-element.27), channel_id=1, source_target_pairs={{0,1},{1,2},{2,3},{3,4},{4,5},{5,6},{6,7},{8,9},{9,10},{10,11},{11... | collective-permute-start | bytes 491528 | tf_op jit(solution)/shard_map/ppermute | solution.py:453
  8.8 6.5 %collective-permute-start.3 = (f32[5,8,1024]{2,1,0:T(8,128)S(1)}, f32[5,8,1024]{2,1,0:T(8,128)S(1)}, u32[]{:S(2)}, u32[]{:S(2)}) collective-permute-start(f32[5,8,1024]{2,1,0:T(8,128)S(1)} %get-tuple-element.28), channel_id=1, source_target_pairs={{1,0},{2,1},{3,2},{4,3},{5,4},{6,5},{7,6},{9,8},{10,9},{11,10},{12... | collective-permute-start | bytes 491528 | tf_op jit(solution)/shard_map/ppermute | solution.py:453
  10.1 5.2 %copy-start = (bf16[512,512]{1,0:T(8,128)(2,1)S(1)}, bf16[512,512]{1,0:T(8,128)(2,1)}, u32[]{:S(2)}) copy-start(bf16[512,512]{1,0:T(8,128)(2,1)} %constant.13.clone.odd_t) | copy-start | bytes 1572868
  10.1 5.2 %copy-start.1 = (bf16[512,512]{1,0:T(8,128)(2,1)S(1)}, bf16[512,512]{1,0:T(8,128)(2,1)}, u32[]{:S(2)}) copy-start(bf16[512,512]{1,0:T(8,128)(2,1)} %constant.12.clone.odd_h) | copy-start | bytes 1572868
  10.1 5.2 %copy-start.2 = (bf16[512,512]{1,0:T(8,128)(2,1)S(1)}, bf16[512,512]{1,0:T(8,128)(2,1)}, u32[]{:S(2)}) copy-start(bf16[512,512]{1,0:T(8,128)(2,1)} %constant.11.clone.even_t) | copy-start | bytes 1572868
  10.1 5.2 %copy-start.3 = (bf16[512,512]{1,0:T(8,128)(2,1)S(1)}, bf16[512,512]{1,0:T(8,128)(2,1)}, u32[]{:S(2)}) copy-start(bf16[512,512]{1,0:T(8,128)(2,1)} %constant.10.clone.even_h) | copy-start | bytes 1572868
  15.3 23.8 %copy-start.4 = (f32[608,128]{1,0:T(8,128)S(1)}, f32[608,128]{1,0:T(8,128)}, u32[]{:S(2)}) copy-start(f32[608,128]{1,0:T(8,128)} %constant.14.clone.table) | copy-start | bytes 933892

commit v5 on v4

--- a/solution.py
+++ b/solution.py
@@ -104,10 +104,9 @@
 
 
 def sides_kernel(
-    motion_hbm, thermal_hbm, flow_hbm, base_hbm,
-    y_first, y_last, z_first, z_last, motion, thermal, flow, base, sems,
+    motion_hbm, thermal_hbm, base_hbm, y_first, y_last, z_first, z_last, motion, thermal, base, sems
 ):
-    pairs = ((base_hbm, base), (thermal_hbm, thermal), (motion_hbm, motion), (flow_hbm, flow))
+    pairs = ((base_hbm, base), (thermal_hbm, thermal), (motion_hbm, motion))
     fetched = start_copies(pairs, sems)
     fetched[0].wait()
     for y in range(ROWS):
@@ -129,7 +128,6 @@
         for y in range(ROWS):
             z_first[c, y:y + 1, :] = motion[c, y, :1, :]
             z_last[c, y:y + 1, :] = motion[c, y, LAYERS - 1:, :]
-    fetched[3].wait()
 
 
 def inner_kernel(motion, thermal, flow, base, moved, row_factors, layer_factors):
@@ -185,8 +183,7 @@
 
 def source_kernel(
     moved, row_factors, layer_factors, y_low, y_high, z_low, z_high, even_h, even_t, odd_h, odd_t,
-    provisional_hbm, thermal_hbm, message,
-    provisional, source, lines, row_p, layer_p, sems,
+    provisional, thermal_hbm, message, thermal, source, lines, row_p, layer_p, sems
 ):
     size_x = moved.shape[-1]
     row = lax.broadcasted_iota(jnp.int32, (8, size_x), 0)
@@ -207,8 +204,9 @@
                 value = value + row_factors[2] * y_high[c]
                 if c == 1:
                     value = value + row_factors[3] * y_high[4]
-            provisional[c, y, :8] = value[:8] + jnp.where(row == 0, lows[c][y:y + 1], 0.0)
-            provisional[c, y, 8:] = value[8:] + jnp.where(row == 7, highs[c][y:y + 1], 0.0)
+            out = provisional.at[c, y] if c < 3 else thermal.at[y]
+            out[:8] = value[:8] + jnp.where(row == 0, lows[c][y:y + 1], 0.0)
+            out[8:] = value[8:] + jnp.where(row == 7, highs[c][y:y + 1], 0.0)
         p0, p1, p2 = (provisional[c, y] for c in range(3))
         if y == 0:
             keep(row_p, 0, p1)
@@ -218,9 +216,7 @@
         above = jnp.where(top, 0.0, pltpu.roll(p2, LAYERS - 1, 0))
         carried = (pltpu.roll(p0, size_x - 1, 1) - p0) - p1 + (above - p2)
     keep(source, (ROWS - 1) * LAYERS, carried)
-    stored = start_copies(
-        ((provisional.at[pl.ds(0, 3)], provisional_hbm), (provisional.at[3], thermal_hbm)), sems
-    )
+    stored = start_copies(((thermal, thermal_hbm),), sems)
 
     for b in range(size_x // 128):
         lanes = pl.ds(b * 128, 128)
@@ -410,10 +406,9 @@
 
 
 def gradient_kernel(
-    received, even_h, even_t, odd_h, odd_t, provisional_hbm, motion_hbm,
-    provisional, motion, lines, pressure, row_p, layer_p, sems,
+    received, even_h, even_t, odd_h, odd_t, provisional, motion_hbm,
+    motion, lines, pressure, row_p, layer_p, sems,
 ):
-    fetched = start_copies(((provisional_hbm, provisional),), sems)
     size_x = provisional.shape[-1]
     for block in range(size_x // 128):
         for j, piece in enumerate(swap_groups([received[4 * block + i] for i in range(4)])):
@@ -429,7 +424,6 @@
                 pressure[b, pl.ds(4 * q + j, ROWS, stride=LAYERS), :] = lines[pl.ds(j * PIECE + q * 8, 8), lanes]
             row_p[b, pl.ds(j, 4, stride=4), :] = lines[pl.ds(j * PIECE + 32, 4), lanes]
             layer_p[b, pl.ds(j, 2, stride=4), :] = lines[pl.ds(j * PIECE + 36, 2), lanes]
-    fetched[0].wait()
     stored = []
     bottom = lax.broadcasted_iota(jnp.int32, (LAYERS, size_x), 0) == 0
     for y in range(ROWS):
@@ -440,7 +434,7 @@
         motion[0, y] = provisional[0, y] - (p - pltpu.roll(p, 1, 1))
         motion[1, y] = provisional[1, y] - (p - before)
         motion[2, y] = provisional[2, y] - slope_z
-        copy = pltpu.make_async_copy(motion.at[:, pl.ds(y, 1)], motion_hbm.at[:, pl.ds(y, 1)], sems.at[1 + y])
+        copy = pltpu.make_async_copy(motion.at[:, pl.ds(y, 1)], motion_hbm.at[:, pl.ds(y, 1)], sems.at[y])
         copy.start()
         stored.append(copy)
     for copy in stored:
@@ -483,16 +477,16 @@
     motion_shape = (3, ROWS, LAYERS, size_x)
     thermal_shape = motion_shape[1:]
     message_shape = (groups_y, PIECE, 128)
-    fields = tuple(jax.ShapeDtypeStruct(a.shape, a.dtype) for a in (dual_motion, dual_thermal, flow, base))
-    y_first, y_last, z_first, z_last, *fields = pl.pallas_call(
+    fields = tuple(jax.ShapeDtypeStruct(a.shape, a.dtype) for a in (dual_motion, dual_thermal, base))
+    y_first, y_last, z_first, z_last, motion, thermal, base = pl.pallas_call(
         sides_kernel,
         out_shape=(rows, rows, layers, layers, *fields),
-        in_specs=[HBM] * 4,
-        out_specs=(VMEM,) * 8,
-        scratch_shapes=[pltpu.SemaphoreType.DMA((4,))],
+        in_specs=[HBM] * 3,
+        out_specs=(VMEM,) * 7,
+        scratch_shapes=[pltpu.SemaphoreType.DMA((3,))],
         compiler_params=params(16),
         name="sides",
-    )(*map(hbm, (dual_motion, dual_thermal, flow, base)))
+    )(*map(hbm, (dual_motion, dual_thermal, base)))
     z_low = shifted(z_last, "gz", 1, False)
     z_high = shifted(z_first, "gz", -1, False)
     y_low = shifted(y_last, "gy", 1, True)
@@ -511,23 +505,23 @@
             flops=80 * ROWS * LAYERS * size_x, transcendentals=0, bytes_accessed=10 << 20
         ),
         name="inner",
-    )(*fields)
+    )(motion, thermal, flow, base)
     provisional, thermal_out, message = pl.pallas_call(
         source_kernel,
         out_shape=(
-            pltpu.HBM(motion_shape, F32),
+            shape_of(*motion_shape),
             pltpu.HBM(thermal_shape, F32),
             shape_of(*message_shape),
         ),
         in_specs=[VMEM] * 11,
-        out_specs=(HBM, HBM, VMEM),
+        out_specs=(VMEM, HBM, VMEM),
         scratch_shapes=[
-            pltpu.VMEM((4, *thermal_shape), F32),
+            pltpu.VMEM(thermal_shape, F32),
             pltpu.VMEM((blocks, ROWS * LAYERS, 128), F32),
             pltpu.VMEM((4 * PIECE, size_x), F32),
             pltpu.VMEM((blocks, LAYERS, 128), F32),
             pltpu.VMEM((blocks, ROWS, 128), F32),
-            pltpu.SemaphoreType.DMA((2,)),
+            pltpu.SemaphoreType.DMA((1,)),
         ],
         compiler_params=params(24),
         name="source",
@@ -554,20 +548,19 @@
     motion = pl.pallas_call(
         gradient_kernel,
         out_shape=pltpu.HBM(motion_shape, F32),
-        in_specs=[VMEM] * 5 + [HBM],
+        in_specs=[VMEM] * 6,
         out_specs=HBM,
         scratch_shapes=[
-            pltpu.VMEM(motion_shape, F32),
             pltpu.VMEM(motion_shape, F32),
             pltpu.VMEM((4 * PIECE, size_x), F32),
             pltpu.VMEM((blocks, ROWS * LAYERS, 128), F32),
             pltpu.VMEM((blocks, LAYERS, 128), F32),
             pltpu.VMEM((blocks, ROWS, 128), F32),
-            pltpu.SemaphoreType.DMA((1 + ROWS,)),
+            pltpu.SemaphoreType.DMA((ROWS,)),
         ],
         compiler_params=params(24),
         name="gradient",
-    )(received, even_h, even_t, odd_h, odd_t, hbm(provisional))
+    )(received, even_h, even_t, odd_h, odd_t, provisional)
     return motion, thermal_out
 
 

time: 81.7 us -> 80.4 us (0.984)
  Pallas kernels: 11.9 us -> 10.6 us
where the time goes in v5:
time: 80.4 us; the launch traced here: 80.2 us
  blocking collectives  58.5 us (73%)
  Pallas kernels  10.6 us (13%)
  starting transfers between devices  7.51 us (9%)
  waiting for transfers between devices  2.7 us (3%)
    all_to_all x3, blocking collectives, exchanged(): return lax.all_to_all(pieces, axis, split_axis=0, concat_axis=0, tiled=True)  58.5 us
    ppermute x4, starting transfers between devices, shifted(): return lax.ppermute(value, axis, pairs)  7.51 us
    pallas_call x1, Pallas kernels, on_device(): pl.pallas_call(gradient_kernel, out_shape=pltpu.HBM(motion_shape, F32), i...  2.74 us
    ppermute x4, waiting for transfers between devices, shifted(): return lax.ppermute(value, axis, pairs)  2.7 us
    pallas_call x1, Pallas kernels, on_device(): pl.pallas_call(inner_kernel, out_shape=(shape_of(4, *thermal_shape), shap...  2.45 us
    pallas_call x1, Pallas kernels, on_device(): pl.pallas_call(sides_kernel, out_shape=(rows, rows, layers, layers, *fiel...  1.82 us
    pallas_call x1, Pallas kernels, on_device(): pl.pallas_call(source_kernel, out_shape=(shape_of(*motion_shape), pltpu.H...  1.63 us
  transfers between devices with their start and end apart: 4, of which 1 were waited for; matrix products, arithmetic and copies ran while one was open for 0% of the time, Pallas kernels for 3%

profile of v5, /device:TPU:1, one launch (start us, length us, event | category | flops | bytes accessed | tf_op | source)
XLA Modules:
  0.0 80.2 jit_solution(12045843450323685509)
XLA Ops:
  0.6 0.0 copy-start.5
  0.6 1.8 %sides.1 = (f32[5,16,1024]{2,1,0:T(8,128)S(1)}, f32[5,16,1024]{2,1,0:T(8,128)S(1)}, f32[5,8,1024]{2,1,0:T(8,128)S(1)}, f32[5,8,1024]{2,1,0:T(8,128)S(1)}, f32[3,...) custom-call(f32[3,8,16,1024]{3,2,1,0:T(8,128)} %motion_hbm.1, ...), custom_call_target="tpu_custom_call" | custom-call | tf_op jit(solution)/shard_map/sides/pallas_call | solution.py:481
  2.5 2.7 %collective-permute-start = (f32[5,16,1024]{2,1,0:T(8,128)S(1)}, f32[5,16,1024]{2,1,0:T(8,128)S(1)}, u32[]{:S(2)}, u32[]{:S(2)}) collective-permute-start(f32[5,16,1024]{2,1,0:T(8,128)S(1)} %get-tuple-element.23), channel_id=1, source_target_pairs={{0,8},{8,16},{16,24},{24,32},{32,40},{40,48},{48,56},{56,64},{64,7... | collective-permute-start | bytes 983048 | tf_op jit(solution)/shard_map/ppermute | solution.py:447
  5.1 0.7 collective-permute-start.1
  5.9 2.8 %collective-permute-start.2 = (f32[5,8,1024]{2,1,0:T(8,128)S(1)}, f32[5,8,1024]{2,1,0:T(8,128)S(1)}, u32[]{:S(2)}, u32[]{:S(2)}) collective-permute-start(f32[5,8,1024]{2,1,0:T(8,128)S(1)} %get-tuple-element.25), channel_id=1, source_target_pairs={{0,1},{1,2},{2,3},{3,4},{4,5},{5,6},{6,7},{8,9},{9,10},{10,11},{11... | collective-permute-start | bytes 491528 | tf_op jit(solution)/shard_map/ppermute | solution.py:447
  8.7 1.3 %collective-permute-start.3 = (f32[5,8,1024]{2,1,0:T(8,128)S(1)}, f32[5,8,1024]{2,1,0:T(8,128)S(1)}, u32[]{:S(2)}, u32[]{:S(2)}) collective-permute-start(f32[5,8,1024]{2,1,0:T(8,128)S(1)} %get-tuple-element.26), channel_id=1, source_target_pairs={{1,0},{2,1},{3,2},{4,3},{5,4},{6,5},{7,6},{9,8},{10,9},{11,10},{12... | collective-permute-start | bytes 491528 | tf_op jit(solution)/shard_map/ppermute | solution.py:447
  10.0 0.0 copy-done.5
  10.0 0.0 copy-start
  10.0 0.0 copy-start.1
  10.0 0.0 copy-start.2
  10.0 0.0 copy-start.3
  10.1 2.4 %inner.1 = (f32[4,8,16,1024]{3,2,1,0:T(8,128)S(1)}, f32[4,16,1024]{2,1,0:T(8,128)S(1)}, f32[4,8,1024]{2,1,0:T(8,128)S(1)}) custom-call(f32[3,8,16,1024]{3,2,1,0:T(8,128)S(1)} %get-tuple-element.17.motion, f32[8,16,1024]{2,1,0:T(8,128)S(1)} %get-tuple-element.18.thermal, bf16[3,8,16,1024]{3,2,1,0:T(8,128)(2,1)S(1)} %copy-done.5, ...), custom_call_target="tpu_custom_call" | custom-call | flops 10485760 | bytes 10485760 | tf_op jit(solution)/shard_map/inner/pallas_call | solution.py:494
  12.5 0.0 collective-permute-done.2.z_low
  12.5 2.7 %collective-permute-done.3.z_high = f32[5,8,1024]{2,1,0:T(8,128)S(1)} collective-permute-done((f32[5,8,1024]{2,1,0:T(8,128)S(1)}, f32[5,8,1024]{2,1,0:T(8,128)S(1)}, u32[]{:S(2)}, u32[]{:S(2)}) %collective-permute-start.3) | collective-permute-done | bytes 163872 | tf_op jit(solution)/shard_map/ppermute | solution.py:447
  15.2 0.0 collective-permute-done.y_low
  15.2 0.0 collective-permute-done.1.y_high
  15.2 0.0 copy-done
  15.2 0.0 copy-done.1
  15.2 0.0 copy-done.2
  15.2 0.0 copy-done.3
  15.3 0.0 copy-start.4
  15.3 1.6 %source.1 = (f32[3,8,16,1024]{3,2,1,0:T(8,128)S(1)}, f32[8,16,1024]{2,1,0:T(8,128)}, f32[32,40,128]{2,1,0:T(8,128)S(1)}) custom-call(f32[4,8,16,1024]{3,2,1,0:T(8,128)S(1)} %get-tuple-element.20.moved, f32[4,16,1024]{2,1,0:T(8,128)S(1)} %get-tuple-element.21.row_factors, f32[4,8,1024]{2,1,0:T(8,128)S(1)} %get-tuple-element.22.layer_factors, ...), custom_call_target="tpu_custom_call" | custom-call | tf_op jit(solution)/shard_map/source/pallas_call | solution.py:509
  16.9 21.7 %all_to_all.15.received = f32[32,40,128]{2,1,0:T(8,128)S(1)} all-to-all(f32[32,40,128]{2,1,0:T(8,128)S(1)} %get-tuple-element.27), channel_id=1, replica_groups=mesh['gy'=32,'gz'=8] {'gy'}, dimensions={0} | all-to-all | bytes 1310720 | tf_op jit(solution)/shard_map/all_to_all | solution.py:451
  38.6 0.0 copy-done.4
  38.6 0.9 %down.1 = (f32[19,64,128]{2,1,0:T(8,128)S(1)}, f32[8,64,128]{2,1,0:T(8,128)S(1)}) custom-call(f32[32,40,128]{2,1,0:T(8,128)S(1)} %all_to_all.15.received, f32[608,128]{1,0:T(8,128)S(1)} %copy-done.4), custom_call_target="tpu_custom_call" | custom-call | tf_op jit(solution)/shard_map/down/pallas_call | solution.py:530
  39.5 18.3 %all_to_all.16.handed = f32[8,64,128]{2,1,0:T(8,128)S(1)} all-to-all(f32[8,64,128]{2,1,0:T(8,128)S(1)} %get-tuple-element.29), channel_id=1, replica_groups=mesh['gy'=32,'gz'=8] {'gz'}, dimensions={0} | all-to-all | bytes 524288 | tf_op jit(solution)/shard_map/all_to_all | solution.py:451
  57.7 1.1 %up.1 = f32[32,40,128]{2,1,0:T(8,128)S(1)} custom-call(f32[19,64,128]{2,1,0:T(8,128)S(1)} %get-tuple-element.28.spectral, f32[8,64,128]{2,1,0:T(8,128)S(1)} %all_to_all.16.handed, f32[608,128]{1,0:T(8,128)S(1)} %copy-done.4), custom_call_target="tpu_custom_call" | custom-call | tf_op jit(solution)/shard_map/up/pallas_call | solution.py:539
  58.9 18.6 %all_to_all.17.received = f32[32,40,128]{2,1,0:T(8,128)S(1)} all-to-all(f32[32,40,128]{2,1,0:T(8,128)S(1)} %up.1), channel_id=1, replica_groups=mesh['gy'=32,'gz'=8] {'gy'}, dimensions={0} | all-to-all | bytes 1310720 | tf_op jit(solution)/shard_map/all_to_all | solution.py:451
  77.4 2.7 %gradient.1 = f32[3,8,16,1024]{3,2,1,0:T(8,128)} custom-call(f32[32,40,128]{2,1,0:T(8,128)S(1)} %all_to_all.17.received, bf16[512,512]{1,0:T(8,128)(2,1)S(1)} %copy-done.3, bf16[512,512]{1,0:T(8,128)(2,1)S(1)} %copy-done.2, bf16[512,512]{1,0:T(8,128)(2,1)S(1)} %copy-done.1, bf16[512,512]{1,0:T(8,128)(2,1)S(1)} %copy-done, ...), custom_call_target="tpu_custom_call" | custom-call | tf_op jit(solution)/shard_map/gradient/pallas_call | solution.py:548
Async XLA Ops:
  0.6 9.4 %copy-start.5 = (bf16[3,8,16,1024]{3,2,1,0:T(8,128)(2,1)S(1)}, bf16[3,8,16,1024]{3,2,1,0:T(8,128)(2,1)}, u32[]{:S(2)}) copy-start(bf16[3,8,16,1024]{3,2,1,0:T(8,128)(2,1)} %flow.1) | copy-start | bytes 2359300
  2.5 12.7 %collective-permute-start = (f32[5,16,1024]{2,1,0:T(8,128)S(1)}, f32[5,16,1024]{2,1,0:T(8,128)S(1)}, u32[]{:S(2)}, u32[]{:S(2)}) collective-permute-start(f32[5,16,1024]{2,1,0:T(8,128)S(1)} %get-tuple-element.23), channel_id=1, source_target_pairs={{0,8},{8,16},{16,24},{24,32},{32,40},{40,48},{48,56},{56,64},{64,7... | collective-permute-start | bytes 983048 | tf_op jit(solution)/shard_map/ppermute | solution.py:447
  5.1 10.1 %collective-permute-start.1 = (f32[5,16,1024]{2,1,0:T(8,128)S(1)}, f32[5,16,1024]{2,1,0:T(8,128)S(1)}, u32[]{:S(2)}, u32[]{:S(2)}) collective-permute-start(f32[5,16,1024]{2,1,0:T(8,128)S(1)} %get-tuple-element.24), channel_id=1, source_target_pairs={{0,248},{8,0},{16,8},{24,16},{32,24},{40,32},{48,40},{56,48},{64,5... | collective-permute-start | bytes 983048 | tf_op jit(solution)/shard_map/ppermute | solution.py:447
  5.9 6.6 %collective-permute-start.2 = (f32[5,8,1024]{2,1,0:T(8,128)S(1)}, f32[5,8,1024]{2,1,0:T(8,128)S(1)}, u32[]{:S(2)}, u32[]{:S(2)}) collective-permute-start(f32[5,8,1024]{2,1,0:T(8,128)S(1)} %get-tuple-element.25), channel_id=1, source_target_pairs={{0,1},{1,2},{2,3},{3,4},{4,5},{5,6},{6,7},{8,9},{9,10},{10,11},{11... | collective-permute-start | bytes 491528 | tf_op jit(solution)/shard_map/ppermute | solution.py:447
  8.7 6.5 %collective-permute-start.3 = (f32[5,8,1024]{2,1,0:T(8,128)S(1)}, f32[5,8,1024]{2,1,0:T(8,128)S(1)}, u32[]{:S(2)}, u32[]{:S(2)}) collective-permute-start(f32[5,8,1024]{2,1,0:T(8,128)S(1)} %get-tuple-element.26), channel_id=1, source_target_pairs={{1,0},{2,1},{3,2},{4,3},{5,4},{6,5},{7,6},{9,8},{10,9},{11,10},{12... | collective-permute-start | bytes 491528 | tf_op jit(solution)/shard_map/ppermute | solution.py:447
  10.0 5.2 %copy-start = (bf16[512,512]{1,0:T(8,128)(2,1)S(1)}, bf16[512,512]{1,0:T(8,128)(2,1)}, u32[]{:S(2)}) copy-start(bf16[512,512]{1,0:T(8,128)(2,1)} %constant.13.clone.odd_t) | copy-start | bytes 1572868
  10.0 5.2 %copy-start.1 = (bf16[512,512]{1,0:T(8,128)(2,1)S(1)}, bf16[512,512]{1,0:T(8,128)(2,1)}, u32[]{:S(2)}) copy-start(bf16[512,512]{1,0:T(8,128)(2,1)} %constant.12.clone.odd_h) | copy-start | bytes 1572868
  10.0 5.2 %copy-start.2 = (bf16[512,512]{1,0:T(8,128)(2,1)S(1)}, bf16[512,512]{1,0:T(8,128)(2,1)}, u32[]{:S(2)}) copy-start(bf16[512,512]{1,0:T(8,128)(2,1)} %constant.11.clone.even_t) | copy-start | bytes 1572868
  10.0 5.2 %copy-start.3 = (bf16[512,512]{1,0:T(8,128)(2,1)S(1)}, bf16[512,512]{1,0:T(8,128)(2,1)}, u32[]{:S(2)}) copy-start(bf16[512,512]{1,0:T(8,128)(2,1)} %constant.10.clone.even_h) | copy-start | bytes 1572868
  15.3 23.3 %copy-start.4 = (f32[608,128]{1,0:T(8,128)S(1)}, f32[608,128]{1,0:T(8,128)}, u32[]{:S(2)}) copy-start(f32[608,128]{1,0:T(8,128)} %constant.14.clone.table) | copy-start | bytes 933892

commit v6 on v5

--- a/solution.py
+++ b/solution.py
@@ -103,31 +103,41 @@
     return copies
 
 
+def odd(axis):
+    return lax.axis_index(axis) % 2 == 1
+
+
 def sides_kernel(
-    motion_hbm, thermal_hbm, base_hbm, y_first, y_last, z_first, z_last, motion, thermal, base, sems
+    motion_hbm, thermal_hbm, base_hbm, row_near, row_far, layer_near, layer_far, motion, thermal, base, sems
 ):
     pairs = ((base_hbm, base), (thermal_hbm, thermal), (motion_hbm, motion))
     fetched = start_copies(pairs, sems)
+    is_odd = odd("gz")
+    near = jnp.where(odd("gy"), 0, ROWS - 1)
+    far = ROWS - 1 - near
+
+    def edges(first, last):
+        return jnp.where(is_odd, first, last), jnp.where(is_odd, last, first)
+
     fetched[0].wait()
+    row_near[4] = base[near].astype(F32)
+    row_far[4] = base[far].astype(F32)
     for y in range(ROWS):
         warm = base[y].astype(F32)
-        z_first[4, y:y + 1, :] = warm[:1]
-        z_last[4, y:y + 1, :] = warm[LAYERS - 1:]
-        if y in (0, ROWS - 1):
-            (y_last if y else y_first)[4] = warm
+        layer_near[4, y:y + 1, :], layer_far[4, y:y + 1, :] = edges(warm[:1], warm[LAYERS - 1:])
     fetched[1].wait()
-    y_first[3] = thermal[0]
-    y_last[3] = thermal[ROWS - 1]
+    row_near[3] = thermal[near]
+    row_far[3] = thermal[far]
     for y in range(ROWS):
-        z_first[3, y:y + 1, :] = thermal[y, :1, :]
-        z_last[3, y:y + 1, :] = thermal[y, LAYERS - 1:, :]
+        layer_near[3, y:y + 1, :], layer_far[3, y:y + 1, :] = edges(thermal[y, :1, :], thermal[y, LAYERS - 1:, :])
     fetched[2].wait()
     for c in range(3):
-        y_first[c] = motion[c, 0]
-        y_last[c] = motion[c, ROWS - 1]
+        row_near[c] = motion[c, near]
+        row_far[c] = motion[c, far]
         for y in range(ROWS):
-            z_first[c, y:y + 1, :] = motion[c, y, :1, :]
-            z_last[c, y:y + 1, :] = motion[c, y, LAYERS - 1:, :]
+            layer_near[c, y:y + 1, :], layer_far[c, y:y + 1, :] = edges(
+                motion[c, y, :1, :], motion[c, y, LAYERS - 1:, :]
+            )
 
 
 def inner_kernel(motion, thermal, flow, base, moved, row_factors, layer_factors):
@@ -182,12 +192,18 @@
 
 
 def source_kernel(
-    moved, row_factors, layer_factors, y_low, y_high, z_low, z_high, even_h, even_t, odd_h, odd_t,
+    moved, row_factors, layer_factors, row_near, row_far, layer_near, layer_far,
+    even_h, even_t, odd_h, odd_t,
     provisional, thermal_hbm, message, thermal, source, lines, row_p, layer_p, sems
 ):
     size_x = moved.shape[-1]
     row = lax.broadcasted_iota(jnp.int32, (8, size_x), 0)
     top = lax.broadcasted_iota(jnp.int32, (LAYERS, size_x), 0) == LAYERS - 1
+    odd_y, odd_z = odd("gy"), odd("gz")
+    y_low = [jnp.where(odd_y, row_near[c], row_far[c]) for c in range(5)]
+    y_high = [jnp.where(odd_y, row_far[c], row_near[c]) for c in range(5)]
+    z_low = [jnp.where(odd_z, layer_near[c], layer_far[c]) for c in range(5)]
+    z_high = [jnp.where(odd_z, layer_far[c], layer_near[c]) for c in range(5)]
     lows = [layer_factors[0] * z_low[c] for c in range(4)]
     highs = [layer_factors[2] * z_high[c] for c in range(4)]
     lows[2] = lows[2] + layer_factors[1] * z_low[4]
@@ -441,9 +457,12 @@
         copy.wait()
 
 
-def shifted(value, axis, by, periodic):
+def swapped(value, axis, first, periodic):
     size = lax.axis_size(axis)
-    pairs = [(i, (i + by) % size) for i in range(size) if periodic or 0 <= i + by < size]
+    pairs = []
+    for i in range(first, size, 2):
+        if periodic or i + 1 < size:
+            pairs += [(i, (i + 1) % size), ((i + 1) % size, i)]
     return lax.ppermute(value, axis, pairs)
 
 
@@ -459,9 +478,9 @@
     size_x = dual_thermal.shape[-1]
     groups_y = lax.axis_size("gy")
     groups_z = lax.axis_size("gz")
-    even, odd, table = tables(size_x, ROWS * groups_y)
-    even_h, even_t = map(jnp.asarray, even)
-    odd_h, odd_t = map(jnp.asarray, odd)
+    evens, odds, table = tables(size_x, ROWS * groups_y)
+    even_h, even_t = map(jnp.asarray, evens)
+    odd_h, odd_t = map(jnp.asarray, odds)
     modes = ROWS * groups_y // 4
     blocks = size_x // 128
 
@@ -478,7 +497,7 @@
     thermal_shape = motion_shape[1:]
     message_shape = (groups_y, PIECE, 128)
     fields = tuple(jax.ShapeDtypeStruct(a.shape, a.dtype) for a in (dual_motion, dual_thermal, base))
-    y_first, y_last, z_first, z_last, motion, thermal, base = pl.pallas_call(
+    row_near, row_far, layer_near, layer_far, motion, thermal, base = pl.pallas_call(
         sides_kernel,
         out_shape=(rows, rows, layers, layers, *fields),
         in_specs=[HBM] * 3,
@@ -487,10 +506,10 @@
         compiler_params=params(16),
         name="sides",
     )(*map(hbm, (dual_motion, dual_thermal, base)))
-    z_low = shifted(z_last, "gz", 1, False)
-    z_high = shifted(z_first, "gz", -1, False)
-    y_low = shifted(y_last, "gy", 1, True)
-    y_high = shifted(y_first, "gy", -1, True)
+    row_near = swapped(row_near, "gy", 0, True)
+    row_far = swapped(row_far, "gy", 1, True)
+    layer_near = swapped(layer_near, "gz", 0, False)
+    layer_far = swapped(layer_far, "gz", 1, False)
     moved, row_factors, layer_factors = pl.pallas_call(
         inner_kernel,
         out_shape=(
@@ -525,7 +544,10 @@
         ],
         compiler_params=params(24),
         name="source",
-    )(moved, row_factors, layer_factors, y_low, y_high, z_low, z_high, even_h, even_t, odd_h, odd_t)
+    )(
+        moved, row_factors, layer_factors, row_near, row_far, layer_near, layer_far,
+        even_h, even_t, odd_h, odd_t,
+    )
     received = exchanged(message, "gy")
     spectral, handed = pl.pallas_call(
         down_kernel,

time: 80.4 us -> 79.1 us (0.984)
  starting transfers between devices: 7.51 us -> 5.08 us
  blocking collectives: 58.5 us -> 59.8 us
    ppermute x4, starting transfers between devices: 7.51 us -> 5.08 us  [swapped(): return lax.ppermute(value, axis, pairs)]
    all_to_all x3, blocking collectives: 58.5 us -> 59.8 us  [exchanged(): return lax.all_to_all(pieces, axis, split_axis=0, concat_axis=0, tiled=True)]
where the time goes in v6:
time: 79.1 us; the launch traced here: 78.9 us
  blocking collectives  59.8 us (76%)
  Pallas kernels  10.7 us (14%)
  starting transfers between devices  5.08 us (6%)
  waiting for transfers between devices  2.49 us (3%)
    all_to_all x3, blocking collectives, exchanged(): return lax.all_to_all(pieces, axis, split_axis=0, concat_axis=0, tiled=True)  59.8 us
    ppermute x4, starting transfers between devices, swapped(): return lax.ppermute(value, axis, pairs)  5.08 us
    pallas_call x1, Pallas kernels, on_device(): pl.pallas_call(gradient_kernel, out_shape=pltpu.HBM(motion_shape, F32), i...  2.74 us
    ppermute x4, waiting for transfers between devices, swapped(): return lax.ppermute(value, axis, pairs)  2.49 us
    pallas_call x1, Pallas kernels, on_device(): pl.pallas_call(inner_kernel, out_shape=(shape_of(4, *thermal_shape), shap...  2.45 us
    pallas_call x1, Pallas kernels, on_device(): pl.pallas_call(sides_kernel, out_shape=(rows, rows, layers, layers, *fiel...  1.82 us
    pallas_call x1, Pallas kernels, on_device(): pl.pallas_call(source_kernel, out_shape=(shape_of(*motion_shape), pltpu.H...  1.71 us
  transfers between devices with their start and end apart: 4, of which 1 were waited for; matrix products, arithmetic and copies ran while one was open for 0% of the time, Pallas kernels for 3%

profile of v6, /device:TPU:1, one launch (start us, length us, event | category | flops | bytes accessed | tf_op | source)
XLA Modules:
  0.0 78.9 jit_solution(1697191675139495644)
XLA Ops:
  0.6 0.0 copy-start.5
  0.6 1.8 %sides.1 = (f32[5,16,1024]{2,1,0:T(8,128)S(1)}, f32[5,16,1024]{2,1,0:T(8,128)S(1)}, f32[5,8,1024]{2,1,0:T(8,128)S(1)}, f32[5,8,1024]{2,1,0:T(8,128)S(1)}, f32[3,...) custom-call(f32[3,8,16,1024]{3,2,1,0:T(8,128)} %motion_hbm.1, ...), custom_call_target="tpu_custom_call" | custom-call | tf_op jit(solution)/shard_map/sides/pallas_call | solution.py:500
  2.5 3.3 %collective-permute-start = (f32[5,16,1024]{2,1,0:T(8,128)S(1)}, f32[5,16,1024]{2,1,0:T(8,128)S(1)}, u32[]{:S(2)}, u32[]{:S(2)}) collective-permute-start(f32[5,16,1024]{2,1,0:T(8,128)S(1)} %get-tuple-element.23), channel_id=1, source_target_pairs={{0,8},{8,0},{16,24},{24,16},{32,40},{40,32},{48,56},{56,48},{64,72... | collective-permute-start | bytes 983048 | tf_op jit(solution)/shard_map/ppermute | solution.py:466
  5.8 0.0 collective-permute-start.1
  5.8 1.1 %collective-permute-start.2 = (f32[5,8,1024]{2,1,0:T(8,128)S(1)}, f32[5,8,1024]{2,1,0:T(8,128)S(1)}, u32[]{:S(2)}, u32[]{:S(2)}) collective-permute-start(f32[5,8,1024]{2,1,0:T(8,128)S(1)} %get-tuple-element.25), channel_id=1, source_target_pairs={{0,1},{1,0},{2,3},{3,2},{4,5},{5,4},{6,7},{7,6},{8,9},{9,8},{10,11... | collective-permute-start | bytes 491528 | tf_op jit(solution)/shard_map/ppermute | solution.py:466
  6.9 0.7 collective-permute-start.3
  7.6 0.0 copy-done.5
  7.6 0.0 copy-start
  7.6 0.0 copy-start.1
  7.6 0.0 copy-start.2
  7.6 0.0 copy-start.3
  7.6 2.4 %inner.1 = (f32[4,8,16,1024]{3,2,1,0:T(8,128)S(1)}, f32[4,16,1024]{2,1,0:T(8,128)S(1)}, f32[4,8,1024]{2,1,0:T(8,128)S(1)}) custom-call(f32[3,8,16,1024]{3,2,1,0:T(8,128)S(1)} %get-tuple-element.17.motion, f32[8,16,1024]{2,1,0:T(8,128)S(1)} %get-tuple-element.18.thermal, bf16[3,8,16,1024]{3,2,1,0:T(8,128)(2,1)S(1)} %copy-done.5, ...), custom_call_target="tpu_custom_call" | custom-call | flops 10485760 | bytes 10485760 | tf_op jit(solution)/shard_map/inner/pallas_call | solution.py:513
  10.1 0.0 collective-permute-done.2.layer_near
  10.1 0.0 collective-permute-done.3.layer_far
  10.1 0.0 collective-permute-done.row_near
  10.1 2.5 %collective-permute-done.1.row_far = f32[5,16,1024]{2,1,0:T(8,128)S(1)} collective-permute-done((f32[5,16,1024]{2,1,0:T(8,128)S(1)}, f32[5,16,1024]{2,1,0:T(8,128)S(1)}, u32[]{:S(2)}, u32[]{:S(2)}) %collective-permute-start.1) | collective-permute-done | bytes 327712 | tf_op jit(solution)/shard_map/ppermute | solution.py:466
  12.6 0.0 copy-done
  12.6 0.0 copy-done.1
  12.6 0.0 copy-done.2
  12.6 0.0 copy-done.3
  12.6 0.0 copy-start.4
  12.6 1.7 %source.1 = (f32[3,8,16,1024]{3,2,1,0:T(8,128)S(1)}, f32[8,16,1024]{2,1,0:T(8,128)}, f32[32,40,128]{2,1,0:T(8,128)S(1)}) custom-call(f32[4,8,16,1024]{3,2,1,0:T(8,128)S(1)} %get-tuple-element.20.moved, f32[4,16,1024]{2,1,0:T(8,128)S(1)} %get-tuple-element.21.row_factors, f32[4,8,1024]{2,1,0:T(8,128)S(1)} %get-tuple-element.22.layer_factors, ...), custom_call_target="tpu_custom_call" | custom-call | tf_op jit(solution)/shard_map/source/pallas_call | solution.py:528
  14.3 20.8 %all_to_all.15.received = f32[32,40,128]{2,1,0:T(8,128)S(1)} all-to-all(f32[32,40,128]{2,1,0:T(8,128)S(1)} %get-tuple-element.27), channel_id=1, replica_groups=mesh['gy'=32,'gz'=8] {'gy'}, dimensions={0} | all-to-all | bytes 1310720 | tf_op jit(solution)/shard_map/all_to_all | solution.py:470
  35.1 0.0 copy-done.4
  35.1 0.9 %down.1 = (f32[19,64,128]{2,1,0:T(8,128)S(1)}, f32[8,64,128]{2,1,0:T(8,128)S(1)}) custom-call(f32[32,40,128]{2,1,0:T(8,128)S(1)} %all_to_all.15.received, f32[608,128]{1,0:T(8,128)S(1)} %copy-done.4), custom_call_target="tpu_custom_call" | custom-call | tf_op jit(solution)/shard_map/down/pallas_call | solution.py:552
  36.0 20.5 %all_to_all.16.handed = f32[8,64,128]{2,1,0:T(8,128)S(1)} all-to-all(f32[8,64,128]{2,1,0:T(8,128)S(1)} %get-tuple-element.29), channel_id=1, replica_groups=mesh['gy'=32,'gz'=8] {'gz'}, dimensions={0} | all-to-all | bytes 524288 | tf_op jit(solution)/shard_map/all_to_all | solution.py:470
  56.5 1.1 %up.1 = f32[32,40,128]{2,1,0:T(8,128)S(1)} custom-call(f32[19,64,128]{2,1,0:T(8,128)S(1)} %get-tuple-element.28.spectral, f32[8,64,128]{2,1,0:T(8,128)S(1)} %all_to_all.16.handed, f32[608,128]{1,0:T(8,128)S(1)} %copy-done.4), custom_call_target="tpu_custom_call" | custom-call | tf_op jit(solution)/shard_map/up/pallas_call | solution.py:561
  57.6 18.6 %all_to_all.17.received = f32[32,40,128]{2,1,0:T(8,128)S(1)} all-to-all(f32[32,40,128]{2,1,0:T(8,128)S(1)} %up.1), channel_id=1, replica_groups=mesh['gy'=32,'gz'=8] {'gy'}, dimensions={0} | all-to-all | bytes 1310720 | tf_op jit(solution)/shard_map/all_to_all | solution.py:470
  76.2 2.7 %gradient.1 = f32[3,8,16,1024]{3,2,1,0:T(8,128)} custom-call(f32[32,40,128]{2,1,0:T(8,128)S(1)} %all_to_all.17.received, bf16[512,512]{1,0:T(8,128)(2,1)S(1)} %copy-done.3, bf16[512,512]{1,0:T(8,128)(2,1)S(1)} %copy-done.2, bf16[512,512]{1,0:T(8,128)(2,1)S(1)} %copy-done.1, bf16[512,512]{1,0:T(8,128)(2,1)S(1)} %copy-done, ...), custom_call_target="tpu_custom_call" | custom-call | tf_op jit(solution)/shard_map/gradient/pallas_call | solution.py:570
Async XLA Ops:
  0.6 6.9 %copy-start.5 = (bf16[3,8,16,1024]{3,2,1,0:T(8,128)(2,1)S(1)}, bf16[3,8,16,1024]{3,2,1,0:T(8,128)(2,1)}, u32[]{:S(2)}) copy-start(bf16[3,8,16,1024]{3,2,1,0:T(8,128)(2,1)} %flow.1) | copy-start | bytes 2359300
  2.5 7.6 %collective-permute-start = (f32[5,16,1024]{2,1,0:T(8,128)S(1)}, f32[5,16,1024]{2,1,0:T(8,128)S(1)}, u32[]{:S(2)}, u32[]{:S(2)}) collective-permute-start(f32[5,16,1024]{2,1,0:T(8,128)S(1)} %get-tuple-element.23), channel_id=1, source_target_pairs={{0,8},{8,0},{16,24},{24,16},{32,40},{40,32},{48,56},{56,48},{64,72... | collective-permute-start | bytes 983048 | tf_op jit(solution)/shard_map/ppermute | solution.py:466
  5.8 6.8 %collective-permute-start.1 = (f32[5,16,1024]{2,1,0:T(8,128)S(1)}, f32[5,16,1024]{2,1,0:T(8,128)S(1)}, u32[]{:S(2)}, u32[]{:S(2)}) collective-permute-start(f32[5,16,1024]{2,1,0:T(8,128)S(1)} %get-tuple-element.24), channel_id=1, source_target_pairs={{8,16},{16,8},{24,32},{32,24},{40,48},{48,40},{56,64},{64,56},{72,... | collective-permute-start | bytes 983048 | tf_op jit(solution)/shard_map/ppermute | solution.py:466
  5.8 4.3 %collective-permute-start.2 = (f32[5,8,1024]{2,1,0:T(8,128)S(1)}, f32[5,8,1024]{2,1,0:T(8,128)S(1)}, u32[]{:S(2)}, u32[]{:S(2)}) collective-permute-start(f32[5,8,1024]{2,1,0:T(8,128)S(1)} %get-tuple-element.25), channel_id=1, source_target_pairs={{0,1},{1,0},{2,3},{3,2},{4,5},{5,4},{6,7},{7,6},{8,9},{9,8},{10,11... | collective-permute-start | bytes 491528 | tf_op jit(solution)/shard_map/ppermute | solution.py:466
  6.9 3.2 %collective-permute-start.3 = (f32[5,8,1024]{2,1,0:T(8,128)S(1)}, f32[5,8,1024]{2,1,0:T(8,128)S(1)}, u32[]{:S(2)}, u32[]{:S(2)}) collective-permute-start(f32[5,8,1024]{2,1,0:T(8,128)S(1)} %get-tuple-element.26), channel_id=1, source_target_pairs={{1,2},{2,1},{3,4},{4,3},{5,6},{6,5},{9,10},{10,9},{11,12},{12,11},... | collective-permute-start | bytes 491528 | tf_op jit(solution)/shard_map/ppermute | solution.py:466
  7.6 5.0 %copy-start = (bf16[512,512]{1,0:T(8,128)(2,1)S(1)}, bf16[512,512]{1,0:T(8,128)(2,1)}, u32[]{:S(2)}) copy-start(bf16[512,512]{1,0:T(8,128)(2,1)} %constant.13.clone.odd_t) | copy-start | bytes 1572868
  7.6 5.0 %copy-start.1 = (bf16[512,512]{1,0:T(8,128)(2,1)S(1)}, bf16[512,512]{1,0:T(8,128)(2,1)}, u32[]{:S(2)}) copy-start(bf16[512,512]{1,0:T(8,128)(2,1)} %constant.12.clone.odd_h) | copy-start | bytes 1572868
  7.6 5.0 %copy-start.2 = (bf16[512,512]{1,0:T(8,128)(2,1)S(1)}, bf16[512,512]{1,0:T(8,128)(2,1)}, u32[]{:S(2)}) copy-start(bf16[512,512]{1,0:T(8,128)(2,1)} %constant.11.clone.even_t) | copy-start | bytes 1572868
  7.6 5.0 %copy-start.3 = (bf16[512,512]{1,0:T(8,128)(2,1)S(1)}, bf16[512,512]{1,0:T(8,128)(2,1)}, u32[]{:S(2)}) copy-start(bf16[512,512]{1,0:T(8,128)(2,1)} %constant.10.clone.even_h) | copy-start | bytes 1572868
  12.6 22.5 %copy-start.4 = (f32[608,128]{1,0:T(8,128)S(1)}, f32[608,128]{1,0:T(8,128)}, u32[]{:S(2)}) copy-start(f32[608,128]{1,0:T(8,128)} %constant.14.clone.table) | copy-start | bytes 933892

commit v7 on v6

--- a/solution.py
+++ b/solution.py
@@ -84,7 +84,9 @@
 
 def product(values, head, tail, how):
     a, b = split(values)
-    return how(a, head) + (how(b, head) + how(a, tail))
+    both = how(jnp.concatenate([a, b], 0), head)
+    count = values.shape[0]
+    return both[:count] + (both[count:] + how(a, tail))
 
 
 def keep(ref, start, values):
@@ -192,7 +194,7 @@
 
 
 def source_kernel(
-    moved, row_factors, layer_factors, row_near, row_far, layer_near, layer_far,
+    moved, row_factors, layer_factors, layer_far, layer_near, row_far, row_near,
     even_h, even_t, odd_h, odd_t,
     provisional, thermal_hbm, message, thermal, source, lines, row_p, layer_p, sems
 ):
@@ -263,7 +265,8 @@
     wide = jnp.concatenate([table[pl.ds(n * size_y, size_y), :] for n in range(size_y // 128)], 1)
     left = split(wide)
     right = split(values)
-    return dot(left[0], right[0]) + (dot(left[0], right[1]) + dot(left[1], right[0]))
+    both = dot(jnp.concatenate(left, 0), right[0])
+    return both[:size_y] + (both[size_y:] + dot(left[0], right[1]))
 
 
 def wall_factors(lam, slab, slabs):
@@ -545,7 +548,7 @@
         compiler_params=params(24),
         name="source",
     )(
-        moved, row_factors, layer_factors, row_near, row_far, layer_near, layer_far,
+        moved, row_factors, layer_factors, layer_far, layer_near, row_far, row_near,
         even_h, even_t, odd_h, odd_t,
     )
     received = exchanged(message, "gy")

time: 79.1 us -> 78.1 us (0.987)
  blocking collectives: 59.8 us -> 53.2 us
  starting transfers between devices: 5.08 us -> 11.5 us
    all_to_all x3, blocking collectives: 59.8 us -> 53.2 us  [exchanged(): return lax.all_to_all(pieces, axis, split_axis=0, concat_axis=0, tiled=True)]
    ppermute x4, starting transfers between devices: 5.08 us -> 11.5 us  [swapped(): return lax.ppermute(value, axis, pairs)]
where the time goes in v7:
time: 78.1 us; the launch traced here: 77.9 us
  blocking collectives  53.2 us (68%)
  starting transfers between devices  11.5 us (15%)
  Pallas kernels  10.5 us (13%)
  waiting for transfers between devices  1.89 us (2%)
    all_to_all x3, blocking collectives, exchanged(): return lax.all_to_all(pieces, axis, split_axis=0, concat_axis=0, tiled=True)  53.2 us
    ppermute x4, starting transfers between devices, swapped(): return lax.ppermute(value, axis, pairs)  11.5 us
    pallas_call x1, Pallas kernels, on_device(): pl.pallas_call(gradient_kernel, out_shape=pltpu.HBM(motion_shape, F32), i...  2.6 us
    pallas_call x1, Pallas kernels, on_device(): pl.pallas_call(inner_kernel, out_shape=(shape_of(4, *thermal_shape), shap...  2.45 us
    ppermute x4, waiting for transfers between devices, swapped(): return lax.ppermute(value, axis, pairs)  1.89 us
    pallas_call x1, Pallas kernels, on_device(): pl.pallas_call(sides_kernel, out_shape=(rows, rows, layers, layers, *fiel...  1.82 us
    pallas_call x1, Pallas kernels, on_device(): pl.pallas_call(source_kernel, out_shape=(shape_of(*motion_shape), pltpu.H...  1.7 us
  transfers between devices with their start and end apart: 4, of which 1 were waited for; matrix products, arithmetic and copies ran while one was open for 0% of the time, Pallas kernels for 3%

profile of v7, /device:TPU:1, one launch (start us, length us, event | category | flops | bytes accessed | tf_op | source)
XLA Modules:
  0.0 77.9 jit_solution(17112705671209965968)
XLA Ops:
  0.6 0.0 copy-start.5
  0.6 1.8 %sides.1 = (f32[5,16,1024]{2,1,0:T(8,128)S(1)}, f32[5,16,1024]{2,1,0:T(8,128)S(1)}, f32[5,8,1024]{2,1,0:T(8,128)S(1)}, f32[5,8,1024]{2,1,0:T(8,128)S(1)}, f32[3,...) custom-call(f32[3,8,16,1024]{3,2,1,0:T(8,128)} %motion_hbm.1, ...), custom_call_target="tpu_custom_call" | custom-call | tf_op jit(solution)/shard_map/sides/pallas_call | solution.py:503
  2.5 2.7 %collective-permute-start.2 = (f32[5,16,1024]{2,1,0:T(8,128)S(1)}, f32[5,16,1024]{2,1,0:T(8,128)S(1)}, u32[]{:S(2)}, u32[]{:S(2)}) collective-permute-start(f32[5,16,1024]{2,1,0:T(8,128)S(1)} %get-tuple-element.25), channel_id=1, source_target_pairs={{8,16},{16,8},{24,32},{32,24},{40,48},{48,40},{56,64},{64,56},{72,... | collective-permute-start | bytes 983048 | tf_op jit(solution)/shard_map/ppermute | solution.py:469
  5.2 3.6 %collective-permute-start.3 = (f32[5,16,1024]{2,1,0:T(8,128)S(1)}, f32[5,16,1024]{2,1,0:T(8,128)S(1)}, u32[]{:S(2)}, u32[]{:S(2)}) collective-permute-start(f32[5,16,1024]{2,1,0:T(8,128)S(1)} %get-tuple-element.26), channel_id=1, source_target_pairs={{0,8},{8,0},{16,24},{24,16},{32,40},{40,32},{48,56},{56,48},{64,72... | collective-permute-start | bytes 983048 | tf_op jit(solution)/shard_map/ppermute | solution.py:469
  8.7 0.7 collective-permute-start
  9.4 4.6 %collective-permute-start.1 = (f32[5,8,1024]{2,1,0:T(8,128)S(1)}, f32[5,8,1024]{2,1,0:T(8,128)S(1)}, u32[]{:S(2)}, u32[]{:S(2)}) collective-permute-start(f32[5,8,1024]{2,1,0:T(8,128)S(1)} %get-tuple-element.24), channel_id=1, source_target_pairs={{0,1},{1,0},{2,3},{3,2},{4,5},{5,4},{6,7},{7,6},{8,9},{9,8},{10,11... | collective-permute-start | bytes 491528 | tf_op jit(solution)/shard_map/ppermute | solution.py:469
  14.0 0.0 copy-done.5
  14.0 0.0 copy-start
  14.0 0.0 copy-start.1
  14.0 0.0 copy-start.2
  14.0 0.0 copy-start.3
  14.0 2.4 %inner.1 = (f32[4,8,16,1024]{3,2,1,0:T(8,128)S(1)}, f32[4,16,1024]{2,1,0:T(8,128)S(1)}, f32[4,8,1024]{2,1,0:T(8,128)S(1)}) custom-call(f32[3,8,16,1024]{3,2,1,0:T(8,128)S(1)} %get-tuple-element.17.motion, f32[8,16,1024]{2,1,0:T(8,128)S(1)} %get-tuple-element.18.thermal, bf16[3,8,16,1024]{3,2,1,0:T(8,128)(2,1)S(1)} %copy-done.5, ...), custom_call_target="tpu_custom_call" | custom-call | flops 10485760 | bytes 10485760 | tf_op jit(solution)/shard_map/inner/pallas_call | solution.py:516
  16.5 0.0 collective-permute-done.layer_far
  16.5 1.9 %collective-permute-done.1.layer_near = f32[5,8,1024]{2,1,0:T(8,128)S(1)} collective-permute-done((f32[5,8,1024]{2,1,0:T(8,128)S(1)}, f32[5,8,1024]{2,1,0:T(8,128)S(1)}, u32[]{:S(2)}, u32[]{:S(2)}) %collective-permute-start.1) | collective-permute-done | bytes 163872 | tf_op jit(solution)/shard_map/ppermute | solution.py:469
  18.3 0.0 collective-permute-done.2.row_far
  18.3 0.0 collective-permute-done.3.row_near
  18.4 0.0 copy-done
  18.4 0.0 copy-done.1
  18.4 0.0 copy-done.2
  18.4 0.0 copy-done.3
  18.4 0.0 copy-start.4
  18.4 1.7 %source.1 = (f32[3,8,16,1024]{3,2,1,0:T(8,128)S(1)}, f32[8,16,1024]{2,1,0:T(8,128)}, f32[32,40,128]{2,1,0:T(8,128)S(1)}) custom-call(f32[4,8,16,1024]{3,2,1,0:T(8,128)S(1)} %get-tuple-element.20.moved, f32[4,16,1024]{2,1,0:T(8,128)S(1)} %get-tuple-element.21.row_factors, f32[4,8,1024]{2,1,0:T(8,128)S(1)} %get-tuple-element.22.layer_factors, ...), custom_call_target="tpu_custom_call" | custom-call | tf_op jit(solution)/shard_map/source/pallas_call | solution.py:531
  20.1 16.7 %all_to_all.15.received = f32[32,40,128]{2,1,0:T(8,128)S(1)} all-to-all(f32[32,40,128]{2,1,0:T(8,128)S(1)} %get-tuple-element.27), channel_id=1, replica_groups=mesh['gy'=32,'gz'=8] {'gy'}, dimensions={0} | all-to-all | bytes 1310720 | tf_op jit(solution)/shard_map/all_to_all | solution.py:473
  36.8 0.0 copy-done.4
  36.9 0.9 %down.1 = (f32[19,64,128]{2,1,0:T(8,128)S(1)}, f32[8,64,128]{2,1,0:T(8,128)S(1)}) custom-call(f32[32,40,128]{2,1,0:T(8,128)S(1)} %all_to_all.15.received, f32[608,128]{1,0:T(8,128)S(1)} %copy-done.4), custom_call_target="tpu_custom_call" | custom-call | tf_op jit(solution)/shard_map/down/pallas_call | solution.py:555
  37.7 17.9 %all_to_all.16.handed = f32[8,64,128]{2,1,0:T(8,128)S(1)} all-to-all(f32[8,64,128]{2,1,0:T(8,128)S(1)} %get-tuple-element.29), channel_id=1, replica_groups=mesh['gy'=32,'gz'=8] {'gz'}, dimensions={0} | all-to-all | bytes 524288 | tf_op jit(solution)/shard_map/all_to_all | solution.py:473
  55.6 1.1 %up.1 = f32[32,40,128]{2,1,0:T(8,128)S(1)} custom-call(f32[19,64,128]{2,1,0:T(8,128)S(1)} %get-tuple-element.28.spectral, f32[8,64,128]{2,1,0:T(8,128)S(1)} %all_to_all.16.handed, f32[608,128]{1,0:T(8,128)S(1)} %copy-done.4), custom_call_target="tpu_custom_call" | custom-call | tf_op jit(solution)/shard_map/up/pallas_call | solution.py:564
  56.7 18.6 %all_to_all.17.received = f32[32,40,128]{2,1,0:T(8,128)S(1)} all-to-all(f32[32,40,128]{2,1,0:T(8,128)S(1)} %up.1), channel_id=1, replica_groups=mesh['gy'=32,'gz'=8] {'gy'}, dimensions={0} | all-to-all | bytes 1310720 | tf_op jit(solution)/shard_map/all_to_all | solution.py:473
  75.3 2.6 %gradient.1 = f32[3,8,16,1024]{3,2,1,0:T(8,128)} custom-call(f32[32,40,128]{2,1,0:T(8,128)S(1)} %all_to_all.17.received, bf16[512,512]{1,0:T(8,128)(2,1)S(1)} %copy-done.3, bf16[512,512]{1,0:T(8,128)(2,1)S(1)} %copy-done.2, bf16[512,512]{1,0:T(8,128)(2,1)S(1)} %copy-done.1, bf16[512,512]{1,0:T(8,128)(2,1)S(1)} %copy-done, ...), custom_call_target="tpu_custom_call" | custom-call | tf_op jit(solution)/shard_map/gradient/pallas_call | solution.py:573
Async XLA Ops:
  0.6 13.3 %copy-start.5 = (bf16[3,8,16,1024]{3,2,1,0:T(8,128)(2,1)S(1)}, bf16[3,8,16,1024]{3,2,1,0:T(8,128)(2,1)}, u32[]{:S(2)}) copy-start(bf16[3,8,16,1024]{3,2,1,0:T(8,128)(2,1)} %flow.1) | copy-start | bytes 2359300
  2.5 15.9 %collective-permute-start.2 = (f32[5,16,1024]{2,1,0:T(8,128)S(1)}, f32[5,16,1024]{2,1,0:T(8,128)S(1)}, u32[]{:S(2)}, u32[]{:S(2)}) collective-permute-start(f32[5,16,1024]{2,1,0:T(8,128)S(1)} %get-tuple-element.25), channel_id=1, source_target_pairs={{8,16},{16,8},{24,32},{32,24},{40,48},{48,40},{56,64},{64,56},{72,... | collective-permute-start | bytes 983048 | tf_op jit(solution)/shard_map/ppermute | solution.py:469
  5.2 13.2 %collective-permute-start.3 = (f32[5,16,1024]{2,1,0:T(8,128)S(1)}, f32[5,16,1024]{2,1,0:T(8,128)S(1)}, u32[]{:S(2)}, u32[]{:S(2)}) collective-permute-start(f32[5,16,1024]{2,1,0:T(8,128)S(1)} %get-tuple-element.26), channel_id=1, source_target_pairs={{0,8},{8,0},{16,24},{24,16},{32,40},{40,32},{48,56},{56,48},{64,72... | collective-permute-start | bytes 983048 | tf_op jit(solution)/shard_map/ppermute | solution.py:469
  8.7 7.7 %collective-permute-start = (f32[5,8,1024]{2,1,0:T(8,128)S(1)}, f32[5,8,1024]{2,1,0:T(8,128)S(1)}, u32[]{:S(2)}, u32[]{:S(2)}) collective-permute-start(f32[5,8,1024]{2,1,0:T(8,128)S(1)} %get-tuple-element.23), channel_id=1, source_target_pairs={{1,2},{2,1},{3,4},{4,3},{5,6},{6,5},{9,10},{10,9},{11,12},{12,11},... | collective-permute-start | bytes 491528 | tf_op jit(solution)/shard_map/ppermute | solution.py:469
  9.4 9.0 %collective-permute-start.1 = (f32[5,8,1024]{2,1,0:T(8,128)S(1)}, f32[5,8,1024]{2,1,0:T(8,128)S(1)}, u32[]{:S(2)}, u32[]{:S(2)}) collective-permute-start(f32[5,8,1024]{2,1,0:T(8,128)S(1)} %get-tuple-element.24), channel_id=1, source_target_pairs={{0,1},{1,0},{2,3},{3,2},{4,5},{5,4},{6,7},{7,6},{8,9},{9,8},{10,11... | collective-permute-start | bytes 491528 | tf_op jit(solution)/shard_map/ppermute | solution.py:469
  14.0 4.4 %copy-start = (bf16[512,512]{1,0:T(8,128)(2,1)S(1)}, bf16[512,512]{1,0:T(8,128)(2,1)}, u32[]{:S(2)}) copy-start(bf16[512,512]{1,0:T(8,128)(2,1)} %constant.13.clone.odd_t) | copy-start | bytes 1572868
  14.0 4.4 %copy-start.1 = (bf16[512,512]{1,0:T(8,128)(2,1)S(1)}, bf16[512,512]{1,0:T(8,128)(2,1)}, u32[]{:S(2)}) copy-start(bf16[512,512]{1,0:T(8,128)(2,1)} %constant.12.clone.odd_h) | copy-start | bytes 1572868
  14.0 4.4 %copy-start.2 = (bf16[512,512]{1,0:T(8,128)(2,1)S(1)}, bf16[512,512]{1,0:T(8,128)(2,1)}, u32[]{:S(2)}) copy-start(bf16[512,512]{1,0:T(8,128)(2,1)} %constant.11.clone.even_t) | copy-start | bytes 1572868
  14.0 4.4 %copy-start.3 = (bf16[512,512]{1,0:T(8,128)(2,1)S(1)}, bf16[512,512]{1,0:T(8,128)(2,1)}, u32[]{:S(2)}) copy-start(bf16[512,512]{1,0:T(8,128)(2,1)} %constant.10.clone.even_h) | copy-start | bytes 1572868
  18.4 18.5 %copy-start.4 = (f32[608,128]{1,0:T(8,128)S(1)}, f32[608,128]{1,0:T(8,128)}, u32[]{:S(2)}) copy-start(f32[608,128]{1,0:T(8,128)} %constant.14.clone.table) | copy-start | bytes 933892

commit v8 on v7

--- a/solution.py
+++ b/solution.py
@@ -33,11 +33,13 @@
 @functools.lru_cache(None)
 def tables(size_x, size_y):
     half = np.arange(size_x // 2)
-    even = two_parts(cas(half[:, None] * half[None, :], size_x // 2))
+    quarter = np.arange(size_x // 4)
+    fourth = two_parts(cas(quarter[:, None] * quarter[None, :], size_x // 4))
+    even = two_parts(cas(quarter[:, None] * (2 * quarter[None, :] + 1), size_x // 2))
     odd = two_parts(cas(half[:, None] * (2 * half[None, :] + 1), size_x))
     full = np.arange(size_y)
     span = cas(full[:, None] * full[None, :], size_y)
-    waves = np.concatenate([2 * half, 2 * half + 1])
+    waves = np.concatenate([4 * quarter, 4 * quarter + 2, 2 * half + 1])
     line_x = 4.0 * np.sin(np.pi * waves / size_x) ** 2
     line_x = np.tile(line_x.reshape(-1, WAVES), (1, 128 // WAVES))
     row = np.arange(size_y // 4)[:, None]
@@ -45,7 +47,7 @@
     wave_y = 32 * (row // 8) + 8 * (lane // WAVES) + row % 8
     line_y = 4.0 * np.sin(np.pi * wave_y / size_y) ** 2
     halves = [span[:, n * 128:(n + 1) * 128] for n in range(size_y // 128)]
-    return even, odd, np.concatenate(halves + [line_y, line_x], 0).astype(np.float32)
+    return fourth + even + odd, np.concatenate(halves + [line_y, line_x], 0).astype(np.float32)
 
 
 def split(values):
@@ -195,7 +197,7 @@
 
 def source_kernel(
     moved, row_factors, layer_factors, layer_far, layer_near, row_far, row_near,
-    even_h, even_t, odd_h, odd_t,
+    fourth_h, fourth_t, even_h, even_t, odd_h, odd_t,
     provisional, thermal_hbm, message, thermal, source, lines, row_p, layer_p, sems
 ):
     size_x = moved.shape[-1]
@@ -246,16 +248,21 @@
             lines[pl.ds(j * PIECE + 38, 2), lanes] = jnp.zeros((2, 128), F32)
     near = lines[:, : size_x // 2]
     far = lines[:, size_x // 2:]
-    half = size_x // 256
-    for turn in range(2):
-        if turn == 0:
-            waves = product(near + far, even_h[...], even_t[...], dot)
-        else:
-            waves = product(near - far, odd_h[...], odd_t[...], dot)
-        for block in range(half):
+    both = near + far
+    left, right = both[:, : size_x // 4], both[:, size_x // 4:]
+    turns = (
+        (left + right, fourth_h, fourth_t),
+        (left - right, even_h, even_t),
+        (near - far, odd_h, odd_t),
+    )
+    at = 0
+    for values, head, tail in turns:
+        waves = product(values, head[...], tail[...], dot)
+        for block in range(waves.shape[1] // 128):
             a = [waves[j * PIECE:(j + 1) * PIECE, block * 128:(block + 1) * 128] for j in range(4)]
             for i, piece in enumerate(swap_groups(a)):
-                message[4 * (turn * half + block) + i] = piece
+                message[at + i] = piece
+            at += 4
     for copy in stored:
         copy.wait()
 
@@ -425,14 +432,16 @@
 
 
 def gradient_kernel(
-    received, even_h, even_t, odd_h, odd_t, provisional, motion_hbm,
+    received, fourth_h, fourth_t, even_h, even_t, odd_h, odd_t, provisional, motion_hbm,
     motion, lines, pressure, row_p, layer_p, sems,
 ):
     size_x = provisional.shape[-1]
     for block in range(size_x // 128):
         for j, piece in enumerate(swap_groups([received[4 * block + i] for i in range(4)])):
             lines[j * PIECE:(j + 1) * PIECE, block * 128:(block + 1) * 128] = piece
-    evens = product(lines[:, : size_x // 2], even_h[...], even_t[...], dot)
+    fourths = product(lines[:, : size_x // 4], fourth_h[...], fourth_t[...], dot)
+    others = product(lines[:, size_x // 4: size_x // 2], even_h[...], even_t[...], dot_nt)
+    evens = jnp.concatenate([fourths + others, fourths - others], 1)
     odds = product(lines[:, size_x // 2:], odd_h[...], odd_t[...], dot_nt)
     lines[:, : size_x // 2] = evens + odds
     lines[:, size_x // 2:] = evens - odds
@@ -481,9 +490,8 @@
     size_x = dual_thermal.shape[-1]
     groups_y = lax.axis_size("gy")
     groups_z = lax.axis_size("gz")
-    evens, odds, table = tables(size_x, ROWS * groups_y)
-    even_h, even_t = map(jnp.asarray, evens)
-    odd_h, odd_t = map(jnp.asarray, odds)
+    waves, table = tables(size_x, ROWS * groups_y)
+    waves = tuple(map(jnp.asarray, waves))
     modes = ROWS * groups_y // 4
     blocks = size_x // 128
 
@@ -535,7 +543,7 @@
             pltpu.HBM(thermal_shape, F32),
             shape_of(*message_shape),
         ),
-        in_specs=[VMEM] * 11,
+        in_specs=[VMEM] * 13,
         out_specs=(VMEM, HBM, VMEM),
         scratch_shapes=[
             pltpu.VMEM(thermal_shape, F32),
@@ -549,7 +557,7 @@
         name="source",
     )(
         moved, row_factors, layer_factors, layer_far, layer_near, row_far, row_near,
-        even_h, even_t, odd_h, odd_t,
+        *waves,
     )
     received = exchanged(message, "gy")
     spectral, handed = pl.pallas_call(
@@ -573,7 +581,7 @@
     motion = pl.pallas_call(
         gradient_kernel,
         out_shape=pltpu.HBM(motion_shape, F32),
-        in_specs=[VMEM] * 6,
+        in_specs=[VMEM] * 8,
         out_specs=HBM,
         scratch_shapes=[
             pltpu.VMEM(motion_shape, F32),
@@ -585,7 +593,7 @@
         ],
         compiler_params=params(24),
         name="gradient",
-    )(received, even_h, even_t, odd_h, odd_t, provisional)
+    )(received, *waves, provisional)
     return motion, thermal_out
 
 

time: 78.1 us -> 77.9 us (level)
  no operation moved by 1% of the time
where the time goes in v8:
time: 77.9 us; the launch traced here: 77.6 us
  blocking collectives  53.2 us (68%)
  starting transfers between devices  11.5 us (15%)
  Pallas kernels  10.2 us (13%)
  waiting for transfers between devices  1.86 us (2%)
  between operations  0.78 us (1%)
    all_to_all x3, blocking collectives, exchanged(): return lax.all_to_all(pieces, axis, split_axis=0, concat_axis=0, tiled=True)  53.2 us
    ppermute x4, starting transfers between devices, swapped(): return lax.ppermute(value, axis, pairs)  11.5 us
    pallas_call x1, Pallas kernels, on_device(): pl.pallas_call(gradient_kernel, out_shape=pltpu.HBM(motion_shape, F32), i...  2.49 us
    pallas_call x1, Pallas kernels, on_device(): pl.pallas_call(inner_kernel, out_shape=(shape_of(4, *thermal_shape), shap...  2.45 us
    ppermute x4, waiting for transfers between devices, swapped(): return lax.ppermute(value, axis, pairs)  1.86 us
    pallas_call x1, Pallas kernels, on_device(): pl.pallas_call(sides_kernel, out_shape=(rows, rows, layers, layers, *fiel...  1.82 us
  transfers between devices with their start and end apart: 4, of which 1 were waited for; matrix products, arithmetic and copies ran while one was open for 0% of the time, Pallas kernels for 3%

profile of v8, /device:TPU:1, one launch (start us, length us, event | category | flops | bytes accessed | tf_op | source)
XLA Modules:
  0.0 77.6 jit_solution(5699937176478732686)
XLA Ops:
  0.6 0.0 copy-start.3
  0.6 1.8 %sides.1 = (f32[5,16,1024]{2,1,0:T(8,128)S(1)}, f32[5,16,1024]{2,1,0:T(8,128)S(1)}, f32[5,8,1024]{2,1,0:T(8,128)S(1)}, f32[5,8,1024]{2,1,0:T(8,128)S(1)}, f32[3,...) custom-call(f32[3,8,16,1024]{3,2,1,0:T(8,128)} %motion_hbm.1, ...), custom_call_target="tpu_custom_call" | custom-call | tf_op jit(solution)/shard_map/sides/pallas_call | solution.py:511
  2.5 2.7 %collective-permute-start.2 = (f32[5,16,1024]{2,1,0:T(8,128)S(1)}, f32[5,16,1024]{2,1,0:T(8,128)S(1)}, u32[]{:S(2)}, u32[]{:S(2)}) collective-permute-start(f32[5,16,1024]{2,1,0:T(8,128)S(1)} %get-tuple-element.25), channel_id=1, source_target_pairs={{8,16},{16,8},{24,32},{32,24},{40,48},{48,40},{56,64},{64,56},{72,... | collective-permute-start | bytes 983048 | tf_op jit(solution)/shard_map/ppermute | solution.py:478
  5.2 3.6 %collective-permute-start.3 = (f32[5,16,1024]{2,1,0:T(8,128)S(1)}, f32[5,16,1024]{2,1,0:T(8,128)S(1)}, u32[]{:S(2)}, u32[]{:S(2)}) collective-permute-start(f32[5,16,1024]{2,1,0:T(8,128)S(1)} %get-tuple-element.26), channel_id=1, source_target_pairs={{0,8},{8,0},{16,24},{24,16},{32,40},{40,32},{48,56},{56,48},{64,72... | collective-permute-start | bytes 983048 | tf_op jit(solution)/shard_map/ppermute | solution.py:478
  8.7 0.7 collective-permute-start
  9.4 4.6 %collective-permute-start.1 = (f32[5,8,1024]{2,1,0:T(8,128)S(1)}, f32[5,8,1024]{2,1,0:T(8,128)S(1)}, u32[]{:S(2)}, u32[]{:S(2)}) collective-permute-start(f32[5,8,1024]{2,1,0:T(8,128)S(1)} %get-tuple-element.24), channel_id=1, source_target_pairs={{0,1},{1,0},{2,3},{3,2},{4,5},{5,4},{6,7},{7,6},{8,9},{9,8},{10,11... | collective-permute-start | bytes 491528 | tf_op jit(solution)/shard_map/ppermute | solution.py:478
  14.0 0.0 copy-done.3
  14.0 0.0 copy-start
  14.0 0.0 copy-start.1
  14.0 0.0 copy-start.5
  14.0 0.0 copy-start.6
  14.0 0.0 copy-start.7
  14.0 2.4 %inner.1 = (f32[4,8,16,1024]{3,2,1,0:T(8,128)S(1)}, f32[4,16,1024]{2,1,0:T(8,128)S(1)}, f32[4,8,1024]{2,1,0:T(8,128)S(1)}) custom-call(f32[3,8,16,1024]{3,2,1,0:T(8,128)S(1)} %get-tuple-element.17.motion, f32[8,16,1024]{2,1,0:T(8,128)S(1)} %get-tuple-element.18.thermal, bf16[3,8,16,1024]{3,2,1,0:T(8,128)(2,1)S(1)} %copy-done.3, ...), custom_call_target="tpu_custom_call" | custom-call | flops 10485760 | bytes 10485760 | tf_op jit(solution)/shard_map/inner/pallas_call | solution.py:524
  16.5 0.0 collective-permute-done.layer_far
  16.5 1.9 %collective-permute-done.1.layer_near = f32[5,8,1024]{2,1,0:T(8,128)S(1)} collective-permute-done((f32[5,8,1024]{2,1,0:T(8,128)S(1)}, f32[5,8,1024]{2,1,0:T(8,128)S(1)}, u32[]{:S(2)}, u32[]{:S(2)}) %collective-permute-start.1) | collective-permute-done | bytes 163872 | tf_op jit(solution)/shard_map/ppermute | solution.py:478
  18.3 0.0 collective-permute-done.2.row_far
  18.3 0.0 collective-permute-done.3.row_near
  18.4 0.0 copy-done
  18.4 0.0 copy-done.1
  18.4 0.0 copy-done.4
  18.4 0.0 copy-done.5
  18.4 0.0 copy-done.6
  18.4 0.0 copy-done.7
  18.4 0.0 copy-start.2
  18.4 1.5 %source.1 = (f32[3,8,16,1024]{3,2,1,0:T(8,128)S(1)}, f32[8,16,1024]{2,1,0:T(8,128)}, f32[32,40,128]{2,1,0:T(8,128)S(1)}) custom-call(f32[4,8,16,1024]{3,2,1,0:T(8,128)S(1)} %get-tuple-element.20.moved, f32[4,16,1024]{2,1,0:T(8,128)S(1)} %get-tuple-element.21.row_factors, f32[4,8,1024]{2,1,0:T(8,128)S(1)} %get-tuple-element.22.layer_factors, ...), custom_call_target="tpu_custom_call" | custom-call | tf_op jit(solution)/shard_map/source/pallas_call | solution.py:539
  20.0 16.7 %all_to_all.15.received = f32[32,40,128]{2,1,0:T(8,128)S(1)} all-to-all(f32[32,40,128]{2,1,0:T(8,128)S(1)} %get-tuple-element.27), channel_id=1, replica_groups=mesh['gy'=32,'gz'=8] {'gy'}, dimensions={0} | all-to-all | bytes 1310720 | tf_op jit(solution)/shard_map/all_to_all | solution.py:482
  36.7 0.0 copy-done.2
  36.7 0.9 %down.1 = (f32[19,64,128]{2,1,0:T(8,128)S(1)}, f32[8,64,128]{2,1,0:T(8,128)S(1)}) custom-call(f32[32,40,128]{2,1,0:T(8,128)S(1)} %all_to_all.15.received, f32[608,128]{1,0:T(8,128)S(1)} %copy-done.2), custom_call_target="tpu_custom_call" | custom-call | tf_op jit(solution)/shard_map/down/pallas_call | solution.py:563
  37.6 17.9 %all_to_all.16.handed = f32[8,64,128]{2,1,0:T(8,128)S(1)} all-to-all(f32[8,64,128]{2,1,0:T(8,128)S(1)} %get-tuple-element.29), channel_id=1, replica_groups=mesh['gy'=32,'gz'=8] {'gz'}, dimensions={0} | all-to-all | bytes 524288 | tf_op jit(solution)/shard_map/all_to_all | solution.py:482
  55.5 1.1 %up.1 = f32[32,40,128]{2,1,0:T(8,128)S(1)} custom-call(f32[19,64,128]{2,1,0:T(8,128)S(1)} %get-tuple-element.28.spectral, f32[8,64,128]{2,1,0:T(8,128)S(1)} %all_to_all.16.handed, f32[608,128]{1,0:T(8,128)S(1)} %copy-done.2), custom_call_target="tpu_custom_call" | custom-call | tf_op jit(solution)/shard_map/up/pallas_call | solution.py:572
  56.6 18.6 %all_to_all.17.received = f32[32,40,128]{2,1,0:T(8,128)S(1)} all-to-all(f32[32,40,128]{2,1,0:T(8,128)S(1)} %up.1), channel_id=1, replica_groups=mesh['gy'=32,'gz'=8] {'gy'}, dimensions={0} | all-to-all | bytes 1310720 | tf_op jit(solution)/shard_map/all_to_all | solution.py:482
  75.1 2.5 %gradient.1 = f32[3,8,16,1024]{3,2,1,0:T(8,128)} custom-call(f32[32,40,128]{2,1,0:T(8,128)S(1)} %all_to_all.17.received, bf16[256,256]{1,0:T(8,128)(2,1)S(1)} %copy-done.7, bf16[256,256]{1,0:T(8,128)(2,1)S(1)} %copy-done.6, bf16[256,256]{1,0:T(8,128)(2,1)S(1)} %copy-done.5, bf16[256,256]{1,0:T(8,128)(2,1)S(1)} %copy-done.4, bf16[512,512]{1,0:T(8,128)(2,1)S(1)} %copy-done.1, ...), custom_call_target="tpu_custom_call" | custom-call | tf_op jit(solution)/shard_map/gradient/pallas_call | solution.py:581
  (1 shorter events, 0.0 us)
Async XLA Ops:
  0.6 13.3 %copy-start.3 = (bf16[3,8,16,1024]{3,2,1,0:T(8,128)(2,1)S(1)}, bf16[3,8,16,1024]{3,2,1,0:T(8,128)(2,1)}, u32[]{:S(2)}) copy-start(bf16[3,8,16,1024]{3,2,1,0:T(8,128)(2,1)} %flow.1) | copy-start | bytes 2359300
  2.5 15.9 %collective-permute-start.2 = (f32[5,16,1024]{2,1,0:T(8,128)S(1)}, f32[5,16,1024]{2,1,0:T(8,128)S(1)}, u32[]{:S(2)}, u32[]{:S(2)}) collective-permute-start(f32[5,16,1024]{2,1,0:T(8,128)S(1)} %get-tuple-element.25), channel_id=1, source_target_pairs={{8,16},{16,8},{24,32},{32,24},{40,48},{48,40},{56,64},{64,56},{72,... | collective-permute-start | bytes 983048 | tf_op jit(solution)/shard_map/ppermute | solution.py:478
  5.2 13.2 %collective-permute-start.3 = (f32[5,16,1024]{2,1,0:T(8,128)S(1)}, f32[5,16,1024]{2,1,0:T(8,128)S(1)}, u32[]{:S(2)}, u32[]{:S(2)}) collective-permute-start(f32[5,16,1024]{2,1,0:T(8,128)S(1)} %get-tuple-element.26), channel_id=1, source_target_pairs={{0,8},{8,0},{16,24},{24,16},{32,40},{40,32},{48,56},{56,48},{64,72... | collective-permute-start | bytes 983048 | tf_op jit(solution)/shard_map/ppermute | solution.py:478
  8.7 7.8 %collective-permute-start = (f32[5,8,1024]{2,1,0:T(8,128)S(1)}, f32[5,8,1024]{2,1,0:T(8,128)S(1)}, u32[]{:S(2)}, u32[]{:S(2)}) collective-permute-start(f32[5,8,1024]{2,1,0:T(8,128)S(1)} %get-tuple-element.23), channel_id=1, source_target_pairs={{1,2},{2,1},{3,4},{4,3},{5,6},{6,5},{9,10},{10,9},{11,12},{12,11},... | collective-permute-start | bytes 491528 | tf_op jit(solution)/shard_map/ppermute | solution.py:478
  9.4 9.0 %collective-permute-start.1 = (f32[5,8,1024]{2,1,0:T(8,128)S(1)}, f32[5,8,1024]{2,1,0:T(8,128)S(1)}, u32[]{:S(2)}, u32[]{:S(2)}) collective-permute-start(f32[5,8,1024]{2,1,0:T(8,128)S(1)} %get-tuple-element.24), channel_id=1, source_target_pairs={{0,1},{1,0},{2,3},{3,2},{4,5},{5,4},{6,7},{7,6},{8,9},{9,8},{10,11... | collective-permute-start | bytes 491528 | tf_op jit(solution)/shard_map/ppermute | solution.py:478
  14.0 4.4 %copy-start = (bf16[512,512]{1,0:T(8,128)(2,1)S(1)}, bf16[512,512]{1,0:T(8,128)(2,1)}, u32[]{:S(2)}) copy-start(bf16[512,512]{1,0:T(8,128)(2,1)} %constant.19.clone.odd_t) | copy-start | bytes 1572868
  14.0 4.4 %copy-start.1 = (bf16[512,512]{1,0:T(8,128)(2,1)S(1)}, bf16[512,512]{1,0:T(8,128)(2,1)}, u32[]{:S(2)}) copy-start(bf16[512,512]{1,0:T(8,128)(2,1)} %constant.18.clone.odd_h) | copy-start | bytes 1572868
  14.0 4.4 %copy-start.4 = (bf16[256,256]{1,0:T(8,128)(2,1)S(1)}, bf16[256,256]{1,0:T(8,128)(2,1)}, u32[]{:S(2)}) copy-start(bf16[256,256]{1,0:T(8,128)(2,1)} %constant.17.clone.even_t) | copy-start | bytes 393220
  14.0 4.4 %copy-start.5 = (bf16[256,256]{1,0:T(8,128)(2,1)S(1)}, bf16[256,256]{1,0:T(8,128)(2,1)}, u32[]{:S(2)}) copy-start(bf16[256,256]{1,0:T(8,128)(2,1)} %constant.16.clone.even_h) | copy-start | bytes 393220
  14.0 4.4 %copy-start.6 = (bf16[256,256]{1,0:T(8,128)(2,1)S(1)}, bf16[256,256]{1,0:T(8,128)(2,1)}, u32[]{:S(2)}) copy-start(bf16[256,256]{1,0:T(8,128)(2,1)} %constant.15.clone.fourth_t) | copy-start | bytes 393220
  14.0 4.4 %copy-start.7 = (bf16[256,256]{1,0:T(8,128)(2,1)S(1)}, bf16[256,256]{1,0:T(8,128)(2,1)}, u32[]{:S(2)}) copy-start(bf16[256,256]{1,0:T(8,128)(2,1)} %constant.14.clone.fourth_h) | copy-start | bytes 393220
  18.4 18.3 %copy-start.2 = (f32[608,128]{1,0:T(8,128)S(1)}, f32[608,128]{1,0:T(8,128)}, u32[]{:S(2)}) copy-start(f32[608,128]{1,0:T(8,128)} %constant.20.clone.table) | copy-start | bytes 933892

commit v9 on v8

--- a/solution.py
+++ b/solution.py
@@ -111,37 +111,32 @@
     return lax.axis_index(axis) % 2 == 1
 
 
-def sides_kernel(
-    motion_hbm, thermal_hbm, base_hbm, row_near, row_far, layer_near, layer_far, motion, thermal, base, sems
-):
-    pairs = ((base_hbm, base), (thermal_hbm, thermal), (motion_hbm, motion))
+def rows_kernel(motion_hbm, thermal_hbm, base_hbm, row_near, row_far, base, sems):
+    near = jnp.where(odd("gy"), 0, ROWS - 1)
+    pairs = []
+    for n, (out, y) in enumerate(((row_near, near), (row_far, ROWS - 1 - near))):
+        pairs += [
+            (base_hbm.at[y], base.at[n]),
+            (motion_hbm.at[:, y], out.at[pl.ds(0, 3)]),
+            (thermal_hbm.at[y], out.at[3]),
+        ]
     fetched = start_copies(pairs, sems)
+    fetched[0].wait()
+    row_near[4] = base[0].astype(F32)
+    fetched[3].wait()
+    row_far[4] = base[1].astype(F32)
+    for n in (1, 2, 4, 5):
+        fetched[n].wait()
+
+
+def layers_kernel(motion, thermal, base, layer_near, layer_far):
     is_odd = odd("gz")
-    near = jnp.where(odd("gy"), 0, ROWS - 1)
-    far = ROWS - 1 - near
-
-    def edges(first, last):
-        return jnp.where(is_odd, first, last), jnp.where(is_odd, last, first)
-
-    fetched[0].wait()
-    row_near[4] = base[near].astype(F32)
-    row_far[4] = base[far].astype(F32)
     for y in range(ROWS):
-        warm = base[y].astype(F32)
-        layer_near[4, y:y + 1, :], layer_far[4, y:y + 1, :] = edges(warm[:1], warm[LAYERS - 1:])
-    fetched[1].wait()
-    row_near[3] = thermal[near]
-    row_far[3] = thermal[far]
-    for y in range(ROWS):
-        layer_near[3, y:y + 1, :], layer_far[3, y:y + 1, :] = edges(thermal[y, :1, :], thermal[y, LAYERS - 1:, :])
-    fetched[2].wait()
-    for c in range(3):
-        row_near[c] = motion[c, near]
-        row_far[c] = motion[c, far]
-        for y in range(ROWS):
-            layer_near[c, y:y + 1, :], layer_far[c, y:y + 1, :] = edges(
-                motion[c, y, :1, :], motion[c, y, LAYERS - 1:, :]
-            )
+        for c in range(5):
+            value = base[y].astype(F32) if c == 4 else thermal[y] if c == 3 else motion[c, y]
+            first, last = value[:1], value[LAYERS - 1:]
+            layer_near[c, y:y + 1, :] = jnp.where(is_odd, first, last)
+            layer_far[c, y:y + 1, :] = jnp.where(is_odd, last, first)
 
 
 def inner_kernel(motion, thermal, flow, base, moved, row_factors, layer_factors):
@@ -507,16 +502,23 @@
     motion_shape = (3, ROWS, LAYERS, size_x)
     thermal_shape = motion_shape[1:]
     message_shape = (groups_y, PIECE, 128)
-    fields = tuple(jax.ShapeDtypeStruct(a.shape, a.dtype) for a in (dual_motion, dual_thermal, base))
-    row_near, row_far, layer_near, layer_far, motion, thermal, base = pl.pallas_call(
-        sides_kernel,
-        out_shape=(rows, rows, layers, layers, *fields),
+    row_near, row_far = pl.pallas_call(
+        rows_kernel,
+        out_shape=(rows, rows),
         in_specs=[HBM] * 3,
-        out_specs=(VMEM,) * 7,
-        scratch_shapes=[pltpu.SemaphoreType.DMA((3,))],
+        out_specs=(VMEM,) * 2,
+        scratch_shapes=[pltpu.VMEM((2, LAYERS, size_x), BF16), pltpu.SemaphoreType.DMA((6,))],
         compiler_params=params(16),
-        name="sides",
+        name="rows",
     )(*map(hbm, (dual_motion, dual_thermal, base)))
+    layer_near, layer_far = pl.pallas_call(
+        layers_kernel,
+        out_shape=(layers, layers),
+        in_specs=[VMEM] * 3,
+        out_specs=(VMEM,) * 2,
+        compiler_params=params(16),
+        name="layers",
+    )(dual_motion, dual_thermal, base)
     row_near = swapped(row_near, "gy", 0, True)
     row_far = swapped(row_far, "gy", 1, True)
     layer_near = swapped(layer_near, "gz", 0, False)
@@ -535,7 +537,7 @@
             flops=80 * ROWS * LAYERS * size_x, transcendentals=0, bytes_accessed=10 << 20
         ),
         name="inner",
-    )(motion, thermal, flow, base)
+    )(dual_motion, dual_thermal, flow, base)
     provisional, thermal_out, message = pl.pallas_call(
         source_kernel,
         out_shape=(

time: 77.9 us -> 77.8 us (level)
    pallas_call x1 -> x2, Pallas kernels: 1.82 us -> 1.66 us  [the longest x1 1.31 us: on_device(): pl.pallas_call(rows_kernel, out_shape=(rows, rows), in_specs=[HBM] * 3, o...]
  transfers between devices with their start and end apart: 4 -> 4, of which waited for: 1 -> 1; matrix products, arithmetic and copies ran while one was open for 0% -> 0% of each run, Pallas kernels for 3% -> 4%
where the time goes in v9:
time: 77.8 us; the launch traced here: 77.5 us
  blocking collectives  53.2 us (68%)
  starting transfers between devices  11.5 us (15%)
  Pallas kernels  10.1 us (13%)
  waiting for transfers between devices  1.9 us (2%)
  between operations  0.82 us (1%)
    all_to_all x3, blocking collectives, exchanged(): return lax.all_to_all(pieces, axis, split_axis=0, concat_axis=0, tiled=True)  53.2 us
    ppermute x4, starting transfers between devices, swapped(): return lax.ppermute(value, axis, pairs)  11.5 us
    pallas_call x1, Pallas kernels, on_device(): pl.pallas_call(gradient_kernel, out_shape=pltpu.HBM(motion_shape, F32), i...  2.48 us
    pallas_call x1, Pallas kernels, on_device(): pl.pallas_call(inner_kernel, out_shape=(shape_of(4, *thermal_shape), shap...  2.44 us
    ppermute x4, waiting for transfers between devices, swapped(): return lax.ppermute(value, axis, pairs)  1.9 us
  transfers between devices with their start and end apart: 4, of which 1 were waited for; matrix products, arithmetic and copies ran while one was open for 0% of the time, Pallas kernels for 4%

profile of v9, /device:TPU:1, one launch (start us, length us, event | category | flops | bytes accessed | tf_op | source)
XLA Modules:
  0.0 77.5 jit_solution(3015614561031014798)
XLA Ops:
  0.6 0.0 copy-start.2
  0.6 0.0 copy-start.1
  0.6 0.0 copy-start
  0.7 1.3 %rows.1 = (f32[5,16,1024]{2,1,0:T(8,128)S(1)}, f32[5,16,1024]{2,1,0:T(8,128)S(1)}) custom-call(f32[3,8,16,1024]{3,2,1,0:T(8,128)} %motion_hbm.1, f32[8,16,1024]{2,1,0:T(8,128)} %thermal_hbm.1, bf16[8,16,1024]{2,1,0:T(8,128)(2,1)} %base_hbm.1), custom_call_target="tpu_custom_call" | custom-call | tf_op jit(solution)/shard_map/rows/pallas_call | solution.py:505
  2.0 0.0 copy-start.6
  2.0 2.7 %collective-permute-start.2 = (f32[5,16,1024]{2,1,0:T(8,128)S(1)}, f32[5,16,1024]{2,1,0:T(8,128)S(1)}, u32[]{:S(2)}, u32[]{:S(2)}) collective-permute-start(f32[5,16,1024]{2,1,0:T(8,128)S(1)} %get-tuple-element.19), channel_id=1, source_target_pairs={{8,16},{16,8},{24,32},{32,24},{40,48},{48,40},{56,64},{64,56},{72,... | collective-permute-start | bytes 983048 | tf_op jit(solution)/shard_map/ppermute | solution.py:473
  4.7 3.6 %collective-permute-start.3 = (f32[5,16,1024]{2,1,0:T(8,128)S(1)}, f32[5,16,1024]{2,1,0:T(8,128)S(1)}, u32[]{:S(2)}, u32[]{:S(2)}) collective-permute-start(f32[5,16,1024]{2,1,0:T(8,128)S(1)} %get-tuple-element.20), channel_id=1, source_target_pairs={{0,8},{8,0},{16,24},{24,16},{32,40},{40,32},{48,56},{56,48},{64,72... | collective-permute-start | bytes 983048 | tf_op jit(solution)/shard_map/ppermute | solution.py:473
  8.2 0.0 copy-done.1
  8.2 0.3 layers.1
  8.6 0.7 collective-permute-start
  9.3 0.0 copy-start.3
  9.3 0.0 copy-start.4
  9.3 0.0 copy-start.7
  9.3 0.0 copy-start.8
  9.3 0.0 copy-start.9
  9.3 0.0 copy-start.10
  9.3 4.6 %collective-permute-start.1 = (f32[5,8,1024]{2,1,0:T(8,128)S(1)}, f32[5,8,1024]{2,1,0:T(8,128)S(1)}, u32[]{:S(2)}, u32[]{:S(2)}) collective-permute-start(f32[5,8,1024]{2,1,0:T(8,128)S(1)} %get-tuple-element.18), channel_id=1, source_target_pairs={{0,1},{1,0},{2,3},{3,2},{4,5},{5,4},{6,7},{7,6},{8,9},{9,8},{10,11... | collective-permute-start | bytes 491528 | tf_op jit(solution)/shard_map/ppermute | solution.py:473
  13.9 0.0 copy-done.6
  13.9 2.4 %inner.1 = (f32[4,8,16,1024]{3,2,1,0:T(8,128)S(1)}, f32[4,16,1024]{2,1,0:T(8,128)S(1)}, f32[4,8,1024]{2,1,0:T(8,128)S(1)}) custom-call(f32[3,8,16,1024]{3,2,1,0:T(8,128)S(1)} %copy-done, f32[8,16,1024]{2,1,0:T(8,128)S(1)} %copy-done.1, bf16[3,8,16,1024]{3,2,1,0:T(8,128)(2,1)S(1)} %copy-done.6, bf16[8,16,1024]{2,1,0:T(8,128)(2,1)S(1)} %copy-done.2), custom_call_target="tpu_custom_call" | custom-call | flops 10485760 | bytes 10485760 | tf_op jit(solution)/shard_map/inner/pallas_call | solution.py:526
  16.4 0.0 collective-permute-done.layer_far
  16.4 1.9 %collective-permute-done.1.layer_near = f32[5,8,1024]{2,1,0:T(8,128)S(1)} collective-permute-done((f32[5,8,1024]{2,1,0:T(8,128)S(1)}, f32[5,8,1024]{2,1,0:T(8,128)S(1)}, u32[]{:S(2)}, u32[]{:S(2)}) %collective-permute-start.1) | collective-permute-done | bytes 163872 | tf_op jit(solution)/shard_map/ppermute | solution.py:473
  18.3 0.0 collective-permute-done.2.row_far
  18.3 0.0 collective-permute-done.3.row_near
  18.3 0.0 copy-done.3
  18.4 0.0 copy-start.5
  18.4 1.5 %source.1 = (f32[3,8,16,1024]{3,2,1,0:T(8,128)S(1)}, f32[8,16,1024]{2,1,0:T(8,128)}, f32[32,40,128]{2,1,0:T(8,128)S(1)}) custom-call(f32[4,8,16,1024]{3,2,1,0:T(8,128)S(1)} %get-tuple-element.14.moved, f32[4,16,1024]{2,1,0:T(8,128)S(1)} %get-tuple-element.15.row_factors, f32[4,8,1024]{2,1,0:T(8,128)S(1)} %get-tuple-element.16.layer_factors, ...), custom_call_target="tpu_custom_call" | custom-call | tf_op jit(solution)/shard_map/source/pallas_call | solution.py:541
  19.9 16.8 %all_to_all.15.received = f32[32,40,128]{2,1,0:T(8,128)S(1)} all-to-all(f32[32,40,128]{2,1,0:T(8,128)S(1)} %get-tuple-element.21), channel_id=1, replica_groups=mesh['gy'=32,'gz'=8] {'gy'}, dimensions={0} | all-to-all | bytes 1310720 | tf_op jit(solution)/shard_map/all_to_all | solution.py:477
  36.7 0.9 %down.1 = (f32[19,64,128]{2,1,0:T(8,128)S(1)}, f32[8,64,128]{2,1,0:T(8,128)S(1)}) custom-call(f32[32,40,128]{2,1,0:T(8,128)S(1)} %all_to_all.15.received, f32[608,128]{1,0:T(8,128)S(1)} %copy-done.5), custom_call_target="tpu_custom_call" | custom-call | tf_op jit(solution)/shard_map/down/pallas_call | solution.py:565
  37.6 17.8 %all_to_all.16.handed = f32[8,64,128]{2,1,0:T(8,128)S(1)} all-to-all(f32[8,64,128]{2,1,0:T(8,128)S(1)} %get-tuple-element.23), channel_id=1, replica_groups=mesh['gy'=32,'gz'=8] {'gz'}, dimensions={0} | all-to-all | bytes 524288 | tf_op jit(solution)/shard_map/all_to_all | solution.py:477
  55.4 1.1 %up.1 = f32[32,40,128]{2,1,0:T(8,128)S(1)} custom-call(f32[19,64,128]{2,1,0:T(8,128)S(1)} %get-tuple-element.22.spectral, f32[8,64,128]{2,1,0:T(8,128)S(1)} %all_to_all.16.handed, f32[608,128]{1,0:T(8,128)S(1)} %copy-done.5), custom_call_target="tpu_custom_call" | custom-call | tf_op jit(solution)/shard_map/up/pallas_call | solution.py:574
  56.5 18.6 %all_to_all.17.received = f32[32,40,128]{2,1,0:T(8,128)S(1)} all-to-all(f32[32,40,128]{2,1,0:T(8,128)S(1)} %up.1), channel_id=1, replica_groups=mesh['gy'=32,'gz'=8] {'gy'}, dimensions={0} | all-to-all | bytes 1310720 | tf_op jit(solution)/shard_map/all_to_all | solution.py:477
  75.0 2.5 %gradient.1 = f32[3,8,16,1024]{3,2,1,0:T(8,128)} custom-call(f32[32,40,128]{2,1,0:T(8,128)S(1)} %all_to_all.17.received, bf16[256,256]{1,0:T(8,128)(2,1)S(1)} %copy-done.10, bf16[256,256]{1,0:T(8,128)(2,1)S(1)} %copy-done.9, bf16[256,256]{1,0:T(8,128)(2,1)S(1)} %copy-done.8, bf16[256,256]{1,0:T(8,128)(2,1)S(1)} %copy-done.7, bf16[512,512]{1,0:T(8,128)(2,1)S(1)} %copy-done.4, ...), custom_call_target="tpu_custom_call" | custom-call | tf_op jit(solution)/shard_map/gradient/pallas_call | solution.py:583
  (8 shorter events, 0.0 us)
Async XLA Ops:
  0.6 7.6 %copy-start.2 = (bf16[8,16,1024]{2,1,0:T(8,128)(2,1)S(1)}, bf16[8,16,1024]{2,1,0:T(8,128)(2,1)}, u32[]{:S(2)}) copy-start(bf16[8,16,1024]{2,1,0:T(8,128)(2,1)} %base_hbm.1) | copy-start | bytes 786436
  0.6 7.6 %copy-start.1 = (f32[8,16,1024]{2,1,0:T(8,128)S(1)}, f32[8,16,1024]{2,1,0:T(8,128)}, u32[]{:S(2)}) copy-start(f32[8,16,1024]{2,1,0:T(8,128)} %thermal_hbm.1) | copy-start | bytes 1572868
  0.6 7.6 %copy-start = (f32[3,8,16,1024]{3,2,1,0:T(8,128)S(1)}, f32[3,8,16,1024]{3,2,1,0:T(8,128)}, u32[]{:S(2)}) copy-start(f32[3,8,16,1024]{3,2,1,0:T(8,128)} %motion_hbm.1) | copy-start | bytes 4718596
  2.0 12.0 %copy-start.6 = (bf16[3,8,16,1024]{3,2,1,0:T(8,128)(2,1)S(1)}, bf16[3,8,16,1024]{3,2,1,0:T(8,128)(2,1)}, u32[]{:S(2)}) copy-start(bf16[3,8,16,1024]{3,2,1,0:T(8,128)(2,1)} %flow.1) | copy-start | bytes 2359300
  2.0 16.3 %collective-permute-start.2 = (f32[5,16,1024]{2,1,0:T(8,128)S(1)}, f32[5,16,1024]{2,1,0:T(8,128)S(1)}, u32[]{:S(2)}, u32[]{:S(2)}) collective-permute-start(f32[5,16,1024]{2,1,0:T(8,128)S(1)} %get-tuple-element.19), channel_id=1, source_target_pairs={{8,16},{16,8},{24,32},{32,24},{40,48},{48,40},{56,64},{64,56},{72,... | collective-permute-start | bytes 983048 | tf_op jit(solution)/shard_map/ppermute | solution.py:473
  4.7 13.6 %collective-permute-start.3 = (f32[5,16,1024]{2,1,0:T(8,128)S(1)}, f32[5,16,1024]{2,1,0:T(8,128)S(1)}, u32[]{:S(2)}, u32[]{:S(2)}) collective-permute-start(f32[5,16,1024]{2,1,0:T(8,128)S(1)} %get-tuple-element.20), channel_id=1, source_target_pairs={{0,8},{8,0},{16,24},{24,16},{32,40},{40,32},{48,56},{56,48},{64,72... | collective-permute-start | bytes 983048 | tf_op jit(solution)/shard_map/ppermute | solution.py:473
  8.6 7.8 %collective-permute-start = (f32[5,8,1024]{2,1,0:T(8,128)S(1)}, f32[5,8,1024]{2,1,0:T(8,128)S(1)}, u32[]{:S(2)}, u32[]{:S(2)}) collective-permute-start(f32[5,8,1024]{2,1,0:T(8,128)S(1)} %get-tuple-element.17), channel_id=1, source_target_pairs={{1,2},{2,1},{3,4},{4,3},{5,6},{6,5},{9,10},{10,9},{11,12},{12,11},... | collective-permute-start | bytes 491528 | tf_op jit(solution)/shard_map/ppermute | solution.py:473
  9.3 9.0 %copy-start.3 = (bf16[512,512]{1,0:T(8,128)(2,1)S(1)}, bf16[512,512]{1,0:T(8,128)(2,1)}, u32[]{:S(2)}) copy-start(bf16[512,512]{1,0:T(8,128)(2,1)} %constant.19.clone.odd_t) | copy-start | bytes 1572868
  9.3 9.0 %copy-start.4 = (bf16[512,512]{1,0:T(8,128)(2,1)S(1)}, bf16[512,512]{1,0:T(8,128)(2,1)}, u32[]{:S(2)}) copy-start(bf16[512,512]{1,0:T(8,128)(2,1)} %constant.18.clone.odd_h) | copy-start | bytes 1572868
  9.3 9.0 %copy-start.7 = (bf16[256,256]{1,0:T(8,128)(2,1)S(1)}, bf16[256,256]{1,0:T(8,128)(2,1)}, u32[]{:S(2)}) copy-start(bf16[256,256]{1,0:T(8,128)(2,1)} %constant.17.clone.even_t) | copy-start | bytes 393220
  9.3 9.0 %copy-start.8 = (bf16[256,256]{1,0:T(8,128)(2,1)S(1)}, bf16[256,256]{1,0:T(8,128)(2,1)}, u32[]{:S(2)}) copy-start(bf16[256,256]{1,0:T(8,128)(2,1)} %constant.16.clone.even_h) | copy-start | bytes 393220
  9.3 9.0 %copy-start.9 = (bf16[256,256]{1,0:T(8,128)(2,1)S(1)}, bf16[256,256]{1,0:T(8,128)(2,1)}, u32[]{:S(2)}) copy-start(bf16[256,256]{1,0:T(8,128)(2,1)} %constant.15.clone.fourth_t) | copy-start | bytes 393220
  9.3 9.0 %copy-start.10 = (bf16[256,256]{1,0:T(8,128)(2,1)S(1)}, bf16[256,256]{1,0:T(8,128)(2,1)}, u32[]{:S(2)}) copy-start(bf16[256,256]{1,0:T(8,128)(2,1)} %constant.14.clone.fourth_h) | copy-start | bytes 393220
  9.3 9.0 %collective-permute-start.1 = (f32[5,8,1024]{2,1,0:T(8,128)S(1)}, f32[5,8,1024]{2,1,0:T(8,128)S(1)}, u32[]{:S(2)}, u32[]{:S(2)}) collective-permute-start(f32[5,8,1024]{2,1,0:T(8,128)S(1)} %get-tuple-element.18), channel_id=1, source_target_pairs={{0,1},{1,0},{2,3},{3,2},{4,5},{5,4},{6,7},{7,6},{8,9},{9,8},{10,11... | collective-permute-start | bytes 491528 | tf_op jit(solution)/shard_map/ppermute | solution.py:473
  18.4 18.3 %copy-start.5 = (f32[608,128]{1,0:T(8,128)S(1)}, f32[608,128]{1,0:T(8,128)}, u32[]{:S(2)}) copy-start(f32[608,128]{1,0:T(8,128)} %constant.20.clone.table) | copy-start | bytes 933892

commit v10 on v9

--- a/solution.py
+++ b/solution.py
@@ -438,15 +438,17 @@
     others = product(lines[:, size_x // 4: size_x // 2], even_h[...], even_t[...], dot_nt)
     evens = jnp.concatenate([fourths + others, fourths - others], 1)
     odds = product(lines[:, size_x // 2:], odd_h[...], odd_t[...], dot_nt)
-    lines[:, : size_x // 2] = evens + odds
-    lines[:, size_x // 2:] = evens - odds
-    for b in range(size_x // 128):
-        lanes = pl.ds(b * 128, 128)
+    half = size_x // 256
+    for b in range(2 * half):
+        lanes = slice(b % half * 128, (b % half + 1) * 128)
+        values = evens[:, lanes] + odds[:, lanes] if b < half else evens[:, lanes] - odds[:, lanes]
         for j in range(4):
             for q in range(QUADS):
-                pressure[b, pl.ds(4 * q + j, ROWS, stride=LAYERS), :] = lines[pl.ds(j * PIECE + q * 8, 8), lanes]
-            row_p[b, pl.ds(j, 4, stride=4), :] = lines[pl.ds(j * PIECE + 32, 4), lanes]
-            layer_p[b, pl.ds(j, 2, stride=4), :] = lines[pl.ds(j * PIECE + 36, 2), lanes]
+                at = j * PIECE + q * 8
+                pressure[b, pl.ds(4 * q + j, ROWS, stride=LAYERS), :] = values[at:at + 8]
+            at = j * PIECE + 8 * QUADS
+            row_p[b, pl.ds(j, 4, stride=4), :] = values[at:at + 4]
+            layer_p[b, pl.ds(j, 2, stride=4), :] = values[at + 4:at + 6]
     stored = []
     bottom = lax.broadcasted_iota(jnp.int32, (LAYERS, size_x), 0) == 0
     for y in range(ROWS):

time: 77.8 us -> 77.8 us (level)
  no operation moved by 1% of the time
where the time goes in v10:
time: 77.8 us; the launch traced here: 77.5 us
  blocking collectives  53.2 us (68%)
  starting transfers between devices  11.5 us (15%)
  Pallas kernels  10.1 us (13%)
  waiting for transfers between devices  1.9 us (2%)
  between operations  0.82 us (1%)
    all_to_all x3, blocking collectives, exchanged(): return lax.all_to_all(pieces, axis, split_axis=0, concat_axis=0, tiled=True)  53.2 us
    ppermute x4, starting transfers between devices, swapped(): return lax.ppermute(value, axis, pairs)  11.5 us
    pallas_call x1, Pallas kernels, on_device(): pl.pallas_call(gradient_kernel, out_shape=pltpu.HBM(motion_shape, F32), i...  2.48 us
    pallas_call x1, Pallas kernels, on_device(): pl.pallas_call(inner_kernel, out_shape=(shape_of(4, *thermal_shape), shap...  2.44 us
    ppermute x4, waiting for transfers between devices, swapped(): return lax.ppermute(value, axis, pairs)  1.9 us
  transfers between devices with their start and end apart: 4, of which 1 were waited for; matrix products, arithmetic and copies ran while one was open for 0% of the time, Pallas kernels for 4%

profile of v10, /device:TPU:1, one launch (start us, length us, event | category | flops | bytes accessed | tf_op | source)
XLA Modules:
  0.0 77.5 jit_solution(9623337881731314740)
XLA Ops:
  0.6 0.0 copy-start.2
  0.6 0.0 copy-start.1
  0.6 0.0 copy-start
  0.7 1.3 %rows.1 = (f32[5,16,1024]{2,1,0:T(8,128)S(1)}, f32[5,16,1024]{2,1,0:T(8,128)S(1)}) custom-call(f32[3,8,16,1024]{3,2,1,0:T(8,128)} %motion_hbm.1, f32[8,16,1024]{2,1,0:T(8,128)} %thermal_hbm.1, bf16[8,16,1024]{2,1,0:T(8,128)(2,1)} %base_hbm.1), custom_call_target="tpu_custom_call" | custom-call | tf_op jit(solution)/shard_map/rows/pallas_call | solution.py:507
  2.0 0.0 copy-start.6
  2.0 2.7 %collective-permute-start.2 = (f32[5,16,1024]{2,1,0:T(8,128)S(1)}, f32[5,16,1024]{2,1,0:T(8,128)S(1)}, u32[]{:S(2)}, u32[]{:S(2)}) collective-permute-start(f32[5,16,1024]{2,1,0:T(8,128)S(1)} %get-tuple-element.19), channel_id=1, source_target_pairs={{8,16},{16,8},{24,32},{32,24},{40,48},{48,40},{56,64},{64,56},{72,... | collective-permute-start | bytes 983048 | tf_op jit(solution)/shard_map/ppermute | solution.py:475
  4.7 3.6 %collective-permute-start.3 = (f32[5,16,1024]{2,1,0:T(8,128)S(1)}, f32[5,16,1024]{2,1,0:T(8,128)S(1)}, u32[]{:S(2)}, u32[]{:S(2)}) collective-permute-start(f32[5,16,1024]{2,1,0:T(8,128)S(1)} %get-tuple-element.20), channel_id=1, source_target_pairs={{0,8},{8,0},{16,24},{24,16},{32,40},{40,32},{48,56},{56,48},{64,72... | collective-permute-start | bytes 983048 | tf_op jit(solution)/shard_map/ppermute | solution.py:475
  8.2 0.0 copy-done.1
  8.2 0.3 layers.1
  8.6 0.7 collective-permute-start
  9.3 0.0 copy-start.3
  9.3 0.0 copy-start.4
  9.3 0.0 copy-start.7
  9.3 0.0 copy-start.8
  9.3 0.0 copy-start.9
  9.3 0.0 copy-start.10
  9.3 4.6 %collective-permute-start.1 = (f32[5,8,1024]{2,1,0:T(8,128)S(1)}, f32[5,8,1024]{2,1,0:T(8,128)S(1)}, u32[]{:S(2)}, u32[]{:S(2)}) collective-permute-start(f32[5,8,1024]{2,1,0:T(8,128)S(1)} %get-tuple-element.18), channel_id=1, source_target_pairs={{0,1},{1,0},{2,3},{3,2},{4,5},{5,4},{6,7},{7,6},{8,9},{9,8},{10,11... | collective-permute-start | bytes 491528 | tf_op jit(solution)/shard_map/ppermute | solution.py:475
  13.9 0.0 copy-done.6
  13.9 2.4 %inner.1 = (f32[4,8,16,1024]{3,2,1,0:T(8,128)S(1)}, f32[4,16,1024]{2,1,0:T(8,128)S(1)}, f32[4,8,1024]{2,1,0:T(8,128)S(1)}) custom-call(f32[3,8,16,1024]{3,2,1,0:T(8,128)S(1)} %copy-done, f32[8,16,1024]{2,1,0:T(8,128)S(1)} %copy-done.1, bf16[3,8,16,1024]{3,2,1,0:T(8,128)(2,1)S(1)} %copy-done.6, bf16[8,16,1024]{2,1,0:T(8,128)(2,1)S(1)} %copy-done.2), custom_call_target="tpu_custom_call" | custom-call | flops 10485760 | bytes 10485760 | tf_op jit(solution)/shard_map/inner/pallas_call | solution.py:528
  16.4 0.0 collective-permute-done.layer_far
  16.4 1.9 %collective-permute-done.1.layer_near = f32[5,8,1024]{2,1,0:T(8,128)S(1)} collective-permute-done((f32[5,8,1024]{2,1,0:T(8,128)S(1)}, f32[5,8,1024]{2,1,0:T(8,128)S(1)}, u32[]{:S(2)}, u32[]{:S(2)}) %collective-permute-start.1) | collective-permute-done | bytes 163872 | tf_op jit(solution)/shard_map/ppermute | solution.py:475
  18.3 0.0 collective-permute-done.2.row_far
  18.3 0.0 collective-permute-done.3.row_near
  18.3 0.0 copy-done.3
  18.4 0.0 copy-start.5
  18.4 1.5 %source.1 = (f32[3,8,16,1024]{3,2,1,0:T(8,128)S(1)}, f32[8,16,1024]{2,1,0:T(8,128)}, f32[32,40,128]{2,1,0:T(8,128)S(1)}) custom-call(f32[4,8,16,1024]{3,2,1,0:T(8,128)S(1)} %get-tuple-element.14.moved, f32[4,16,1024]{2,1,0:T(8,128)S(1)} %get-tuple-element.15.row_factors, f32[4,8,1024]{2,1,0:T(8,128)S(1)} %get-tuple-element.16.layer_factors, ...), custom_call_target="tpu_custom_call" | custom-call | tf_op jit(solution)/shard_map/source/pallas_call | solution.py:543
  19.9 16.8 %all_to_all.15.received = f32[32,40,128]{2,1,0:T(8,128)S(1)} all-to-all(f32[32,40,128]{2,1,0:T(8,128)S(1)} %get-tuple-element.21), channel_id=1, replica_groups=mesh['gy'=32,'gz'=8] {'gy'}, dimensions={0} | all-to-all | bytes 1310720 | tf_op jit(solution)/shard_map/all_to_all | solution.py:479
  36.7 0.9 %down.1 = (f32[19,64,128]{2,1,0:T(8,128)S(1)}, f32[8,64,128]{2,1,0:T(8,128)S(1)}) custom-call(f32[32,40,128]{2,1,0:T(8,128)S(1)} %all_to_all.15.received, f32[608,128]{1,0:T(8,128)S(1)} %copy-done.5), custom_call_target="tpu_custom_call" | custom-call | tf_op jit(solution)/shard_map/down/pallas_call | solution.py:567
  37.6 17.8 %all_to_all.16.handed = f32[8,64,128]{2,1,0:T(8,128)S(1)} all-to-all(f32[8,64,128]{2,1,0:T(8,128)S(1)} %get-tuple-element.23), channel_id=1, replica_groups=mesh['gy'=32,'gz'=8] {'gz'}, dimensions={0} | all-to-all | bytes 524288 | tf_op jit(solution)/shard_map/all_to_all | solution.py:479
  55.4 1.1 %up.1 = f32[32,40,128]{2,1,0:T(8,128)S(1)} custom-call(f32[19,64,128]{2,1,0:T(8,128)S(1)} %get-tuple-element.22.spectral, f32[8,64,128]{2,1,0:T(8,128)S(1)} %all_to_all.16.handed, f32[608,128]{1,0:T(8,128)S(1)} %copy-done.5), custom_call_target="tpu_custom_call" | custom-call | tf_op jit(solution)/shard_map/up/pallas_call | solution.py:576
  56.5 18.6 %all_to_all.17.received = f32[32,40,128]{2,1,0:T(8,128)S(1)} all-to-all(f32[32,40,128]{2,1,0:T(8,128)S(1)} %up.1), channel_id=1, replica_groups=mesh['gy'=32,'gz'=8] {'gy'}, dimensions={0} | all-to-all | bytes 1310720 | tf_op jit(solution)/shard_map/all_to_all | solution.py:479
  75.0 2.5 %gradient.1 = f32[3,8,16,1024]{3,2,1,0:T(8,128)} custom-call(f32[32,40,128]{2,1,0:T(8,128)S(1)} %all_to_all.17.received, bf16[256,256]{1,0:T(8,128)(2,1)S(1)} %copy-done.10, bf16[256,256]{1,0:T(8,128)(2,1)S(1)} %copy-done.9, bf16[256,256]{1,0:T(8,128)(2,1)S(1)} %copy-done.8, bf16[256,256]{1,0:T(8,128)(2,1)S(1)} %copy-done.7, bf16[512,512]{1,0:T(8,128)(2,1)S(1)} %copy-done.4, ...), custom_call_target="tpu_custom_call" | custom-call | tf_op jit(solution)/shard_map/gradient/pallas_call | solution.py:585
  (8 shorter events, 0.0 us)
Async XLA Ops:
  0.6 7.6 %copy-start.2 = (bf16[8,16,1024]{2,1,0:T(8,128)(2,1)S(1)}, bf16[8,16,1024]{2,1,0:T(8,128)(2,1)}, u32[]{:S(2)}) copy-start(bf16[8,16,1024]{2,1,0:T(8,128)(2,1)} %base_hbm.1) | copy-start | bytes 786436
  0.6 7.6 %copy-start.1 = (f32[8,16,1024]{2,1,0:T(8,128)S(1)}, f32[8,16,1024]{2,1,0:T(8,128)}, u32[]{:S(2)}) copy-start(f32[8,16,1024]{2,1,0:T(8,128)} %thermal_hbm.1) | copy-start | bytes 1572868
  0.6 7.6 %copy-start = (f32[3,8,16,1024]{3,2,1,0:T(8,128)S(1)}, f32[3,8,16,1024]{3,2,1,0:T(8,128)}, u32[]{:S(2)}) copy-start(f32[3,8,16,1024]{3,2,1,0:T(8,128)} %motion_hbm.1) | copy-start | bytes 4718596
  2.0 12.0 %copy-start.6 = (bf16[3,8,16,1024]{3,2,1,0:T(8,128)(2,1)S(1)}, bf16[3,8,16,1024]{3,2,1,0:T(8,128)(2,1)}, u32[]{:S(2)}) copy-start(bf16[3,8,16,1024]{3,2,1,0:T(8,128)(2,1)} %flow.1) | copy-start | bytes 2359300
  2.0 16.3 %collective-permute-start.2 = (f32[5,16,1024]{2,1,0:T(8,128)S(1)}, f32[5,16,1024]{2,1,0:T(8,128)S(1)}, u32[]{:S(2)}, u32[]{:S(2)}) collective-permute-start(f32[5,16,1024]{2,1,0:T(8,128)S(1)} %get-tuple-element.19), channel_id=1, source_target_pairs={{8,16},{16,8},{24,32},{32,24},{40,48},{48,40},{56,64},{64,56},{72,... | collective-permute-start | bytes 983048 | tf_op jit(solution)/shard_map/ppermute | solution.py:475
  4.7 13.6 %collective-permute-start.3 = (f32[5,16,1024]{2,1,0:T(8,128)S(1)}, f32[5,16,1024]{2,1,0:T(8,128)S(1)}, u32[]{:S(2)}, u32[]{:S(2)}) collective-permute-start(f32[5,16,1024]{2,1,0:T(8,128)S(1)} %get-tuple-element.20), channel_id=1, source_target_pairs={{0,8},{8,0},{16,24},{24,16},{32,40},{40,32},{48,56},{56,48},{64,72... | collective-permute-start | bytes 983048 | tf_op jit(solution)/shard_map/ppermute | solution.py:475
  8.6 7.8 %collective-permute-start = (f32[5,8,1024]{2,1,0:T(8,128)S(1)}, f32[5,8,1024]{2,1,0:T(8,128)S(1)}, u32[]{:S(2)}, u32[]{:S(2)}) collective-permute-start(f32[5,8,1024]{2,1,0:T(8,128)S(1)} %get-tuple-element.17), channel_id=1, source_target_pairs={{1,2},{2,1},{3,4},{4,3},{5,6},{6,5},{9,10},{10,9},{11,12},{12,11},... | collective-permute-start | bytes 491528 | tf_op jit(solution)/shard_map/ppermute | solution.py:475
  9.3 9.0 %copy-start.3 = (bf16[512,512]{1,0:T(8,128)(2,1)S(1)}, bf16[512,512]{1,0:T(8,128)(2,1)}, u32[]{:S(2)}) copy-start(bf16[512,512]{1,0:T(8,128)(2,1)} %constant.19.clone.odd_t) | copy-start | bytes 1572868
  9.3 9.0 %copy-start.4 = (bf16[512,512]{1,0:T(8,128)(2,1)S(1)}, bf16[512,512]{1,0:T(8,128)(2,1)}, u32[]{:S(2)}) copy-start(bf16[512,512]{1,0:T(8,128)(2,1)} %constant.18.clone.odd_h) | copy-start | bytes 1572868
  9.3 9.0 %copy-start.7 = (bf16[256,256]{1,0:T(8,128)(2,1)S(1)}, bf16[256,256]{1,0:T(8,128)(2,1)}, u32[]{:S(2)}) copy-start(bf16[256,256]{1,0:T(8,128)(2,1)} %constant.17.clone.even_t) | copy-start | bytes 393220
  9.3 9.0 %copy-start.8 = (bf16[256,256]{1,0:T(8,128)(2,1)S(1)}, bf16[256,256]{1,0:T(8,128)(2,1)}, u32[]{:S(2)}) copy-start(bf16[256,256]{1,0:T(8,128)(2,1)} %constant.16.clone.even_h) | copy-start | bytes 393220
  9.3 9.0 %copy-start.9 = (bf16[256,256]{1,0:T(8,128)(2,1)S(1)}, bf16[256,256]{1,0:T(8,128)(2,1)}, u32[]{:S(2)}) copy-start(bf16[256,256]{1,0:T(8,128)(2,1)} %constant.15.clone.fourth_t) | copy-start | bytes 393220
  9.3 9.0 %copy-start.10 = (bf16[256,256]{1,0:T(8,128)(2,1)S(1)}, bf16[256,256]{1,0:T(8,128)(2,1)}, u32[]{:S(2)}) copy-start(bf16[256,256]{1,0:T(8,128)(2,1)} %constant.14.clone.fourth_h) | copy-start | bytes 393220
  9.3 9.0 %collective-permute-start.1 = (f32[5,8,1024]{2,1,0:T(8,128)S(1)}, f32[5,8,1024]{2,1,0:T(8,128)S(1)}, u32[]{:S(2)}, u32[]{:S(2)}) collective-permute-start(f32[5,8,1024]{2,1,0:T(8,128)S(1)} %get-tuple-element.18), channel_id=1, source_target_pairs={{0,1},{1,0},{2,3},{3,2},{4,5},{5,4},{6,7},{7,6},{8,9},{9,8},{10,11... | collective-permute-start | bytes 491528 | tf_op jit(solution)/shard_map/ppermute | solution.py:475
  18.4 18.3 %copy-start.5 = (f32[608,128]{1,0:T(8,128)S(1)}, f32[608,128]{1,0:T(8,128)}, u32[]{:S(2)}) copy-start(f32[608,128]{1,0:T(8,128)} %constant.20.clone.table) | copy-start | bytes 933892
